TPU v7x, 256 devices: a whole 4x4x8 slice. The times are simulated.
256 devices in a mesh: strip: 16 (over z_lo, y, core), tensor: 16 (over x, z_hi).
Axes of the slice: x: 4, y: 4, z: 8 (z_hi: 4, z_lo: 2; z = z_hi * 2 + z_lo), core: 2. Of those that a mesh axis runs over, the one named last changes fastest.
Arguments:
- conv_out: bfloat16 [128, 256, 1536], P('strip', 'tensor'), may hold values from -425 to 425
- out_grad: bfloat16 [128, 256, 1536], P('strip', 'tensor'), may hold values from -6 to 6
- layer_norm_gain: float32 [1536], replicated, may hold values from 0.5 to 2
- layer_norm_bias: float32 [1536], replicated, may hold values from -3 to 3
- w_in: bfloat16 [1536, 6144], P('strip', 'tensor'), may hold values from -0.15625 to 0.15625
- b_in: float32 [6144], P('tensor'), may hold values from -3 to 3
- w_out: bfloat16 [6144, 1536], P('tensor', 'strip'), may hold values from -0.078125 to 0.078125
- layer_scale: float32 [1536], replicated, may hold values from 0.25 to 2
- dw_kernel: float32 [7, 7, 1536], replicated, may hold values from -0.875 to 0.875
Outputs:
- grad_input: bfloat16 [128, 256, 1536], P('strip', 'tensor')
- grad_w_in: float32 [1536, 6144], P('strip', 'tensor')
- grad_w_out: float32 [6144, 1536], P('tensor', 'strip')
All inputs are finite; a program needn't handle non-finite values.
Results may differ from a plain program's by a relative error of at most 0.0063.
Values may be sent and summed in bfloat16 or wider, within the bound.
No kernel may reach another device: no remote copies, remote signals or barrier semaphores. Data moves between devices by JAX's collectives and lax.ppermute only.
A program may use at most 128 MiB of HBM per device.

v0:
```python
import math

import jax
import jax.numpy as jnp
from jax import lax
from jax.experimental import pallas as pl
from jax.experimental.pallas import tpu as pltpu
from jax.sharding import Mesh
from jax.sharding import PartitionSpec as P

ln_eps = 1e-06
root_half = 0.7071067811865476
density_norm = 0.3989422804014327

FINE = ("zl", "y", "c", "x", "zh")
SIZES = (2, 4, 2, 4, 4)
STRIP = ("zl", "y", "c")
TENSOR = ("x", "zh")
Z = ("zl", "zh")
NX, NY, NZ = 4, 4, 8
CHAN, HIDDEN = 1536, 1536
ROWS, COLS = 96, 384
AY, BY = 32, 64
BLOCK = 128
TOKENS = BLOCK * NX

bf16, f32 = jnp.bfloat16, jnp.float32


def shift(n, k):
    return [(i, (i + k) % n) for i in range(n)]


def to_x(value, k):
    return lax.ppermute(value, "x", shift(NX, k)) if k else value


def to_y(value, k):
    return lax.ppermute(value, "y", shift(NY, k)) if k else value


def exchange_z(value):
    return lax.all_to_all(value, Z, 0, 0, tiled=True)


def gather_bias(value):
    parts = [lax.ppermute(value, "zh", shift(4, -q)) if q else value for q in range(4)]
    twice = jnp.stack(parts + parts)
    start = lax.rem(4 - lax.axis_index("zh"), 4)
    return lax.dynamic_slice_in_dim(twice, start, 4, 0).reshape(1, HIDDEN)


def gather_z(value):
    return exchange_z(jnp.broadcast_to(value, (NZ, *value.shape)))


def swap(value):
    return lax.ppermute(value, "c", shift(2, 1))


def with_halo(block, sides, width):
    for axis, dim in sides:
        count = lax.axis_size(axis)
        forward = [(i, i + 1) for i in range(count - 1)]
        backward = [(target, source) for source, target in forward]
        low = lax.ppermute(
            lax.slice_in_dim(block, block.shape[dim] - width, None, axis=dim), axis, forward
        )
        high = lax.ppermute(lax.slice_in_dim(block, 0, width, axis=dim), axis, backward)
        block = jnp.concatenate([low, block, high], axis=dim)
    return block


def apply_layer_norm(flattened_rows):
    centre = jnp.mean(flattened_rows, axis=-1, keepdims=True)
    centred = flattened_rows - centre
    spread = jnp.mean(centred * centred, axis=-1, keepdims=True)
    inverse_deviation = lax.rsqrt(spread + ln_eps)
    return (centred * inverse_deviation, inverse_deviation)


def layer_norm_backward(normed_gradient, centred_input, inverse_deviation, layer_norm_gain):
    gain_scaled = normed_gradient * layer_norm_gain
    first_moment = jnp.mean(gain_scaled, axis=-1, keepdims=True)
    second_moment = jnp.mean(gain_scaled * centred_input, axis=-1, keepdims=True)
    return inverse_deviation * (gain_scaled - first_moment - centred_input * second_moment)


def transpose_conv(padded, dw_kernel, image_height, image_breadth):
    taps = dw_kernel.shape[0]
    total = jnp.zeros((image_height, image_breadth, padded.shape[2]), jnp.float32)
    for row_tap in range(taps):
        for col_tap in range(taps):
            start_row = taps - 1 - row_tap
            start_col = taps - 1 - col_tap
            total = (
                total
                + dw_kernel[row_tap, col_tap]
                * padded[
                    start_row : start_row + image_height, start_col : start_col + image_breadth
                ]
            )
    return total


def place(where, d, k, r):
    y, c = where[0], where[1]
    row = (k // 4 * 8 + lax.rem(y + r, NY) * 2 + lax.rem(c + d, 2)) * ROWS
    return pl.multiple_of(row, 32), slice(k % 4 * COLS, k % 4 * COLS + COLS)


def compute_kernel(where, *refs):
    n = 0

    def take(count):
        nonlocal n
        n += count
        return refs[n - count : n]

    bias = take(1)[0]
    tok = take(NX)
    first = take(2)
    second = [take(NY), take(NY)]
    out_y = take(2)
    out_z = take(2)
    gn = take(NX)
    w, xs, xt, acts, g = take(5)
    for i in range(NX):
        rows = slice(i * BLOCK, (i + 1) * BLOCK)
        xs[0, rows, :] = tok[i][:BLOCK]
        xs[1, rows, :] = tok[i][BLOCK:]
    for d in range(2):
        for k in range(NZ):
            for r in range(NY):
                row, col = place(where, d, k, r)
                for m in range(2):
                    row2 = pl.multiple_of(row + AY, 32)
                    w[m, pl.ds(row, AY), col] = first[d][k, r, m]
                    w[m, pl.ds(row2, BY), col] = second[d][r][k, m]
    for m in range(2):
        for i in range(CHAN // 256):
            xt[m, i * 256 : (i + 1) * 256, :] = xs[m, :, i * 256 : (i + 1) * 256].T

    width = 256

    def activations(i, _):
        cols = pl.ds(pl.multiple_of(i * width, width), width)
        pre = jnp.dot(xs[0], w[0, :, cols], preferred_element_type=f32) + bias[:, cols]
        back = jnp.dot(xs[1], w[1, :, cols], preferred_element_type=f32)
        cdf = 0.5 * (1.0 + lax.erf(pre * root_half))
        slope = cdf + pre * jnp.exp(-0.5 * pre * pre) * density_norm
        act = (pre * cdf).astype(bf16)
        acts[:, cols] = (back * slope).astype(bf16)
        g[:, cols] = jnp.dot(xt[1], act, preferred_element_type=f32).astype(bf16)
        return 0

    def flush(m):
        for d in range(2):
            for k in range(NZ):
                for r in range(NY):
                    row, col = place(where, d, k, r)
                    row2 = pl.multiple_of(row + AY, 32)
                    out_z[d][k, r, m] = g[pl.ds(row, AY), col]
                    out_y[d][r, k, m] = g[pl.ds(row2, BY), col]

    lax.fori_loop(0, HIDDEN // width, activations, 0)
    flush(1)

    def gradient_in(i, _):
        cols = pl.ds(pl.multiple_of(i * width, width), width)
        g[:, cols] = jnp.dot(xt[0], acts[:, cols], preferred_element_type=f32).astype(bf16)
        return 0

    lax.fori_loop(0, HIDDEN // width, gradient_in, 0)
    flush(0)

    def gradient_normed(i, _):
        cols = pl.ds(pl.multiple_of(i * width, width), width)
        part = lax.dot_general(
            acts[...], w[0, cols, :], (((1,), (1,)), ((), ())), preferred_element_type=f32
        ).astype(bf16)
        for b in range(NX):
            gn[b][:, cols] = part[b * BLOCK : (b + 1) * BLOCK]
        return 0

    lax.fori_loop(0, CHAN // width, gradient_normed, 0)


def compute(where, bias, tok, first, second):
    vmem = pl.BlockSpec(memory_space=pltpu.VMEM)
    gy = jax.ShapeDtypeStruct((NY, NZ, 2, BY, COLS), bf16)
    gz = jax.ShapeDtypeStruct((NZ, NY, 2, AY, COLS), bf16)
    gn = jax.ShapeDtypeStruct((BLOCK, CHAN), bf16)
    operands = [bias, *tok, *first, *second[0], *second[1]]
    out = pl.pallas_call(
        compute_kernel,
        out_shape=[gy, gy, gz, gz] + [gn] * NX,
        in_specs=[pl.BlockSpec(memory_space=pltpu.SMEM)] + [vmem] * len(operands),
        out_specs=[vmem] * (4 + NX),
        scratch_shapes=[
            pltpu.VMEM((2, CHAN, HIDDEN), bf16),
            pltpu.VMEM((2, TOKENS, CHAN), bf16),
            pltpu.VMEM((2, CHAN, TOKENS), bf16),
            pltpu.VMEM((TOKENS, HIDDEN), bf16),
            pltpu.VMEM((CHAN, HIDDEN), bf16),
        ],
        compiler_params=pltpu.CompilerParams(vmem_limit_bytes=60 * 2**20),
        cost_estimate=pl.CostEstimate(
            flops=10 * TOKENS * CHAN * HIDDEN, bytes_accessed=25_000_000, transcendentals=0
        ),
        name="block",
    )(where, *operands)
    return out[0:2], out[2:4], out[4:]


def add_kernel(*refs):
    own_y, got_y, own_z, got_z = refs[:4]
    ys, zs = refs[4 : 4 + NY], refs[4 + NY]
    for r in range(NY):
        for k in range(NZ):
            ys[r][k] = (own_y[r, k].astype(f32) + got_y[r, k].astype(f32)).astype(bf16)
    for k in range(NZ):
        for r in range(NY):
            zs[k, r] = (own_z[k, r].astype(f32) + got_z[k, r].astype(f32)).astype(bf16)


def add_cores(own_y, got_y, own_z, got_z):
    vmem = pl.BlockSpec(memory_space=pltpu.VMEM)
    out = pl.pallas_call(
        add_kernel,
        out_shape=[jax.ShapeDtypeStruct(own_y.shape[1:], bf16)] * NY
        + [jax.ShapeDtypeStruct(own_z.shape, bf16)],
        in_specs=[vmem] * 4,
        out_specs=[vmem] * (NY + 1),
        compiler_params=pltpu.CompilerParams(vmem_limit_bytes=40 * 2**20),
        name="add_cores",
    )(own_y, got_y, own_z, got_z)
    return out[:NY], out[NY]


def sum_y_kernel(*refs):
    for k in range(NZ):
        total = refs[0][k].astype(f32)
        for ref in refs[1:NY]:
            total = total + ref[k].astype(f32)
        refs[NY][k] = total.astype(bf16)


def sum_y(parts):
    vmem = pl.BlockSpec(memory_space=pltpu.VMEM)
    return pl.pallas_call(
        sum_y_kernel,
        out_shape=jax.ShapeDtypeStruct(parts[0].shape, bf16),
        in_specs=[vmem] * NY,
        out_specs=vmem,
        compiler_params=pltpu.CompilerParams(vmem_limit_bytes=24 * 2**20),
        name="sum_y",
    )(*parts)


def sum_z_kernel(parts, *outs):
    for r in range(NY):
        total = parts[0, r].astype(f32)
        for k in range(1, NZ):
            total = total + parts[k, r].astype(f32)
        outs[r][...] = total.astype(bf16)


def sum_z(parts):
    vmem = pl.BlockSpec(memory_space=pltpu.VMEM)
    return pl.pallas_call(
        sum_z_kernel,
        out_shape=[jax.ShapeDtypeStruct(parts.shape[2:], bf16)] * NY,
        in_specs=[vmem],
        out_specs=[vmem] * NY,
        compiler_params=pltpu.CompilerParams(vmem_limit_bytes=24 * 2**20),
        name="sum_z",
    )(parts)


def total(parts):
    result = parts[0].astype(f32)
    for part in parts[1:]:
        result = result + part.astype(f32)
    return result


def body(
    conv_out, out_grad, layer_norm_gain, layer_norm_bias, w_in, b_in, w_out, layer_scale, dw_kernel
):
    tile_rows, tile_cols, channel_count = conv_out.shape
    local_count = tile_rows * tile_cols
    flattened_rows = conv_out.astype(jnp.float32).reshape(local_count, channel_count)
    centred_input, inverse_deviation = apply_layer_norm(flattened_rows)
    normed_output = (centred_input * layer_norm_gain + layer_norm_bias).astype(jnp.bfloat16)
    upstream = out_grad.astype(jnp.float32)
    scaled_grad = (upstream.reshape(local_count, channel_count) * layer_scale).astype(jnp.bfloat16)
    token = jnp.concatenate([normed_output, scaled_grad])
    tok = [to_x(token, -r) for r in range(NX)]

    shards = jnp.stack([w_in, w_out.T])
    lead, rest = shards[:, :AY], shards[:, AY:]
    rest_z = gather_z(rest)
    lead_y = jnp.stack([to_y(lead, -r) for r in range(NY)])
    bias = gather_bias(b_in)
    rest_z, lead_y, bias, tok[1], tok[3] = lax.optimization_barrier(
        (rest_z, lead_y, bias, tok[1], tok[3])
    )
    second = [to_y(rest_z, -r) for r in range(NY)]
    first = gather_z(lead_y)
    second = [second, [swap(v) for v in second]]
    first = [first, swap(first)]

    where = jnp.stack([lax.axis_index("y"), lax.axis_index("c")]).astype(jnp.int32)
    grad_y, grad_z, part = compute(where, bias, tok, first, second)

    ys, zs = add_cores(grad_y[0], swap(grad_y[1]), grad_z[0], swap(grad_z[1]))
    ys, part = list(ys), list(part)
    ys[0], part[2] = lax.optimization_barrier((ys[0], part[2]))
    part = [to_x(v, r) for r, v in enumerate(part)]
    ys = [to_y(v, r) for r, v in enumerate(ys)]
    part[0], ys[1], ys[3] = lax.optimization_barrier((part[0], ys[1], ys[3]))
    normed_gradient = total(part)

    ys = sum_y(ys)
    zs = sum_z(exchange_z(zs))
    zs = [to_y(v, r) for r, v in enumerate(zs)]
    ys = exchange_z(ys)
    total_tokens = local_count * lax.axis_size(STRIP) * lax.axis_size(TENSOR)
    factor = 1.0 / math.sqrt(total_tokens)
    summed = jnp.concatenate([total(zs), total(ys)], axis=1) * factor

    convolution_gradient = (
        layer_norm_backward(normed_gradient, centred_input, inverse_deviation, layer_norm_gain)
        .astype(jnp.bfloat16)
        .reshape(tile_rows, tile_cols, channel_count)
    )
    margin = dw_kernel.shape[0] // 2
    padded = with_halo(convolution_gradient, ((STRIP, 0), (TENSOR, 1)), margin)
    grad_input = (
        upstream + transpose_conv(padded.astype(jnp.float32), dw_kernel, tile_rows, tile_cols)
    ).astype(jnp.bfloat16)
    return (grad_input, summed[0], summed[1].T)


def solution(mesh):
    fine = Mesh(mesh.devices.reshape(SIZES), FINE)
    token = P(STRIP, TENSOR, None)
    return jax.shard_map(
        body,
        mesh=fine,
        in_specs=(
            token,
            token,
            P(),
            P(),
            P(STRIP, TENSOR),
            P(TENSOR),
            P(TENSOR, STRIP),
            P(),
            P(),
        ),
        out_specs=(token, P(STRIP, TENSOR), P(TENSOR, STRIP)),
        check_vma=False,
    )
```

profile of v0, /device:TPU:32, one launch (start us, length us, event | category | flops | bytes accessed | tf_op | source)
XLA Modules:
  0.0 243.2 jit_solution(6477032385838356516)
XLA Ops:
  2.6 8.6 %all-to-all-start = ((bf16[8,2,64,384]{3,2,1,0:T(8,128)(2,1)}), bf16[8,2,64,384]{3,2,1,0:T(8,128)(2,1)S(1)}, u32[]{:S(2)}, u32[]{:S(2)}) async-start(bf16[8,2,64,384]{3,2,1,0:T(8,128)(2,1)} %broadcast_in_dim.4), calls=%async_computation | async-start | bytes 1572864 | tf_op jit(solution)/shard_map/all_to_all | solution.py:43
  12.2 2.8 %collective-permute-start.6 = (bf16[256,1536]{1,0:T(8,128)(2,1)S(1)}, bf16[256,1536]{1,0:T(8,128)(2,1)S(1)}, u32[]{:S(2)}, u32[]{:S(2)}) collective-permute-start(bf16[256,1536]{1,0:T(8,128)(2,1)S(1)} %pad_maximum_fusion.refs_1_), channel_id=1, source_target_pairs={{0,12},{4,0},{8,4},{12,8},{1,13},{5,1},{9,5},{13,9},{2,14},{6,2},{... | collective-permute-start | bytes 2359304 | tf_op jit(solution)/shard_map/ppermute | solution.py:35
  17.7 3.3 %collective-permute-start.4 = (f32[384]{0:T(512)S(1)}, f32[384]{0:T(512)S(1)}, u32[]{:S(2)}, u32[]{:S(2)}) collective-permute-start(f32[384]{0:T(512)S(1)} %copy-done.54), channel_id=1, source_target_pairs={{0,2},{1,3},{2,0},{3,1},{4,6},{5,7},{6,4},{7,5},{8,10},{9,11},{10,... | collective-permute-start | bytes 4616 | tf_op jit(solution)/shard_map/ppermute | solution.py:47
  22.5 7.0 %collective-permute-done.3 = f32[384]{0:T(512)S(1)} collective-permute-done((f32[384]{0:T(512)S(1)}, f32[384]{0:T(512)S(1)}, u32[]{:S(2)}, u32[]{:S(2)}) %collective-permute-start.3) | collective-permute-done | bytes 1568 | tf_op jit(solution)/shard_map/ppermute | solution.py:47
  29.5 3.0 %collective-permute-start = (bf16[2,32,384]{2,1,0:T(8,128)(2,1)S(1)}, bf16[2,32,384]{2,1,0:T(8,128)(2,1)S(1)}, u32[]{:S(2)}, u32[]{:S(2)}) collective-permute-start(bf16[2,32,384]{2,1,0:T(8,128)(2,1)S(1)} %pad_maximum_fusion.5), channel_id=1, source_target_pairs={{0,96},{32,0},{64,32},{96,64},{1,97},{33,1},{65,33},{97,65},{2,98}... | collective-permute-start | bytes 147464 | tf_op jit(solution)/shard_map/ppermute | solution.py:39
  32.8 3.2 %collective-permute-start.1 = (bf16[2,32,384]{2,1,0:T(8,128)(2,1)S(1)}, bf16[2,32,384]{2,1,0:T(8,128)(2,1)S(1)}, u32[]{:S(2)}, u32[]{:S(2)}) collective-permute-start(bf16[2,32,384]{2,1,0:T(8,128)(2,1)S(1)} %pad_maximum_fusion.5), channel_id=1, source_target_pairs={{0,64},{32,96},{64,0},{96,32},{1,65},{33,97},{65,1},{97,33},{2,66}... | collective-permute-start | bytes 147464 | tf_op jit(solution)/shard_map/ppermute | solution.py:39
  38.4 2.9 %collective-permute-done.2 = bf16[2,32,384]{2,1,0:T(8,128)(2,1)S(1)} collective-permute-done((bf16[2,32,384]{2,1,0:T(8,128)(2,1)S(1)}, bf16[2,32,384]{2,1,0:T(8,128)(2,1)S(1)}, u32[]{:S(2)}, u32[]{:S(2)}) %collective-permute-start.2) | collective-permute-done | bytes 49184 | tf_op jit(solution)/shard_map/ppermute | solution.py:39
  43.0 5.1 %all-to-all-start.1 = ((bf16[8,4,2,32,384]{4,3,2,1,0:T(8,128)(2,1)}), bf16[8,4,2,32,384]{4,3,2,1,0:T(8,128)(2,1)S(1)}, u32[]{:S(2)}, u32[]{:S(2)}) async-start(bf16[8,4,2,32,384]{4,3,2,1,0:T(8,128)(2,1)} %broadcast_in_dim.5), calls=%async_computation.1 | async-start | bytes 3145728 | tf_op jit(solution)/shard_map/all_to_all | solution.py:43
  48.1 3.0 %collective-permute-start.8 = (bf16[256,1536]{1,0:T(8,128)(2,1)S(1)}, bf16[256,1536]{1,0:T(8,128)(2,1)}, u32[]{:S(2)}, u32[]{:S(2)}) collective-permute-start(bf16[256,1536]{1,0:T(8,128)(2,1)S(1)} %pad_maximum_fusion.refs_1_), channel_id=1, source_target_pairs={{0,8},{4,12},{8,0},{12,4},{1,9},{5,13},{9,1},{13,5},{2,10},{6,14},... | collective-permute-start | bytes 2359304 | tf_op jit(solution)/shard_map/ppermute | solution.py:35
  53.2 29.9 %all-to-all-done.1.refs_5_ = bf16[8,4,2,32,384]{4,3,2,1,0:T(8,128)(2,1)S(1)} async-done(((bf16[8,4,2,32,384]{4,3,2,1,0:T(8,128)(2,1)}), bf16[8,4,2,32,384]{4,3,2,1,0:T(8,128)(2,1)S(1)}, u32[]{:S(2)}, u32[]{:S(2)}) %all-to-all-start.1) | async-done | bytes 1572896 | tf_op jit(solution)/shard_map/all_to_all | solution.py:43
  85.5 2.9 %collective-permute-done.13.refs_11_ = bf16[8,2,64,384]{3,2,1,0:T(8,128)(2,1)S(1)} collective-permute-done((bf16[8,2,64,384]{3,2,1,0:T(8,128)(2,1)S(1)}, bf16[8,2,64,384]{3,2,1,0:T(8,128)(2,1)S(1)}, u32[]{:S(2)}, u32[]{:S(2)}) %collective-permute-start.13) | collective-permute-done | bytes 786464 | tf_op jit(solution)/shard_map/ppermute | solution.py:58
  91.4 27.6 %block.1 = (bf16[4,8,2,64,384]{4,3,2,1,0:T(8,128)(2,1)}, bf16[4,8,2,64,384]{4,3,2,1,0:T(8,128)(2,1)}, bf16[8,4,2,32,384]{4,3,2,1,0:T(8,128)(2,1)}, bf16[8,4,2,32...) custom-call(s32[2]{0:T(128)} %pad_add_fusion.where, ...), custom_call_target="tpu_custom_call" | custom-call | flops 12079595520 | bytes 25000000 | tf_op jit(solution)/shard_map/block/pallas_call | solution.py:195
  119.5 7.6 %collective-permute-done.18.refs_3_ = bf16[8,4,2,32,384]{4,3,2,1,0:T(8,128)(2,1)S(1)} collective-permute-done((bf16[8,4,2,32,384]{4,3,2,1,0:T(8,128)(2,1)}, bf16[8,4,2,32,384]{4,3,2,1,0:T(8,128)(2,1)S(1)}, u32[]{:S(2)}, u32[]{:S(2)}) %collective-permute-start.18) | collective-permute-done | bytes 1572896 | tf_op jit(solution)/shard_map/ppermute | solution.py:58
  133.2 3.2 %collective-permute-start.20 = (bf16[8,2,64,384]{3,2,1,0:T(8,128)(2,1)}, bf16[8,2,64,384]{3,2,1,0:T(8,128)(2,1)}, u32[]{:S(2)}, u32[]{:S(2)}) collective-permute-start(bf16[8,2,64,384]{3,2,1,0:T(8,128)(2,1)} %get-tuple-element.41), channel_id=1, source_target_pairs={{0,96},{32,0},{64,32},{96,64},{1,97},{33,1},{65,33},{97,65},{2,98}... | collective-permute-start | bytes 2359304 | tf_op jit(solution)/shard_map/ppermute | solution.py:39
  141.2 3.7 %all-to-all-start.2 = ((bf16[8,4,2,32,384]{4,3,2,1,0:T(8,128)(2,1)}), bf16[8,4,2,32,384]{4,3,2,1,0:T(8,128)(2,1)S(1)}, u32[]{:S(2)}, u32[]{:S(2)}) async-start(bf16[8,4,2,32,384]{4,3,2,1,0:T(8,128)(2,1)} %get-tuple-element.48), calls=%async_computation.2 | async-start | bytes 3145728 | tf_op jit(solution)/shard_map/all_to_all | solution.py:43
  144.9 9.3 %collective-permute-done.19.refs_1_ = bf16[8,2,64,384]{3,2,1,0:T(8,128)(2,1)S(1)} collective-permute-done((bf16[8,2,64,384]{3,2,1,0:T(8,128)(2,1)}, bf16[8,2,64,384]{3,2,1,0:T(8,128)(2,1)S(1)}, u32[]{:S(2)}, u32[]{:S(2)}) %collective-permute-start.19) | collective-permute-done | bytes 786464 | tf_op jit(solution)/shard_map/ppermute | solution.py:39
  162.0 5.8 %collective-permute-start.25 = (bf16[3,16,1536]{2,1,0:T(8,128)(2,1)S(1)}, bf16[3,16,1536]{2,1,0:T(8,128)(2,1)S(1)}, u32[]{:S(2)}, u32[]{:S(2)}) collective-permute-start(bf16[3,16,1536]{2,1,0:T(8,128)(2,1)S(1)} %bitcast.48), channel_id=1, source_target_pairs={{16,0},{32,16},{48,32},{64,48},{80,64},{96,80},{112,96},{128,112},... | collective-permute-start | bytes 442376 | tf_op jit(solution)/shard_map/ppermute | solution.py:69
  169.5 9.6 %collective-permute-done.24 = bf16[3,16,1536]{2,1,0:T(8,128)(2,1)S(1)} collective-permute-done((bf16[3,16,1536]{2,1,0:T(8,128)(2,1)S(1)}, bf16[3,16,1536]{2,1,0:T(8,128)(2,1)S(1)}, u32[]{:S(2)}, u32[]{:S(2)}) %collective-permute-start.24) | collective-permute-done | bytes 147488 | tf_op jit(solution)/shard_map/ppermute | solution.py:66
  179.1 3.9 %collective-permute-done.25 = bf16[3,16,1536]{2,1,0:T(8,128)(2,1)S(1)} collective-permute-done((bf16[3,16,1536]{2,1,0:T(8,128)(2,1)S(1)}, bf16[3,16,1536]{2,1,0:T(8,128)(2,1)S(1)}, u32[]{:S(2)}, u32[]{:S(2)}) %collective-permute-start.25) | collective-permute-done | bytes 147488 | tf_op jit(solution)/shard_map/ppermute | solution.py:69
  183.2 4.6 %collective-permute-start.26 = (bf16[14,3,1536]{2,1,0:T(4,128)(2,1)S(1)}, bf16[14,3,1536]{2,1,0:T(4,128)(2,1)S(1)}, u32[]{:S(2)}, u32[]{:S(2)}) collective-permute-start(bf16[14,3,1536]{2,1,0:T(4,128)(2,1)S(1)} %get-tuple-element.109), channel_id=1, source_target_pairs={{0,1},{1,2},{2,3},{3,4},{4,5},{5,6},{6,7},{7,8},{8,9},{9,10},{10,1... | collective-permute-start | bytes 387080 | tf_op jit(solution)/shard_map/ppermute | solution.py:66
  192.6 3.8 %collective-permute-done.27 = bf16[14,3,1536]{2,1,0:T(4,128)(2,1)S(1)} collective-permute-done((bf16[14,3,1536]{2,1,0:T(4,128)(2,1)S(1)}, bf16[14,3,1536]{2,1,0:T(4,128)(2,1)S(1)}, u32[]{:S(2)}, u32[]{:S(2)}) %collective-permute-start.27) | collective-permute-done | bytes 129056 | tf_op jit(solution)/shard_map/ppermute | solution.py:69
  198.2 8.7 %all-to-all-start.3 = ((bf16[8,2,64,384]{3,2,1,0:T(8,128)(2,1)}), bf16[8,2,64,384]{3,2,1,0:T(8,128)(2,1)S(1)}, u32[]{:S(2)}, u32[]{:S(2)}) async-start(bf16[8,2,64,384]{3,2,1,0:T(8,128)(2,1)} %sum_y.1), calls=%async_computation.3 | async-start | bytes 1572864 | tf_op jit(solution)/shard_map/all_to_all | solution.py:43
  207.2 28.2 %fusion.2 = bf16[8,16,1536]{2,1,0:T(8,128)(2,1)} fusion(f32[14,22,1536]{2,1,0:T(8,128)} %maximum_convert_fusion, f32[1536]{0:T(1024)S(1)} %get-tuple-element.106, f32[1536]{0:T(1024)S(1)} %get-tuple-element.107, f32[1536]{0:T(1024)S(1)} %get-tuple-element.60, f32[1536]{0:T(1024)S(1)} %copy-done.13, f32[1536]{0:T(1024)S(1)} %copy-done.14, ...), kind=kLoop, calls=%fused_computation.4 | loop fusion | flops 19660800 | bytes 39622656 | tf_op jit(solution)/shard_map/convert_element_type | solution.py:342
  235.8 3.1 %collective-permute-start.30 = (bf16[2,32,384]{2,1,0:T(8,128)(2,1)S(1)}, bf16[2,32,384]{2,1,0:T(8,128)(2,1)S(1)}, u32[]{:S(2)}, u32[]{:S(2)}) collective-permute-start(bf16[2,32,384]{2,1,0:T(8,128)(2,1)S(1)} %get-tuple-element.52), channel_id=1, source_target_pairs={{0,96},{32,0},{64,32},{96,64},{1,97},{33,1},{65,33},{97,65},{2,98}... | collective-permute-start | bytes 147464 | tf_op jit(solution)/shard_map/ppermute | solution.py:39
  (203 shorter events, 50.8 us)
Async XLA Ops:
  2.6 38.8 %all-to-all-start = ((bf16[8,2,64,384]{3,2,1,0:T(8,128)(2,1)}), bf16[8,2,64,384]{3,2,1,0:T(8,128)(2,1)S(1)}, u32[]{:S(2)}, u32[]{:S(2)}) async-start(bf16[8,2,64,384]{3,2,1,0:T(8,128)(2,1)} %broadcast_in_dim.4), calls=%async_computation | async-start | bytes 1572864 | tf_op jit(solution)/shard_map/all_to_all | solution.py:43
  12.2 29.1 %collective-permute-start.6 = (bf16[256,1536]{1,0:T(8,128)(2,1)S(1)}, bf16[256,1536]{1,0:T(8,128)(2,1)S(1)}, u32[]{:S(2)}, u32[]{:S(2)}) collective-permute-start(bf16[256,1536]{1,0:T(8,128)(2,1)S(1)} %pad_maximum_fusion.refs_1_), channel_id=1, source_target_pairs={{0,12},{4,0},{8,4},{12,8},{1,13},{5,1},{9,5},{13,9},{2,14},{6,2},{... | collective-permute-start | bytes 2359304 | tf_op jit(solution)/shard_map/ppermute | solution.py:35
  15.0 26.3 %collective-permute-start.7 = (bf16[256,1536]{1,0:T(8,128)(2,1)S(1)}, bf16[256,1536]{1,0:T(8,128)(2,1)}, u32[]{:S(2)}, u32[]{:S(2)}) collective-permute-start(bf16[256,1536]{1,0:T(8,128)(2,1)S(1)} %pad_maximum_fusion.refs_1_), channel_id=1, source_target_pairs={{0,4},{4,8},{8,12},{12,0},{1,5},{5,9},{9,13},{13,1},{2,6},{6,10},{... | collective-permute-start | bytes 2359304 | tf_op jit(solution)/shard_map/ppermute | solution.py:35
  15.0 14.4 %collective-permute-start.3 = (f32[384]{0:T(512)S(1)}, f32[384]{0:T(512)S(1)}, u32[]{:S(2)}, u32[]{:S(2)}) collective-permute-start(f32[384]{0:T(512)S(1)} %copy-done.54), channel_id=1, source_target_pairs={{0,3},{1,0},{2,1},{3,2},{4,7},{5,4},{6,5},{7,6},{8,11},{9,8},{10,9... | collective-permute-start | bytes 4616 | tf_op jit(solution)/shard_map/ppermute | solution.py:47
  17.7 15.1 %collective-permute-start.4 = (f32[384]{0:T(512)S(1)}, f32[384]{0:T(512)S(1)}, u32[]{:S(2)}, u32[]{:S(2)}) collective-permute-start(f32[384]{0:T(512)S(1)} %copy-done.54), channel_id=1, source_target_pairs={{0,2},{1,3},{2,0},{3,1},{4,6},{5,7},{6,4},{7,5},{8,10},{9,11},{10,... | collective-permute-start | bytes 4616 | tf_op jit(solution)/shard_map/ppermute | solution.py:47
  21.0 15.0 %collective-permute-start.5 = (f32[384]{0:T(512)S(1)}, f32[384]{0:T(512)S(1)}, u32[]{:S(2)}, u32[]{:S(2)}) collective-permute-start(f32[384]{0:T(512)S(1)} %copy-done.54), channel_id=1, source_target_pairs={{0,1},{1,2},{2,3},{3,0},{4,5},{5,6},{6,7},{7,4},{8,9},{9,10},{10,1... | collective-permute-start | bytes 4616 | tf_op jit(solution)/shard_map/ppermute | solution.py:47
  43.0 40.1 %all-to-all-start.1 = ((bf16[8,4,2,32,384]{4,3,2,1,0:T(8,128)(2,1)}), bf16[8,4,2,32,384]{4,3,2,1,0:T(8,128)(2,1)S(1)}, u32[]{:S(2)}, u32[]{:S(2)}) async-start(bf16[8,4,2,32,384]{4,3,2,1,0:T(8,128)(2,1)} %broadcast_in_dim.5), calls=%async_computation.1 | async-start | bytes 3145728 | tf_op jit(solution)/shard_map/all_to_all | solution.py:43
  48.1 35.0 %collective-permute-start.8 = (bf16[256,1536]{1,0:T(8,128)(2,1)S(1)}, bf16[256,1536]{1,0:T(8,128)(2,1)}, u32[]{:S(2)}, u32[]{:S(2)}) collective-permute-start(bf16[256,1536]{1,0:T(8,128)(2,1)S(1)} %pad_maximum_fusion.refs_1_), channel_id=1, source_target_pairs={{0,8},{4,12},{8,0},{12,4},{1,9},{5,13},{9,1},{13,5},{2,10},{6,14},... | collective-permute-start | bytes 2359304 | tf_op jit(solution)/shard_map/ppermute | solution.py:35
  51.1 32.5 %collective-permute-start.10 = (bf16[8,2,64,384]{3,2,1,0:T(8,128)(2,1)S(1)}, bf16[8,2,64,384]{3,2,1,0:T(8,128)(2,1)}, u32[]{:S(2)}, u32[]{:S(2)}) collective-permute-start(bf16[8,2,64,384]{3,2,1,0:T(8,128)(2,1)S(1)} %all-to-all-done.refs_7_), channel_id=1, source_target_pairs={{0,96},{32,0},{64,32},{96,64},{1,97},{33,1},{65,33},{97,65},{2,98}... | collective-permute-start | bytes 2359304 | tf_op jit(solution)/shard_map/ppermute | solution.py:39
  51.2 32.5 %collective-permute-start.11 = (bf16[8,2,64,384]{3,2,1,0:T(8,128)(2,1)S(1)}, bf16[8,2,64,384]{3,2,1,0:T(8,128)(2,1)}, u32[]{:S(2)}, u32[]{:S(2)}) collective-permute-start(bf16[8,2,64,384]{3,2,1,0:T(8,128)(2,1)S(1)} %all-to-all-done.refs_7_), channel_id=1, source_target_pairs={{0,64},{32,96},{64,0},{96,32},{1,65},{33,97},{65,1},{97,33},{2,66}... | collective-permute-start | bytes 2359304 | tf_op jit(solution)/shard_map/ppermute | solution.py:39
  52.7 32.2 %collective-permute-start.12 = (bf16[8,2,64,384]{3,2,1,0:T(8,128)(2,1)S(1)}, bf16[8,2,64,384]{3,2,1,0:T(8,128)(2,1)}, u32[]{:S(2)}, u32[]{:S(2)}) collective-permute-start(bf16[8,2,64,384]{3,2,1,0:T(8,128)(2,1)S(1)} %all-to-all-done.refs_7_), channel_id=1, source_target_pairs={{0,32},{32,64},{64,96},{96,0},{1,33},{33,65},{65,97},{97,1},{2,34}... | collective-permute-start | bytes 2359304 | tf_op jit(solution)/shard_map/ppermute | solution.py:39
  83.1 8.3 %collective-permute-start.9 = (bf16[8,4,2,32,384]{4,3,2,1,0:T(8,128)(2,1)S(1)}, bf16[8,4,2,32,384]{4,3,2,1,0:T(8,128)(2,1)}, u32[]{:S(2)}, u32[]{:S(2)}) collective-permute-start(bf16[8,4,2,32,384]{4,3,2,1,0:T(8,128)(2,1)S(1)} %all-to-all-done.1.refs_5_), channel_id=1, source_target_pairs={{0,16},{16,0},{1,17},{17,1},{2,18},{18,2},{3,19},{19,3},{4,20},{20... | collective-permute-start | bytes 4718600 | tf_op jit(solution)/shard_map/ppermute | solution.py:58
  133.2 21.0 %collective-permute-start.19 = (bf16[8,2,64,384]{3,2,1,0:T(8,128)(2,1)}, bf16[8,2,64,384]{3,2,1,0:T(8,128)(2,1)S(1)}, u32[]{:S(2)}, u32[]{:S(2)}) collective-permute-start(bf16[8,2,64,384]{3,2,1,0:T(8,128)(2,1)} %get-tuple-element.40), channel_id=1, source_target_pairs={{0,32},{32,64},{64,96},{96,0},{1,33},{33,65},{65,97},{97,1},{2,34}... | collective-permute-start | bytes 2359304 | tf_op jit(solution)/shard_map/ppermute | solution.py:39
  133.2 21.4 %collective-permute-start.20 = (bf16[8,2,64,384]{3,2,1,0:T(8,128)(2,1)}, bf16[8,2,64,384]{3,2,1,0:T(8,128)(2,1)}, u32[]{:S(2)}, u32[]{:S(2)}) collective-permute-start(bf16[8,2,64,384]{3,2,1,0:T(8,128)(2,1)} %get-tuple-element.41), channel_id=1, source_target_pairs={{0,96},{32,0},{64,32},{96,64},{1,97},{33,1},{65,33},{97,65},{2,98}... | collective-permute-start | bytes 2359304 | tf_op jit(solution)/shard_map/ppermute | solution.py:39
  136.4 18.2 %collective-permute-start.21 = (bf16[128,1536]{1,0:T(8,128)(2,1)}, bf16[128,1536]{1,0:T(8,128)(2,1)}, u32[]{:S(2)}, u32[]{:S(2)}) collective-permute-start(bf16[128,1536]{1,0:T(8,128)(2,1)} %get-tuple-element.43), channel_id=1, source_target_pairs={{0,4},{4,8},{8,12},{12,0},{1,5},{5,9},{9,13},{13,1},{2,6},{6,10},{... | collective-permute-start | bytes 1179656 | tf_op jit(solution)/shard_map/ppermute | solution.py:35
  137.6 18.6 %collective-permute-start.23 = (bf16[128,1536]{1,0:T(8,128)(2,1)}, bf16[128,1536]{1,0:T(8,128)(2,1)}, u32[]{:S(2)}, u32[]{:S(2)}) collective-permute-start(bf16[128,1536]{1,0:T(8,128)(2,1)} %get-tuple-element.47), channel_id=1, source_target_pairs={{0,12},{4,0},{8,4},{12,8},{1,13},{5,1},{9,5},{13,9},{2,14},{6,2},{... | collective-permute-start | bytes 1179656 | tf_op jit(solution)/shard_map/ppermute | solution.py:35
  139.7 18.2 %collective-permute-start.22 = (bf16[128,1536]{1,0:T(8,128)(2,1)}, bf16[128,1536]{1,0:T(8,128)(2,1)}, u32[]{:S(2)}, u32[]{:S(2)}) collective-permute-start(bf16[128,1536]{1,0:T(8,128)(2,1)} %get-tuple-element.46), channel_id=1, source_target_pairs={{0,8},{4,12},{8,0},{12,4},{1,9},{5,13},{9,1},{13,5},{2,10},{6,14},... | collective-permute-start | bytes 1179656 | tf_op jit(solution)/shard_map/ppermute | solution.py:35
  141.2 57.0 %all-to-all-start.2 = ((bf16[8,4,2,32,384]{4,3,2,1,0:T(8,128)(2,1)}), bf16[8,4,2,32,384]{4,3,2,1,0:T(8,128)(2,1)S(1)}, u32[]{:S(2)}, u32[]{:S(2)}) async-start(bf16[8,4,2,32,384]{4,3,2,1,0:T(8,128)(2,1)} %get-tuple-element.48), calls=%async_computation.2 | async-start | bytes 3145728 | tf_op jit(solution)/shard_map/all_to_all | solution.py:43
  154.2 35.6 %collective-permute-start.31 = (bf16[8,2,64,384]{3,2,1,0:T(8,128)(2,1)}, bf16[8,2,64,384]{3,2,1,0:T(8,128)(2,1)S(1)}, u32[]{:S(2)}, u32[]{:S(2)}) collective-permute-start(bf16[8,2,64,384]{3,2,1,0:T(8,128)(2,1)} %copy-done.2), channel_id=1, source_target_pairs={{0,64},{32,96},{64,0},{96,32},{1,65},{33,97},{65,1},{97,33},{2,66}... | collective-permute-start | bytes 2359304 | tf_op jit(solution)/shard_map/ppermute | solution.py:39
  160.0 19.1 %collective-permute-start.24 = (bf16[3,16,1536]{2,1,0:T(8,128)(2,1)S(1)}, bf16[3,16,1536]{2,1,0:T(8,128)(2,1)S(1)}, u32[]{:S(2)}, u32[]{:S(2)}) collective-permute-start(bf16[3,16,1536]{2,1,0:T(8,128)(2,1)S(1)} %bitcast.49), channel_id=1, source_target_pairs={{0,16},{16,32},{32,48},{48,64},{64,80},{80,96},{96,112},{112,128},... | collective-permute-start | bytes 442376 | tf_op jit(solution)/shard_map/ppermute | solution.py:66
  162.0 21.1 %collective-permute-start.25 = (bf16[3,16,1536]{2,1,0:T(8,128)(2,1)S(1)}, bf16[3,16,1536]{2,1,0:T(8,128)(2,1)S(1)}, u32[]{:S(2)}, u32[]{:S(2)}) collective-permute-start(bf16[3,16,1536]{2,1,0:T(8,128)(2,1)S(1)} %bitcast.48), channel_id=1, source_target_pairs={{16,0},{32,16},{48,32},{64,48},{80,64},{96,80},{112,96},{128,112},... | collective-permute-start | bytes 442376 | tf_op jit(solution)/shard_map/ppermute | solution.py:69
  183.2 9.5 %collective-permute-start.26 = (bf16[14,3,1536]{2,1,0:T(4,128)(2,1)S(1)}, bf16[14,3,1536]{2,1,0:T(4,128)(2,1)S(1)}, u32[]{:S(2)}, u32[]{:S(2)}) collective-permute-start(bf16[14,3,1536]{2,1,0:T(4,128)(2,1)S(1)} %get-tuple-element.109), channel_id=1, source_target_pairs={{0,1},{1,2},{2,3},{3,4},{4,5},{5,6},{6,7},{7,8},{8,9},{9,10},{10,1... | collective-permute-start | bytes 387080 | tf_op jit(solution)/shard_map/ppermute | solution.py:66
  187.7 8.7 %collective-permute-start.27 = (bf16[14,3,1536]{2,1,0:T(4,128)(2,1)S(1)}, bf16[14,3,1536]{2,1,0:T(4,128)(2,1)S(1)}, u32[]{:S(2)}, u32[]{:S(2)}) collective-permute-start(bf16[14,3,1536]{2,1,0:T(4,128)(2,1)S(1)} %get-tuple-element.110), channel_id=1, source_target_pairs={{1,0},{2,1},{3,2},{4,3},{5,4},{6,5},{7,6},{8,7},{9,8},{10,9},{11,1... | collective-permute-start | bytes 387080 | tf_op jit(solution)/shard_map/ppermute | solution.py:69
  198.2 40.8 %all-to-all-start.3 = ((bf16[8,2,64,384]{3,2,1,0:T(8,128)(2,1)}), bf16[8,2,64,384]{3,2,1,0:T(8,128)(2,1)S(1)}, u32[]{:S(2)}, u32[]{:S(2)}) async-start(bf16[8,2,64,384]{3,2,1,0:T(8,128)(2,1)} %sum_y.1), calls=%async_computation.3 | async-start | bytes 1572864 | tf_op jit(solution)/shard_map/all_to_all | solution.py:43
  (69 other events, 849.8 us)
where the time goes:
time: 244 us; the launch traced here: 243 us
  waiting for transfers between devices  88.5 us (36%)
  starting transfers between devices  75.1 us (31%)
  other arithmetic  34.7 us (14%)
  Pallas kernels  32.2 us (13%)
  local copies, waits for them, and re-layouts  11.1 us (5%)
    all_to_all x4, waiting for transfers between devices, exchange_z(): return lax.all_to_all(value, Z, 0, 0, tiled=True)  29.9 us
    convert_element_type x1, other arithmetic, body(): grad_input = (upstream + transpose_conv(padded.astype(jnp.float32), dw_ke...  28.2 us
    pallas_call x1, Pallas kernels, compute(): pl.pallas_call(compute_kernel, out_shape=[gy, gy, gz, gz] + [gn] * NX, in...  27.6 us
    all_to_all x4, starting transfers between devices, exchange_z(): return lax.all_to_all(value, Z, 0, 0, tiled=True)  26.1 us
    ppermute x12, waiting for transfers between devices, to_y(): return lax.ppermute(value, 'y', shift(NY, k)) if k else value  17.3 us
    ppermute x12, starting transfers between devices, to_y(): return lax.ppermute(value, 'y', shift(NY, k)) if k else value  15.9 us
    ppermute x7, waiting for transfers between devices, swap(): return lax.ppermute(value, 'c', shift(2, 1))  13.5 us
    ppermute x6, starting transfers between devices, to_x(): return lax.ppermute(value, 'x', shift(NX, k)) if k else value  10.6 us
  transfers between devices with their start and end apart: 36, of which 19 were waited for; matrix products, arithmetic and copies ran while one was open for 15% of the time, Pallas kernels for 1%

commit v1 on v0

--- a/solution.py
+++ b/solution.py
@@ -43,11 +43,13 @@
     return lax.all_to_all(value, Z, 0, 0, tiled=True)
 
 
-def gather_bias(value):
-    parts = [lax.ppermute(value, "zh", shift(4, -q)) if q else value for q in range(4)]
-    twice = jnp.stack(parts + parts)
-    start = lax.rem(4 - lax.axis_index("zh"), 4)
-    return lax.dynamic_slice_in_dim(twice, start, 4, 0).reshape(1, HIDDEN)
+def bias_rows(bias):
+    rows = []
+    for _ in range(3):
+        term = lax.reduce_precision(bias, 8, 7)
+        rows.append(term.astype(bf16))
+        bias = bias - term
+    return jnp.concatenate([jnp.stack(rows), jnp.zeros((13, COLS), bf16)])
 
 
 def gather_z(value):
@@ -58,49 +60,138 @@
     return lax.ppermute(value, "c", shift(2, 1))
 
 
-def with_halo(block, sides, width):
-    for axis, dim in sides:
-        count = lax.axis_size(axis)
-        forward = [(i, i + 1) for i in range(count - 1)]
-        backward = [(target, source) for source, target in forward]
-        low = lax.ppermute(
-            lax.slice_in_dim(block, block.shape[dim] - width, None, axis=dim), axis, forward
-        )
-        high = lax.ppermute(lax.slice_in_dim(block, 0, width, axis=dim), axis, backward)
-        block = jnp.concatenate([low, block, high], axis=dim)
-    return block
-
-
-def apply_layer_norm(flattened_rows):
-    centre = jnp.mean(flattened_rows, axis=-1, keepdims=True)
-    centred = flattened_rows - centre
-    spread = jnp.mean(centred * centred, axis=-1, keepdims=True)
-    inverse_deviation = lax.rsqrt(spread + ln_eps)
-    return (centred * inverse_deviation, inverse_deviation)
-
-
-def layer_norm_backward(normed_gradient, centred_input, inverse_deviation, layer_norm_gain):
-    gain_scaled = normed_gradient * layer_norm_gain
-    first_moment = jnp.mean(gain_scaled, axis=-1, keepdims=True)
-    second_moment = jnp.mean(gain_scaled * centred_input, axis=-1, keepdims=True)
-    return inverse_deviation * (gain_scaled - first_moment - centred_input * second_moment)
-
-
-def transpose_conv(padded, dw_kernel, image_height, image_breadth):
-    taps = dw_kernel.shape[0]
-    total = jnp.zeros((image_height, image_breadth, padded.shape[2]), jnp.float32)
-    for row_tap in range(taps):
-        for col_tap in range(taps):
-            start_row = taps - 1 - row_tap
-            start_col = taps - 1 - col_tap
-            total = (
-                total
-                + dw_kernel[row_tap, col_tap]
-                * padded[
-                    start_row : start_row + image_height, start_col : start_col + image_breadth
-                ]
-            )
-    return total
+HALO = (
+    (1, 0, slice(5, 8), slice(0, 16)),
+    (-1, 0, slice(0, 3), slice(0, 16)),
+    (0, 1, slice(0, 8), slice(13, 16)),
+    (0, -1, slice(0, 8), slice(0, 3)),
+    (1, 1, slice(5, 8), slice(13, 16)),
+    (1, -1, slice(5, 8), slice(0, 3)),
+    (-1, 1, slice(0, 3), slice(13, 16)),
+    (-1, -1, slice(0, 3), slice(0, 3)),
+)
+TILE_ROWS, TILE_COLS, TAPS, MARGIN = 8, 16, 7, 3
+
+
+def to_tile(value, down, right):
+    pairs = [
+        (s * 16 + t, (s + down) * 16 + t + right)
+        for s in range(16)
+        for t in range(16)
+        if 0 <= s + down < 16 and 0 <= t + right < 16
+    ]
+    return lax.ppermute(value, FINE, pairs)
+
+
+def vmem_specs(count):
+    return [pl.BlockSpec(memory_space=pltpu.VMEM)] * count
+
+
+def norm_kernel(x, grad, gain, bias, scale, token, xhat, inverse):
+    for i in range(0, BLOCK, 16):
+        rows = slice(i, i + 16)
+        value = x[rows].astype(f32)
+        value = value - jnp.mean(value, axis=-1, keepdims=True)
+        inv = lax.rsqrt(jnp.mean(value * value, axis=-1, keepdims=True) + ln_eps)
+        value = value * inv
+        xhat[rows] = value
+        inverse[rows] = inv
+        token[rows] = (value * gain[...] + bias[...]).astype(bf16)
+        token[i + BLOCK : i + BLOCK + 16] = (grad[rows].astype(f32) * scale[...]).astype(bf16)
+
+
+def layer_norm(x, grad, gain, bias, scale):
+    return pl.pallas_call(
+        norm_kernel,
+        out_shape=[
+            jax.ShapeDtypeStruct((2 * BLOCK, CHAN), bf16),
+            jax.ShapeDtypeStruct((BLOCK, CHAN), f32),
+            jax.ShapeDtypeStruct((BLOCK, 1), f32),
+        ],
+        in_specs=vmem_specs(5),
+        out_specs=vmem_specs(3),
+        compiler_params=pltpu.CompilerParams(vmem_limit_bytes=16 * 2**20),
+        name="layer_norm",
+    )(x, grad, gain, bias, scale)
+
+
+def norm_backward_kernel(*refs):
+    parts, (xhat, inverse, gain, out), halos = refs[:NX], refs[NX : NX + 4], refs[NX + 4 :]
+    for i in range(TILE_ROWS):
+        rows = slice(i * TILE_COLS, (i + 1) * TILE_COLS)
+        value = parts[0][rows].astype(f32)
+        for part in parts[1:]:
+            value = value + part[rows].astype(f32)
+        value = value * gain[...]
+        hat = xhat[rows]
+        first = jnp.mean(value, axis=-1, keepdims=True)
+        second = jnp.mean(value * hat, axis=-1, keepdims=True)
+        value = inverse[rows] * (value - first - hat * second)
+        out[i] = value.astype(bf16)
+        for (_, _, height, breadth), halo in zip(HALO, halos, strict=True):
+            if height.start <= i < height.stop:
+                halo[i - height.start] = value[breadth].astype(bf16)
+
+
+def layer_norm_backward(parts, xhat, inverse, gain):
+    return pl.pallas_call(
+        norm_backward_kernel,
+        out_shape=[jax.ShapeDtypeStruct((TILE_ROWS, TILE_COLS, CHAN), bf16)]
+        + [
+            jax.ShapeDtypeStruct((h.stop - h.start, b.stop - b.start, CHAN), bf16)
+            for _, _, h, b in HALO
+        ],
+        in_specs=vmem_specs(NX + 3),
+        out_specs=vmem_specs(9),
+        compiler_params=pltpu.CompilerParams(vmem_limit_bytes=16 * 2**20),
+        name="layer_norm_backward",
+    )(*parts, xhat, inverse, gain)
+
+
+def conv_kernel(own, up, down, left, right, ul, ur, dl, dr, kernel, grad, out, pad):
+    low, mid, high = slice(0, 3), slice(3, 11), slice(11, 14)
+    west, here, east = slice(0, 3), slice(3, 19), slice(19, 22)
+    for rows, cols, ref in (
+        (mid, here, own),
+        (low, here, up),
+        (high, here, down),
+        (mid, west, left),
+        (mid, east, right),
+        (low, west, ul),
+        (low, east, ur),
+        (high, west, dl),
+        (high, east, dr),
+    ):
+        pad[rows, cols, :] = ref[...].astype(f32)
+    total = None
+    for col_tap in range(TAPS):
+        column = pad[:, TAPS - 1 - col_tap : TAPS - 1 - col_tap + TILE_COLS, :]
+        for row_tap in range(TAPS):
+            start = TAPS - 1 - row_tap
+            n = row_tap * TAPS + col_tap
+            term = column[start : start + TILE_ROWS] * kernel[n : n + 1, :][None]
+            total = term if total is None else total + term
+    out[...] = (grad[...].astype(f32) + total).astype(bf16)
+
+
+def convolution(own, halos, kernel, grad):
+    width = 128
+
+    def spec(shape):
+        lead = (0,) * (len(shape) - 1)
+        return pl.BlockSpec((*shape[:-1], width), lambda i: (*lead, i))
+
+    operands = [own, *halos, kernel, grad]
+    return pl.pallas_call(
+        conv_kernel,
+        grid=(CHAN // width,),
+        out_shape=jax.ShapeDtypeStruct(grad.shape, bf16),
+        in_specs=[spec(v.shape) for v in operands],
+        out_specs=spec(grad.shape),
+        scratch_shapes=[pltpu.VMEM((14, 24, width), f32)],
+        compiler_params=pltpu.CompilerParams(vmem_limit_bytes=8 * 2**20),
+        name="convolution",
+    )(*operands)
 
 
 def place(where, d, k, r):
@@ -288,24 +379,21 @@
 def body(
     conv_out, out_grad, layer_norm_gain, layer_norm_bias, w_in, b_in, w_out, layer_scale, dw_kernel
 ):
-    tile_rows, tile_cols, channel_count = conv_out.shape
-    local_count = tile_rows * tile_cols
-    flattened_rows = conv_out.astype(jnp.float32).reshape(local_count, channel_count)
-    centred_input, inverse_deviation = apply_layer_norm(flattened_rows)
-    normed_output = (centred_input * layer_norm_gain + layer_norm_bias).astype(jnp.bfloat16)
-    upstream = out_grad.astype(jnp.float32)
-    scaled_grad = (upstream.reshape(local_count, channel_count) * layer_scale).astype(jnp.bfloat16)
-    token = jnp.concatenate([normed_output, scaled_grad])
+    gain, shift_row, scale = (
+        v.reshape(1, CHAN) for v in (layer_norm_gain, layer_norm_bias, layer_scale)
+    )
+    token, xhat, inverse = layer_norm(
+        conv_out.reshape(BLOCK, CHAN), out_grad.reshape(BLOCK, CHAN), gain, shift_row, scale
+    )
     tok = [to_x(token, -r) for r in range(NX)]
 
     shards = jnp.stack([w_in, w_out.T])
     lead, rest = shards[:, :AY], shards[:, AY:]
-    rest_z = gather_z(rest)
+    got = gather_z(jnp.concatenate([rest.reshape(2 * BY, COLS), bias_rows(b_in)]))
     lead_y = jnp.stack([to_y(lead, -r) for r in range(NY)])
-    bias = gather_bias(b_in)
-    rest_z, lead_y, bias, tok[1], tok[3] = lax.optimization_barrier(
-        (rest_z, lead_y, bias, tok[1], tok[3])
-    )
+    got, lead_y, tok[1], tok[3] = lax.optimization_barrier((got, lead_y, tok[1], tok[3]))
+    rest_z = got[:, : 2 * BY].reshape(NZ, 2, BY, COLS)
+    bias = jnp.sum(got[:4, 2 * BY : 2 * BY + 3].astype(f32), axis=1).reshape(1, HIDDEN)
     second = [to_y(rest_z, -r) for r in range(NY)]
     first = gather_z(lead_y)
     second = [second, [swap(v) for v in second]]
@@ -314,32 +402,24 @@
     where = jnp.stack([lax.axis_index("y"), lax.axis_index("c")]).astype(jnp.int32)
     grad_y, grad_z, part = compute(where, bias, tok, first, second)
 
-    ys, zs = add_cores(grad_y[0], swap(grad_y[1]), grad_z[0], swap(grad_z[1]))
-    ys, part = list(ys), list(part)
-    ys[0], part[2] = lax.optimization_barrier((ys[0], part[2]))
     part = [to_x(v, r) for r, v in enumerate(part)]
+    other_y, other_z, part[1], part[3] = lax.optimization_barrier(
+        (swap(grad_y[1]), swap(grad_z[1]), part[1], part[3])
+    )
+    ys, zs = add_cores(grad_y[0], other_y, grad_z[0], other_z)
     ys = [to_y(v, r) for r, v in enumerate(ys)]
-    part[0], ys[1], ys[3] = lax.optimization_barrier((part[0], ys[1], ys[3]))
-    normed_gradient = total(part)
-
+    own, *halos = layer_norm_backward(part, xhat, inverse, gain)
+    halos = [to_tile(v, *where[:2]) for v, where in zip(halos, HALO, strict=True)]
     ys = sum_y(ys)
+    ys, own, *halos = lax.optimization_barrier((ys, own, *halos))
     zs = sum_z(exchange_z(zs))
+    own, *zs = lax.optimization_barrier((own, *zs))
     zs = [to_y(v, r) for r, v in enumerate(zs)]
     ys = exchange_z(ys)
-    total_tokens = local_count * lax.axis_size(STRIP) * lax.axis_size(TENSOR)
-    factor = 1.0 / math.sqrt(total_tokens)
+    grad_input = convolution(own, halos, dw_kernel.reshape(TAPS * TAPS, CHAN), out_grad)
+    grad_input, ys = lax.optimization_barrier((grad_input, ys))
+    factor = 1.0 / math.sqrt(BLOCK * lax.axis_size(FINE))
     summed = jnp.concatenate([total(zs), total(ys)], axis=1) * factor
-
-    convolution_gradient = (
-        layer_norm_backward(normed_gradient, centred_input, inverse_deviation, layer_norm_gain)
-        .astype(jnp.bfloat16)
-        .reshape(tile_rows, tile_cols, channel_count)
-    )
-    margin = dw_kernel.shape[0] // 2
-    padded = with_halo(convolution_gradient, ((STRIP, 0), (TENSOR, 1)), margin)
-    grad_input = (
-        upstream + transpose_conv(padded.astype(jnp.float32), dw_kernel, tile_rows, tile_cols)
-    ).astype(jnp.bfloat16)
     return (grad_input, summed[0], summed[1].T)
 
 

time: 244 us -> 240 us (0.984)
  other arithmetic: 34.7 us -> 3.59 us
  local copies, waits for them, and re-layouts: 11.1 us -> 21.6 us
  waiting for transfers between devices: 88.5 us -> 96.7 us
  Pallas kernels: 32.2 us -> 37.7 us
  starting transfers between devices: 75.1 us -> 78.6 us
    convert_element_type x4 -> x1, other arithmetic: 30.6 us -> 0.69 us  [bias_rows(): rows.append(term.astype(bf16))]
    ppermute x6, waiting for transfers between devices: 3.22 us -> 28.7 us  [to_x(): return lax.ppermute(value, 'x', shift(NX, k)) if k else value]
    all_to_all x4, waiting for transfers between devices: 29.9 us -> 41.3 us  [exchange_z(): return lax.all_to_all(value, Z, 0, 0, tiled=True)]
    ppermute x7, waiting for transfers between devices: 13.5 us -> 2.23 us  [swap(): return lax.ppermute(value, 'c', shift(2, 1))]
    unnamed x116 -> x81, local copies, waits for them, and re-layouts: 5.05 us -> 16.2 us
    ppermute x12, waiting for transfers between devices: 17.3 us -> 8.27 us  [to_y(): return lax.ppermute(value, 'y', shift(NY, k)) if k else value]
    ppermute x7 -> x8, waiting for transfers between devices: 24.6 us -> 16.1 us  [to_tile(): return lax.ppermute(value, FINE, pairs)]
    pallas_call x0 -> x3, Pallas kernels: none -> 6.65 us  [the longest x1 5.68 us: convolution(): pl.pallas_call(conv_kernel, grid=(CHAN // width,), out_shape=jax.ShapeDty...]
  transfers between devices with their start and end apart: 36 -> 37, of which waited for: 19 -> 15; matrix products, arithmetic and copies ran while one was open for 15% -> 2% of each run, Pallas kernels for 1% -> 4%
where the time goes in v1:
time: 240 us; the launch traced here: 239 us
  waiting for transfers between devices  96.7 us (40%)
  starting transfers between devices  78.6 us (33%)
  Pallas kernels  37.7 us (16%)
  local copies, waits for them, and re-layouts  21.6 us (9%)
  other arithmetic  3.59 us (1%)
    all_to_all x4, waiting for transfers between devices, exchange_z(): return lax.all_to_all(value, Z, 0, 0, tiled=True)  41.3 us
    ppermute x6, waiting for transfers between devices, to_x(): return lax.ppermute(value, 'x', shift(NX, k)) if k else value  28.7 us
    all_to_all x4, starting transfers between devices, exchange_z(): return lax.all_to_all(value, Z, 0, 0, tiled=True)  28.3 us
    pallas_call x1, Pallas kernels, compute(): pl.pallas_call(compute_kernel, out_shape=[gy, gy, gz, gz] + [gn] * NX, in...  27.6 us
    ppermute x8, starting transfers between devices, to_tile(): return lax.ppermute(value, FINE, pairs)  24 us
    ppermute x12, starting transfers between devices, to_y(): return lax.ppermute(value, 'y', shift(NY, k)) if k else value  17.4 us
    unnamed x81, local copies, waits for them, and re-layouts  16.2 us
    ppermute x8, waiting for transfers between devices, to_tile(): return lax.ppermute(value, FINE, pairs)  16.1 us
  transfers between devices with their start and end apart: 37, of which 15 were waited for; matrix products, arithmetic and copies ran while one was open for 2% of the time, Pallas kernels for 4%

profile of v1, /device:TPU:32, one launch (start us, length us, event | category | flops | bytes accessed | tf_op | source)
XLA Modules:
  0.0 239.3 jit_solution(10360394639869619522)
XLA Ops:
  3.5 8.6 %all-to-all-start = ((bf16[8,144,384]{2,1,0:T(8,128)(2,1)}), bf16[8,144,384]{2,1,0:T(8,128)(2,1)S(1)}, u32[]{:S(2)}, u32[]{:S(2)}) async-start(bf16[8,144,384]{2,1,0:T(8,128)(2,1)} %broadcast_in_dim.10), calls=%async_computation | async-start | bytes 1769472 | tf_op jit(solution)/shard_map/all_to_all | solution.py:43
  13.2 2.8 %collective-permute-start.3 = (bf16[256,1536]{1,0:T(8,128)(2,1)S(1)}, bf16[256,1536]{1,0:T(8,128)(2,1)S(1)}, u32[]{:S(2)}, u32[]{:S(2)}) collective-permute-start(bf16[256,1536]{1,0:T(8,128)(2,1)S(1)} %get-tuple-element.57.refs_1_), channel_id=1, source_target_pairs={{0,12},{4,0},{8,4},{12,8},{1,13},{5,1},{9,5},{13,9},{2,14},{6,2},{... | collective-permute-start | bytes 2359304 | tf_op jit(solution)/shard_map/ppermute | solution.py:35
  16.0 3.1 %collective-permute-start = (bf16[2,32,384]{2,1,0:T(8,128)(2,1)S(1)}, bf16[2,32,384]{2,1,0:T(8,128)(2,1)S(1)}, u32[]{:S(2)}, u32[]{:S(2)}) collective-permute-start(bf16[2,32,384]{2,1,0:T(8,128)(2,1)S(1)} %pad_maximum_fusion.1), channel_id=1, source_target_pairs={{0,96},{32,0},{64,32},{96,64},{1,97},{33,1},{65,33},{97,65},{2,98}... | collective-permute-start | bytes 147464 | tf_op jit(solution)/shard_map/ppermute | solution.py:39
  20.8 3.9 %collective-permute-done.1 = bf16[2,32,384]{2,1,0:T(8,128)(2,1)S(1)} collective-permute-done((bf16[2,32,384]{2,1,0:T(8,128)(2,1)S(1)}, bf16[2,32,384]{2,1,0:T(8,128)(2,1)S(1)}, u32[]{:S(2)}, u32[]{:S(2)}) %collective-permute-start.1) | collective-permute-done | bytes 49184 | tf_op jit(solution)/shard_map/ppermute | solution.py:39
  25.2 7.0 %collective-permute-done.3.refs_2_ = bf16[256,1536]{1,0:T(8,128)(2,1)S(1)} collective-permute-done((bf16[256,1536]{1,0:T(8,128)(2,1)S(1)}, bf16[256,1536]{1,0:T(8,128)(2,1)S(1)}, u32[]{:S(2)}, u32[]{:S(2)}) %collective-permute-start.3) | collective-permute-done | bytes 786464 | tf_op jit(solution)/shard_map/ppermute | solution.py:35
  33.1 2.6 %collective-permute-done.4.refs_4_ = bf16[256,1536]{1,0:T(8,128)(2,1)} collective-permute-done((bf16[256,1536]{1,0:T(8,128)(2,1)S(1)}, bf16[256,1536]{1,0:T(8,128)(2,1)}, u32[]{:S(2)}, u32[]{:S(2)}) %collective-permute-start.4) | collective-permute-done | bytes 786464 | tf_op jit(solution)/shard_map/ppermute | solution.py:35
  37.1 7.2 %all-to-all-start.1 = ((bf16[8,4,2,32,384]{4,3,2,1,0:T(8,128)(2,1)}), bf16[8,4,2,32,384]{4,3,2,1,0:T(8,128)(2,1)}, u32[]{:S(2)}, u32[]{:S(2)}) async-start(bf16[8,4,2,32,384]{4,3,2,1,0:T(8,128)(2,1)} %broadcast_in_dim.11), calls=%async_computation.1 | async-start | bytes 3145728 | tf_op jit(solution)/shard_map/all_to_all | solution.py:43
  45.4 3.0 %collective-permute-start.7 = (bf16[8,2,64,384]{3,2,1,0:T(8,128)(2,1)}, bf16[8,2,64,384]{3,2,1,0:T(8,128)(2,1)}, u32[]{:S(2)}, u32[]{:S(2)}) collective-permute-start(bf16[8,2,64,384]{3,2,1,0:T(8,128)(2,1)} %bitcast.12.refs_7_), channel_id=1, source_target_pairs={{0,96},{32,0},{64,32},{96,64},{1,97},{33,1},{65,33},{97,65},{2,98}... | collective-permute-start | bytes 2359304 | tf_op jit(solution)/shard_map/ppermute | solution.py:39
  50.0 30.9 %all-to-all-done.1.refs_5_ = bf16[8,4,2,32,384]{4,3,2,1,0:T(8,128)(2,1)} async-done(((bf16[8,4,2,32,384]{4,3,2,1,0:T(8,128)(2,1)}), bf16[8,4,2,32,384]{4,3,2,1,0:T(8,128)(2,1)}, u32[]{:S(2)}, u32[]{:S(2)}) %all-to-all-start.1) | async-done | bytes 1572896 | tf_op jit(solution)/shard_map/all_to_all | solution.py:43
  82.5 3.2 %collective-permute-done.9.refs_10_ = bf16[8,2,64,384]{3,2,1,0:T(8,128)(2,1)} collective-permute-done((bf16[8,2,64,384]{3,2,1,0:T(8,128)(2,1)}, bf16[8,2,64,384]{3,2,1,0:T(8,128)(2,1)}, u32[]{:S(2)}, u32[]{:S(2)}) %collective-permute-start.9) | collective-permute-done | bytes 786464 | tf_op jit(solution)/shard_map/ppermute | solution.py:39
  89.1 27.6 %block.1 = (bf16[4,8,2,64,384]{4,3,2,1,0:T(8,128)(2,1)}, bf16[4,8,2,64,384]{4,3,2,1,0:T(8,128)(2,1)}, bf16[8,4,2,32,384]{4,3,2,1,0:T(8,128)(2,1)}, bf16[8,4,2,32...) custom-call(s32[2]{0:T(128)} %pad_add_fusion.where, ...), custom_call_target="tpu_custom_call" | custom-call | flops 12079595520 | bytes 25000000 | tf_op jit(solution)/shard_map/block/pallas_call | solution.py:286
  117.3 3.2 %collective-permute-start.17 = (bf16[128,1536]{1,0:T(8,128)(2,1)}, bf16[128,1536]{1,0:T(8,128)(2,1)S(1)}, u32[]{:S(2)}, u32[]{:S(2)}) collective-permute-start(bf16[128,1536]{1,0:T(8,128)(2,1)} %get-tuple-element.66), channel_id=1, source_target_pairs={{0,12},{4,0},{8,4},{12,8},{1,13},{5,1},{9,5},{13,9},{2,14},{6,2},{... | collective-permute-start | bytes 1179656 | tf_op jit(solution)/shard_map/ppermute | solution.py:35
  120.5 9.3 %collective-permute-done.16.refs_1_ = bf16[128,1536]{1,0:T(8,128)(2,1)S(1)} collective-permute-done((bf16[128,1536]{1,0:T(8,128)(2,1)}, bf16[128,1536]{1,0:T(8,128)(2,1)S(1)}, u32[]{:S(2)}, u32[]{:S(2)}) %collective-permute-start.16) | collective-permute-done | bytes 393248 | tf_op jit(solution)/shard_map/ppermute | solution.py:35
  137.6 4.9 %all-to-all-start.2 = ((bf16[8,4,2,32,384]{4,3,2,1,0:T(8,128)(2,1)}), bf16[8,4,2,32,384]{4,3,2,1,0:T(8,128)(2,1)S(1)}, u32[]{:S(2)}, u32[]{:S(2)}) async-start(bf16[8,4,2,32,384]{4,3,2,1,0:T(8,128)(2,1)} %get-tuple-element.90), calls=%async_computation.2 | async-start | bytes 3145728 | tf_op jit(solution)/shard_map/all_to_all | solution.py:43
  142.9 3.4 %collective-permute-start.19 = (bf16[8,2,64,384]{3,2,1,0:T(8,128)(2,1)}, bf16[8,2,64,384]{3,2,1,0:T(8,128)(2,1)S(1)}, u32[]{:S(2)}, u32[]{:S(2)}) collective-permute-start(bf16[8,2,64,384]{3,2,1,0:T(8,128)(2,1)} %copy-done.31), channel_id=1, source_target_pairs={{0,64},{32,96},{64,0},{96,32},{1,65},{33,97},{65,1},{97,33},{2,66}... | collective-permute-start | bytes 2359304 | tf_op jit(solution)/shard_map/ppermute | solution.py:39
  148.4 9.8 %collective-permute-done.21.refs_2_ = bf16[128,1536]{1,0:T(8,128)(2,1)S(1)} collective-permute-done((bf16[128,1536]{1,0:T(8,128)(2,1)}, bf16[128,1536]{1,0:T(8,128)(2,1)S(1)}, u32[]{:S(2)}, u32[]{:S(2)}) %collective-permute-start.21) | collective-permute-done | bytes 393248 | tf_op jit(solution)/shard_map/ppermute | solution.py:35
  166.0 11.0 %collective-permute-done.26.ul = bf16[3,3,1536]{2,1,0:T(4,128)(2,1)S(1)} collective-permute-done((bf16[3,3,1536]{2,1,0:T(4,128)(2,1)S(1)}, bf16[3,3,1536]{2,1,0:T(4,128)(2,1)S(1)}, u32[]{:S(2)}, u32[]{:S(2)}) %collective-permute-start.26) | collective-permute-done | bytes 27680 | tf_op jit(solution)/shard_map/ppermute | solution.py:83
  177.0 5.6 %collective-permute-start.28 = (bf16[3,3,1536]{2,1,0:T(4,128)(2,1)S(1)}, bf16[3,3,1536]{2,1,0:T(4,128)(2,1)S(1)}, u32[]{:S(2)}, u32[]{:S(2)}) collective-permute-start(bf16[3,3,1536]{2,1,0:T(4,128)(2,1)S(1)} %get-tuple-element.87), channel_id=1, source_target_pairs={{16,1},{17,2},{18,3},{19,4},{20,5},{21,6},{22,7},{23,8},{24,9},{25... | collective-permute-start | bytes 82952 | tf_op jit(solution)/shard_map/ppermute | solution.py:83
  184.6 5.8 %collective-permute-start.23 = (bf16[3,16,1536]{2,1,0:T(8,128)(2,1)S(1)}, bf16[3,16,1536]{2,1,0:T(8,128)(2,1)S(1)}, u32[]{:S(2)}, u32[]{:S(2)}) collective-permute-start(bf16[3,16,1536]{2,1,0:T(8,128)(2,1)S(1)} %get-tuple-element.82), channel_id=1, source_target_pairs={{16,0},{17,1},{18,2},{19,3},{20,4},{21,5},{22,6},{23,7},{24,8},{25... | collective-permute-start | bytes 442376 | tf_op jit(solution)/shard_map/ppermute | solution.py:83
  190.4 5.5 %collective-permute-start.24 = (bf16[8,3,1536]{2,1,0:T(4,128)(2,1)S(1)}, bf16[8,3,1536]{2,1,0:T(4,128)(2,1)S(1)}, u32[]{:S(2)}, u32[]{:S(2)}) collective-permute-start(bf16[8,3,1536]{2,1,0:T(4,128)(2,1)S(1)} %get-tuple-element.83), channel_id=1, source_target_pairs={{0,1},{1,2},{2,3},{3,4},{4,5},{5,6},{6,7},{7,8},{8,9},{9,10},{10,1... | collective-permute-start | bytes 221192 | tf_op jit(solution)/shard_map/ppermute | solution.py:83
  199.8 5.1 %collective-permute-done.29.dr = bf16[3,3,1536]{2,1,0:T(4,128)(2,1)S(1)} collective-permute-done((bf16[3,3,1536]{2,1,0:T(4,128)(2,1)S(1)}, bf16[3,3,1536]{2,1,0:T(4,128)(2,1)S(1)}, u32[]{:S(2)}, u32[]{:S(2)}) %collective-permute-start.29) | collective-permute-done | bytes 27680 | tf_op jit(solution)/shard_map/ppermute | solution.py:83
  208.2 7.6 %all-to-all-start.3 = ((bf16[8,2,64,384]{3,2,1,0:T(8,128)(2,1)}), bf16[8,2,64,384]{3,2,1,0:T(8,128)(2,1)}, u32[]{:S(2)}, u32[]{:S(2)}) async-start(bf16[8,2,64,384]{3,2,1,0:T(8,128)(2,1)} %sum_y.1), calls=%async_computation.3 | async-start | bytes 1572864 | tf_op jit(solution)/shard_map/all_to_all | solution.py:43
  221.0 5.7 %convolution.1 = bf16[8,16,1536]{2,1,0:T(8,128)(2,1)} custom-call(bf16[8,16,1536]{2,1,0:T(8,128)(2,1)S(1)} %copy-done.5, bf16[3,16,1536]{2,1,0:T(8,128)(2,1)S(1)} %copy-done.12, bf16[3,16,1536]{2,1,0:T(8,128)(2,1)S(1)} %copy-done.14, bf16[8,3,1536]{2,1,0:T(4,128)(2,1)S(1)} %copy-done.16, bf16[8,3,1536]{2,1,0:T(4,128)(2,1)S(1)} %copy-done.18, ...), custom_call_target="tpu_custom_call" | custom-call | tf_op jit(solution)/shard_map/convolution/pallas_call | solution.py:185
  226.7 10.4 %all-to-all-done.3 = bf16[8,2,64,384]{3,2,1,0:T(8,128)(2,1)} async-done(((bf16[8,2,64,384]{3,2,1,0:T(8,128)(2,1)}), bf16[8,2,64,384]{3,2,1,0:T(8,128)(2,1)}, u32[]{:S(2)}, u32[]{:S(2)}) %all-to-all-start.3) | async-done | bytes 786464 | tf_op jit(solution)/shard_map/all_to_all | solution.py:43
  (161 shorter events, 51.1 us)
Async XLA Ops:
  3.5 32.2 %all-to-all-start = ((bf16[8,144,384]{2,1,0:T(8,128)(2,1)}), bf16[8,144,384]{2,1,0:T(8,128)(2,1)S(1)}, u32[]{:S(2)}, u32[]{:S(2)}) async-start(bf16[8,144,384]{2,1,0:T(8,128)(2,1)} %broadcast_in_dim.10), calls=%async_computation | async-start | bytes 1769472 | tf_op jit(solution)/shard_map/all_to_all | solution.py:43
  13.2 19.0 %collective-permute-start.3 = (bf16[256,1536]{1,0:T(8,128)(2,1)S(1)}, bf16[256,1536]{1,0:T(8,128)(2,1)S(1)}, u32[]{:S(2)}, u32[]{:S(2)}) collective-permute-start(bf16[256,1536]{1,0:T(8,128)(2,1)S(1)} %get-tuple-element.57.refs_1_), channel_id=1, source_target_pairs={{0,12},{4,0},{8,4},{12,8},{1,13},{5,1},{9,5},{13,9},{2,14},{6,2},{... | collective-permute-start | bytes 2359304 | tf_op jit(solution)/shard_map/ppermute | solution.py:35
  16.0 19.8 %collective-permute-start.4 = (bf16[256,1536]{1,0:T(8,128)(2,1)S(1)}, bf16[256,1536]{1,0:T(8,128)(2,1)}, u32[]{:S(2)}, u32[]{:S(2)}) collective-permute-start(bf16[256,1536]{1,0:T(8,128)(2,1)S(1)} %get-tuple-element.57.refs_1_), channel_id=1, source_target_pairs={{0,4},{4,8},{8,12},{12,0},{1,5},{5,9},{9,13},{13,1},{2,6},{6,10},{... | collective-permute-start | bytes 2359304 | tf_op jit(solution)/shard_map/ppermute | solution.py:35
  37.1 43.8 %all-to-all-start.1 = ((bf16[8,4,2,32,384]{4,3,2,1,0:T(8,128)(2,1)}), bf16[8,4,2,32,384]{4,3,2,1,0:T(8,128)(2,1)}, u32[]{:S(2)}, u32[]{:S(2)}) async-start(bf16[8,4,2,32,384]{4,3,2,1,0:T(8,128)(2,1)} %broadcast_in_dim.11), calls=%async_computation.1 | async-start | bytes 3145728 | tf_op jit(solution)/shard_map/all_to_all | solution.py:43
  44.3 36.6 %collective-permute-start.5 = (bf16[256,1536]{1,0:T(8,128)(2,1)S(1)}, bf16[256,1536]{1,0:T(8,128)(2,1)}, u32[]{:S(2)}, u32[]{:S(2)}) collective-permute-start(bf16[256,1536]{1,0:T(8,128)(2,1)S(1)} %get-tuple-element.57.refs_1_), channel_id=1, source_target_pairs={{0,8},{4,12},{8,0},{12,4},{1,9},{5,13},{9,1},{13,5},{2,10},{6,14},... | collective-permute-start | bytes 2359304 | tf_op jit(solution)/shard_map/ppermute | solution.py:35
  45.4 36.6 %collective-permute-start.7 = (bf16[8,2,64,384]{3,2,1,0:T(8,128)(2,1)}, bf16[8,2,64,384]{3,2,1,0:T(8,128)(2,1)}, u32[]{:S(2)}, u32[]{:S(2)}) collective-permute-start(bf16[8,2,64,384]{3,2,1,0:T(8,128)(2,1)} %bitcast.12.refs_7_), channel_id=1, source_target_pairs={{0,96},{32,0},{64,32},{96,64},{1,97},{33,1},{65,33},{97,65},{2,98}... | collective-permute-start | bytes 2359304 | tf_op jit(solution)/shard_map/ppermute | solution.py:39
  48.4 33.5 %collective-permute-start.8 = (bf16[8,2,64,384]{3,2,1,0:T(8,128)(2,1)}, bf16[8,2,64,384]{3,2,1,0:T(8,128)(2,1)}, u32[]{:S(2)}, u32[]{:S(2)}) collective-permute-start(bf16[8,2,64,384]{3,2,1,0:T(8,128)(2,1)} %bitcast.12.refs_7_), channel_id=1, source_target_pairs={{0,64},{32,96},{64,0},{96,32},{1,65},{33,97},{65,1},{97,33},{2,66}... | collective-permute-start | bytes 2359304 | tf_op jit(solution)/shard_map/ppermute | solution.py:39
  49.0 36.6 %collective-permute-start.9 = (bf16[8,2,64,384]{3,2,1,0:T(8,128)(2,1)}, bf16[8,2,64,384]{3,2,1,0:T(8,128)(2,1)}, u32[]{:S(2)}, u32[]{:S(2)}) collective-permute-start(bf16[8,2,64,384]{3,2,1,0:T(8,128)(2,1)} %bitcast.12.refs_7_), channel_id=1, source_target_pairs={{0,32},{32,64},{64,96},{96,0},{1,33},{33,65},{65,97},{97,1},{2,34}... | collective-permute-start | bytes 2359304 | tf_op jit(solution)/shard_map/ppermute | solution.py:39
  116.7 13.1 %collective-permute-start.14 = (bf16[4,8,2,64,384]{4,3,2,1,0:T(8,128)(2,1)}, bf16[4,8,2,64,384]{4,3,2,1,0:T(8,128)(2,1)S(1)}, u32[]{:S(2)}, u32[]{:S(2)}) collective-permute-start(bf16[4,8,2,64,384]{4,3,2,1,0:T(8,128)(2,1)} %get-tuple-element.63), channel_id=1, source_target_pairs={{0,16},{16,0},{1,17},{17,1},{2,18},{18,2},{3,19},{19,3},{4,20},{20... | collective-permute-start | bytes 9437192 | tf_op jit(solution)/shard_map/ppermute | solution.py:60
  116.9 13.0 %collective-permute-start.15 = (bf16[8,4,2,32,384]{4,3,2,1,0:T(8,128)(2,1)}, bf16[8,4,2,32,384]{4,3,2,1,0:T(8,128)(2,1)S(1)}, u32[]{:S(2)}, u32[]{:S(2)}) collective-permute-start(bf16[8,4,2,32,384]{4,3,2,1,0:T(8,128)(2,1)} %get-tuple-element.64), channel_id=1, source_target_pairs={{0,16},{16,0},{1,17},{17,1},{2,18},{18,2},{3,19},{19,3},{4,20},{20... | collective-permute-start | bytes 4718600 | tf_op jit(solution)/shard_map/ppermute | solution.py:60
  117.3 12.6 %collective-permute-start.17 = (bf16[128,1536]{1,0:T(8,128)(2,1)}, bf16[128,1536]{1,0:T(8,128)(2,1)S(1)}, u32[]{:S(2)}, u32[]{:S(2)}) collective-permute-start(bf16[128,1536]{1,0:T(8,128)(2,1)} %get-tuple-element.66), channel_id=1, source_target_pairs={{0,12},{4,0},{8,4},{12,8},{1,13},{5,1},{9,5},{13,9},{2,14},{6,2},{... | collective-permute-start | bytes 1179656 | tf_op jit(solution)/shard_map/ppermute | solution.py:35
  137.6 70.6 %all-to-all-start.2 = ((bf16[8,4,2,32,384]{4,3,2,1,0:T(8,128)(2,1)}), bf16[8,4,2,32,384]{4,3,2,1,0:T(8,128)(2,1)S(1)}, u32[]{:S(2)}, u32[]{:S(2)}) async-start(bf16[8,4,2,32,384]{4,3,2,1,0:T(8,128)(2,1)} %get-tuple-element.90), calls=%async_computation.2 | async-start | bytes 3145728 | tf_op jit(solution)/shard_map/all_to_all | solution.py:43
  142.5 47.8 %collective-permute-start.18 = (bf16[8,2,64,384]{3,2,1,0:T(8,128)(2,1)}, bf16[8,2,64,384]{3,2,1,0:T(8,128)(2,1)S(1)}, u32[]{:S(2)}, u32[]{:S(2)}) collective-permute-start(bf16[8,2,64,384]{3,2,1,0:T(8,128)(2,1)} %copy-done.32), channel_id=1, source_target_pairs={{0,32},{32,64},{64,96},{96,0},{1,33},{33,65},{65,97},{97,1},{2,34}... | collective-permute-start | bytes 2359304 | tf_op jit(solution)/shard_map/ppermute | solution.py:39
  142.9 53.0 %collective-permute-start.19 = (bf16[8,2,64,384]{3,2,1,0:T(8,128)(2,1)}, bf16[8,2,64,384]{3,2,1,0:T(8,128)(2,1)S(1)}, u32[]{:S(2)}, u32[]{:S(2)}) collective-permute-start(bf16[8,2,64,384]{3,2,1,0:T(8,128)(2,1)} %copy-done.31), channel_id=1, source_target_pairs={{0,64},{32,96},{64,0},{96,32},{1,65},{33,97},{65,1},{97,33},{2,66}... | collective-permute-start | bytes 2359304 | tf_op jit(solution)/shard_map/ppermute | solution.py:39
  146.2 51.0 %collective-permute-start.20 = (bf16[8,2,64,384]{3,2,1,0:T(8,128)(2,1)}, bf16[8,2,64,384]{3,2,1,0:T(8,128)(2,1)S(1)}, u32[]{:S(2)}, u32[]{:S(2)}) collective-permute-start(bf16[8,2,64,384]{3,2,1,0:T(8,128)(2,1)} %copy-done.30), channel_id=1, source_target_pairs={{0,96},{32,0},{64,32},{96,64},{1,97},{33,1},{65,33},{97,65},{2,98}... | collective-permute-start | bytes 2359304 | tf_op jit(solution)/shard_map/ppermute | solution.py:39
  163.4 13.6 %collective-permute-start.26 = (bf16[3,3,1536]{2,1,0:T(4,128)(2,1)S(1)}, bf16[3,3,1536]{2,1,0:T(4,128)(2,1)S(1)}, u32[]{:S(2)}, u32[]{:S(2)}) collective-permute-start(bf16[3,3,1536]{2,1,0:T(4,128)(2,1)S(1)} %get-tuple-element.85), channel_id=1, source_target_pairs={{0,17},{1,18},{2,19},{3,20},{4,21},{5,22},{6,23},{7,24},{8,25},{9,... | collective-permute-start | bytes 82952 | tf_op jit(solution)/shard_map/ppermute | solution.py:83
  164.7 18.0 %collective-permute-start.27 = (bf16[3,3,1536]{2,1,0:T(4,128)(2,1)S(1)}, bf16[3,3,1536]{2,1,0:T(4,128)(2,1)S(1)}, u32[]{:S(2)}, u32[]{:S(2)}) collective-permute-start(bf16[3,3,1536]{2,1,0:T(4,128)(2,1)S(1)} %get-tuple-element.86), channel_id=1, source_target_pairs={{1,16},{2,17},{3,18},{4,19},{5,20},{6,21},{7,22},{8,23},{9,24},{10... | collective-permute-start | bytes 82952 | tf_op jit(solution)/shard_map/ppermute | solution.py:83
  182.6 24.2 %collective-permute-start.22 = (bf16[3,16,1536]{2,1,0:T(8,128)(2,1)S(1)}, bf16[3,16,1536]{2,1,0:T(8,128)(2,1)S(1)}, u32[]{:S(2)}, u32[]{:S(2)}) collective-permute-start(bf16[3,16,1536]{2,1,0:T(8,128)(2,1)S(1)} %get-tuple-element.81), channel_id=1, source_target_pairs={{0,16},{1,17},{2,18},{3,19},{4,20},{5,21},{6,22},{7,23},{8,24},{9,... | collective-permute-start | bytes 442376 | tf_op jit(solution)/shard_map/ppermute | solution.py:83
  184.6 22.9 %collective-permute-start.23 = (bf16[3,16,1536]{2,1,0:T(8,128)(2,1)S(1)}, bf16[3,16,1536]{2,1,0:T(8,128)(2,1)S(1)}, u32[]{:S(2)}, u32[]{:S(2)}) collective-permute-start(bf16[3,16,1536]{2,1,0:T(8,128)(2,1)S(1)} %get-tuple-element.82), channel_id=1, source_target_pairs={{16,0},{17,1},{18,2},{19,3},{20,4},{21,5},{22,6},{23,7},{24,8},{25... | collective-permute-start | bytes 442376 | tf_op jit(solution)/shard_map/ppermute | solution.py:83
  190.4 15.1 %collective-permute-start.24 = (bf16[8,3,1536]{2,1,0:T(4,128)(2,1)S(1)}, bf16[8,3,1536]{2,1,0:T(4,128)(2,1)S(1)}, u32[]{:S(2)}, u32[]{:S(2)}) collective-permute-start(bf16[8,3,1536]{2,1,0:T(4,128)(2,1)S(1)} %get-tuple-element.83), channel_id=1, source_target_pairs={{0,1},{1,2},{2,3},{3,4},{4,5},{5,6},{6,7},{7,8},{8,9},{9,10},{10,1... | collective-permute-start | bytes 221192 | tf_op jit(solution)/shard_map/ppermute | solution.py:83
  208.2 28.9 %all-to-all-start.3 = ((bf16[8,2,64,384]{3,2,1,0:T(8,128)(2,1)}), bf16[8,2,64,384]{3,2,1,0:T(8,128)(2,1)}, u32[]{:S(2)}, u32[]{:S(2)}) async-start(bf16[8,2,64,384]{3,2,1,0:T(8,128)(2,1)} %sum_y.1), calls=%async_computation.3 | async-start | bytes 1572864 | tf_op jit(solution)/shard_map/all_to_all | solution.py:43
  217.5 21.0 %collective-permute-start.30 = (bf16[2,32,384]{2,1,0:T(8,128)(2,1)}, bf16[2,32,384]{2,1,0:T(8,128)(2,1)S(1)}, u32[]{:S(2)}, u32[]{:S(2)}) collective-permute-start(bf16[2,32,384]{2,1,0:T(8,128)(2,1)} %get-tuple-element.107), channel_id=1, source_target_pairs={{0,32},{32,64},{64,96},{96,0},{1,33},{33,65},{65,97},{97,1},{2,34}... | collective-permute-start | bytes 147464 | tf_op jit(solution)/shard_map/ppermute | solution.py:39
  217.5 21.0 %collective-permute-start.31 = (bf16[2,32,384]{2,1,0:T(8,128)(2,1)S(1)}, bf16[2,32,384]{2,1,0:T(8,128)(2,1)S(1)}, u32[]{:S(2)}, u32[]{:S(2)}) collective-permute-start(bf16[2,32,384]{2,1,0:T(8,128)(2,1)S(1)} %get-tuple-element.108), channel_id=1, source_target_pairs={{0,64},{32,96},{64,0},{96,32},{1,65},{33,97},{65,1},{97,33},{2,66}... | collective-permute-start | bytes 147464 | tf_op jit(solution)/shard_map/ppermute | solution.py:39
  219.7 18.8 %collective-permute-start.32 = (bf16[2,32,384]{2,1,0:T(8,128)(2,1)S(1)}, bf16[2,32,384]{2,1,0:T(8,128)(2,1)S(1)}, u32[]{:S(2)}, u32[]{:S(2)}) collective-permute-start(bf16[2,32,384]{2,1,0:T(8,128)(2,1)S(1)} %get-tuple-element.109), channel_id=1, source_target_pairs={{0,96},{32,0},{64,32},{96,64},{1,97},{33,1},{65,33},{97,65},{2,98}... | collective-permute-start | bytes 147464 | tf_op jit(solution)/shard_map/ppermute | solution.py:39
  (53 other events, 402.0 us)

commit v2 on v1

--- a/solution.py
+++ b/solution.py
@@ -60,16 +60,6 @@
     return lax.ppermute(value, "c", shift(2, 1))
 
 
-HALO = (
-    (1, 0, slice(5, 8), slice(0, 16)),
-    (-1, 0, slice(0, 3), slice(0, 16)),
-    (0, 1, slice(0, 8), slice(13, 16)),
-    (0, -1, slice(0, 8), slice(0, 3)),
-    (1, 1, slice(5, 8), slice(13, 16)),
-    (1, -1, slice(5, 8), slice(0, 3)),
-    (-1, 1, slice(0, 3), slice(13, 16)),
-    (-1, -1, slice(0, 3), slice(0, 3)),
-)
 TILE_ROWS, TILE_COLS, TAPS, MARGIN = 8, 16, 7, 3
 
 
@@ -116,7 +106,7 @@
 
 
 def norm_backward_kernel(*refs):
-    parts, (xhat, inverse, gain, out), halos = refs[:NX], refs[NX : NX + 4], refs[NX + 4 :]
+    parts, (xhat, inverse, gain, out, first_cols, last_cols) = refs[:NX], refs[NX:]
     for i in range(TILE_ROWS):
         rows = slice(i * TILE_COLS, (i + 1) * TILE_COLS)
         value = parts[0][rows].astype(f32)
@@ -128,41 +118,51 @@
         second = jnp.mean(value * hat, axis=-1, keepdims=True)
         value = inverse[rows] * (value - first - hat * second)
         out[i] = value.astype(bf16)
-        for (_, _, height, breadth), halo in zip(HALO, halos, strict=True):
-            if height.start <= i < height.stop:
-                halo[i - height.start] = value[breadth].astype(bf16)
+        first_cols[i] = value[:MARGIN].astype(bf16)
+        last_cols[i] = value[TILE_COLS - MARGIN :].astype(bf16)
 
 
 def layer_norm_backward(parts, xhat, inverse, gain):
     return pl.pallas_call(
         norm_backward_kernel,
         out_shape=[jax.ShapeDtypeStruct((TILE_ROWS, TILE_COLS, CHAN), bf16)]
-        + [
-            jax.ShapeDtypeStruct((h.stop - h.start, b.stop - b.start, CHAN), bf16)
-            for _, _, h, b in HALO
-        ],
+        + [jax.ShapeDtypeStruct((TILE_ROWS, MARGIN, CHAN), bf16)] * 2,
         in_specs=vmem_specs(NX + 3),
-        out_specs=vmem_specs(9),
+        out_specs=vmem_specs(3),
         compiler_params=pltpu.CompilerParams(vmem_limit_bytes=16 * 2**20),
         name="layer_norm_backward",
     )(*parts, xhat, inverse, gain)
 
 
-def conv_kernel(own, up, down, left, right, ul, ur, dl, dr, kernel, grad, out, pad):
-    low, mid, high = slice(0, 3), slice(3, 11), slice(11, 14)
-    west, here, east = slice(0, 3), slice(3, 19), slice(19, 22)
-    for rows, cols, ref in (
-        (mid, here, own),
-        (low, here, up),
-        (high, here, down),
-        (mid, west, left),
-        (mid, east, right),
-        (low, west, ul),
-        (low, east, ur),
-        (high, west, dl),
-        (high, east, dr),
-    ):
-        pad[rows, cols, :] = ref[...].astype(f32)
+def widen(out, rows, own, left, right):
+    out[:, :MARGIN] = left[rows].astype(out.dtype)
+    out[:, MARGIN : MARGIN + TILE_COLS] = own[rows].astype(out.dtype)
+    out[:, MARGIN + TILE_COLS : TILE_COLS + 2 * MARGIN] = right[rows].astype(out.dtype)
+
+
+def edge_kernel(own, left, right, first_rows, last_rows, scratch):
+    for out, rows in ((first_rows, slice(0, 3)), (last_rows, slice(5, 8))):
+        scratch[:, 16:, :] = jnp.zeros((MARGIN, 8, CHAN), f32)
+        widen(scratch, rows, own, left, right)
+        out[...] = scratch[...].astype(bf16)
+
+
+def edges(own, left, right):
+    return pl.pallas_call(
+        edge_kernel,
+        out_shape=[jax.ShapeDtypeStruct((MARGIN, 24, CHAN), bf16)] * 2,
+        in_specs=vmem_specs(3),
+        out_specs=vmem_specs(2),
+        scratch_shapes=[pltpu.VMEM((MARGIN, 24, CHAN), f32)],
+        compiler_params=pltpu.CompilerParams(vmem_limit_bytes=8 * 2**20),
+        name="edges",
+    )(own, left, right)
+
+
+def conv_kernel(own, left, right, up, down, kernel, grad, out, pad):
+    pad[:MARGIN] = up[...].astype(f32)
+    widen(pad.at[MARGIN : MARGIN + TILE_ROWS], slice(0, TILE_ROWS), own, left, right)
+    pad[MARGIN + TILE_ROWS :] = down[...].astype(f32)
     total = None
     for col_tap in range(TAPS):
         column = pad[:, TAPS - 1 - col_tap : TAPS - 1 - col_tap + TILE_COLS, :]
@@ -174,14 +174,14 @@
     out[...] = (grad[...].astype(f32) + total).astype(bf16)
 
 
-def convolution(own, halos, kernel, grad):
+def convolution(own, left, right, up, down, kernel, grad):
     width = 128
 
     def spec(shape):
         lead = (0,) * (len(shape) - 1)
         return pl.BlockSpec((*shape[:-1], width), lambda i: (*lead, i))
 
-    operands = [own, *halos, kernel, grad]
+    operands = [own, left, right, up, down, kernel, grad]
     return pl.pallas_call(
         conv_kernel,
         grid=(CHAN // width,),
@@ -369,11 +369,35 @@
     )(parts)
 
 
-def total(parts):
-    result = parts[0].astype(f32)
-    for part in parts[1:]:
-        result = result + part.astype(f32)
-    return result
+def finish_kernel(*refs):
+    zs, (ys, grad_in, grad_out) = refs[:NY], refs[NY:]
+    factor = 1.0 / math.sqrt(BLOCK * 256)
+    for m in range(2):
+        lead = zs[0][m].astype(f32)
+        for part in zs[1:]:
+            lead = lead + part[m].astype(f32)
+        rest = ys[0, m].astype(f32)
+        for k in range(1, NZ):
+            rest = rest + ys[k, m].astype(f32)
+        value = jnp.concatenate([lead, rest]) * factor
+        if m == 0:
+            grad_in[...] = value
+        else:
+            grad_out[...] = value.T
+
+
+def finish(zs, ys):
+    return pl.pallas_call(
+        finish_kernel,
+        out_shape=[
+            jax.ShapeDtypeStruct((ROWS, COLS), f32),
+            jax.ShapeDtypeStruct((COLS, ROWS), f32),
+        ],
+        in_specs=vmem_specs(NY + 1),
+        out_specs=vmem_specs(2),
+        compiler_params=pltpu.CompilerParams(vmem_limit_bytes=8 * 2**20),
+        name="finish",
+    )(*zs, ys)
 
 
 def body(
@@ -396,7 +420,12 @@
     bias = jnp.sum(got[:4, 2 * BY : 2 * BY + 3].astype(f32), axis=1).reshape(1, HIDDEN)
     second = [to_y(rest_z, -r) for r in range(NY)]
     first = gather_z(lead_y)
-    second = [second, [swap(v) for v in second]]
+    swapped = [swap(v) for v in second[:2]] + [None, swap(second[3])]
+    first, swapped[1], swapped[3], second[2], tok[2] = lax.optimization_barrier(
+        (first, swapped[1], swapped[3], second[2], tok[2])
+    )
+    swapped[2] = swap(second[2])
+    second = [second, swapped]
     first = [first, swap(first)]
 
     where = jnp.stack([lax.axis_index("y"), lax.axis_index("c")]).astype(jnp.int32)
@@ -408,19 +437,21 @@
     )
     ys, zs = add_cores(grad_y[0], other_y, grad_z[0], other_z)
     ys = [to_y(v, r) for r, v in enumerate(ys)]
-    own, *halos = layer_norm_backward(part, xhat, inverse, gain)
-    halos = [to_tile(v, *where[:2]) for v, where in zip(halos, HALO, strict=True)]
+    own, first_cols, last_cols = layer_norm_backward(part, xhat, inverse, gain)
+    left, right = to_tile(last_cols, 0, 1), to_tile(first_cols, 0, -1)
     ys = sum_y(ys)
-    ys, own, *halos = lax.optimization_barrier((ys, own, *halos))
+    ys, own, left, right = lax.optimization_barrier((ys, own, left, right))
     zs = sum_z(exchange_z(zs))
-    own, *zs = lax.optimization_barrier((own, *zs))
+    left, right, *zs = lax.optimization_barrier((left, right, *zs))
+    first_rows, last_rows = edges(own, left, right)
+    up, down = to_tile(last_rows, 1, 0), to_tile(first_rows, -1, 0)
     zs = [to_y(v, r) for r, v in enumerate(zs)]
     ys = exchange_z(ys)
-    grad_input = convolution(own, halos, dw_kernel.reshape(TAPS * TAPS, CHAN), out_grad)
+    kernel = dw_kernel.reshape(TAPS * TAPS, CHAN)
+    grad_input = convolution(own, left, right, up, down, kernel, out_grad)
     grad_input, ys = lax.optimization_barrier((grad_input, ys))
-    factor = 1.0 / math.sqrt(BLOCK * lax.axis_size(FINE))
-    summed = jnp.concatenate([total(zs), total(ys)], axis=1) * factor
-    return (grad_input, summed[0], summed[1].T)
+    grad_in, grad_out = finish(zs, ys)
+    return (grad_input, grad_in, grad_out)
 
 
 def solution(mesh):

time: 240 us -> 225 us (0.938)
  starting transfers between devices: 78.6 us -> 66.7 us
    ppermute x12, waiting for transfers between devices: 8.27 us -> 51.1 us  [to_y(): return lax.ppermute(value, 'y', shift(NY, k)) if k else value]
    all_to_all x4, waiting for transfers between devices: 41.3 us -> 2.2 us  [exchange_z(): return lax.all_to_all(value, Z, 0, 0, tiled=True)]
    ppermute x8 -> x4, starting transfers between devices: 24 us -> 13.5 us  [to_tile(): return lax.ppermute(value, FINE, pairs)]
    ppermute x8 -> x4, waiting for transfers between devices: 16.1 us -> 9.13 us  [to_tile(): return lax.ppermute(value, FINE, pairs)]
    unnamed x81 -> x62, local copies, waits for them, and re-layouts: 16.2 us -> 15.8 us
  transfers between devices with their start and end apart: 37 -> 33, of which waited for: 15 -> 16; matrix products, arithmetic and copies ran while one was open for 2% -> 1% of each run, Pallas kernels for 4% -> 4%
where the time goes in v2:
time: 225 us; the launch traced here: 224 us
  waiting for transfers between devices  95.4 us (42%)
  starting transfers between devices  66.7 us (30%)
  Pallas kernels  38.1 us (17%)
  local copies, waits for them, and re-layouts  20.5 us (9%)
  other arithmetic  2.26 us (1%)
    ppermute x12, waiting for transfers between devices, to_y(): return lax.ppermute(value, 'y', shift(NY, k)) if k else value  51.1 us
    ppermute x6, waiting for transfers between devices, to_x(): return lax.ppermute(value, 'x', shift(NX, k)) if k else value  28.8 us
    all_to_all x4, starting transfers between devices, exchange_z(): return lax.all_to_all(value, Z, 0, 0, tiled=True)  28.2 us
    pallas_call x1, Pallas kernels, compute(): pl.pallas_call(compute_kernel, out_shape=[gy, gy, gz, gz] + [gn] * NX, in...  27.6 us
    ppermute x12, starting transfers between devices, to_y(): return lax.ppermute(value, 'y', shift(NY, k)) if k else value  16.5 us
    unnamed x62, local copies, waits for them, and re-layouts  15.8 us
    ppermute x4, starting transfers between devices, to_tile(): return lax.ppermute(value, FINE, pairs)  13.5 us
    ppermute x4, waiting for transfers between devices, to_tile(): return lax.ppermute(value, FINE, pairs)  9.13 us
  transfers between devices with their start and end apart: 33, of which 16 were waited for; matrix products, arithmetic and copies ran while one was open for 1% of the time, Pallas kernels for 4%

profile of v2, /device:TPU:32, one launch (start us, length us, event | category | flops | bytes accessed | tf_op | source)
XLA Modules:
  0.0 224.0 jit_solution(17869864339586382820)
XLA Ops:
  3.6 8.6 %all-to-all-start = ((bf16[8,144,384]{2,1,0:T(8,128)(2,1)}), bf16[8,144,384]{2,1,0:T(8,128)(2,1)S(1)}, u32[]{:S(2)}, u32[]{:S(2)}) async-start(bf16[8,144,384]{2,1,0:T(8,128)(2,1)} %broadcast_in_dim.10), calls=%async_computation | async-start | bytes 1769472 | tf_op jit(solution)/shard_map/all_to_all | solution.py:43
  13.3 2.8 %collective-permute-start.3 = (bf16[256,1536]{1,0:T(8,128)(2,1)S(1)}, bf16[256,1536]{1,0:T(8,128)(2,1)S(1)}, u32[]{:S(2)}, u32[]{:S(2)}) collective-permute-start(bf16[256,1536]{1,0:T(8,128)(2,1)S(1)} %get-tuple-element.55.refs_1_), channel_id=1, source_target_pairs={{0,12},{4,0},{8,4},{12,8},{1,13},{5,1},{9,5},{13,9},{2,14},{6,2},{... | collective-permute-start | bytes 2359304 | tf_op jit(solution)/shard_map/ppermute | solution.py:35
  16.1 3.1 %collective-permute-start = (bf16[2,32,384]{2,1,0:T(8,128)(2,1)S(1)}, bf16[2,32,384]{2,1,0:T(8,128)(2,1)S(1)}, u32[]{:S(2)}, u32[]{:S(2)}) collective-permute-start(bf16[2,32,384]{2,1,0:T(8,128)(2,1)S(1)} %pad_maximum_fusion.1), channel_id=1, source_target_pairs={{0,96},{32,0},{64,32},{96,64},{1,97},{33,1},{65,33},{97,65},{2,98}... | collective-permute-start | bytes 147464 | tf_op jit(solution)/shard_map/ppermute | solution.py:39
  20.9 3.9 %collective-permute-done.1 = bf16[2,32,384]{2,1,0:T(8,128)(2,1)S(1)} collective-permute-done((bf16[2,32,384]{2,1,0:T(8,128)(2,1)S(1)}, bf16[2,32,384]{2,1,0:T(8,128)(2,1)S(1)}, u32[]{:S(2)}, u32[]{:S(2)}) %collective-permute-start.1) | collective-permute-done | bytes 49184 | tf_op jit(solution)/shard_map/ppermute | solution.py:39
  25.3 7.0 %collective-permute-done.3.refs_2_ = bf16[256,1536]{1,0:T(8,128)(2,1)S(1)} collective-permute-done((bf16[256,1536]{1,0:T(8,128)(2,1)S(1)}, bf16[256,1536]{1,0:T(8,128)(2,1)S(1)}, u32[]{:S(2)}, u32[]{:S(2)}) %collective-permute-start.3) | collective-permute-done | bytes 786464 | tf_op jit(solution)/shard_map/ppermute | solution.py:35
  33.2 2.6 %collective-permute-done.4.refs_4_ = bf16[256,1536]{1,0:T(8,128)(2,1)} collective-permute-done((bf16[256,1536]{1,0:T(8,128)(2,1)S(1)}, bf16[256,1536]{1,0:T(8,128)(2,1)}, u32[]{:S(2)}, u32[]{:S(2)}) %collective-permute-start.4) | collective-permute-done | bytes 786464 | tf_op jit(solution)/shard_map/ppermute | solution.py:35
  37.2 7.2 %all-to-all-start.1 = ((bf16[8,4,2,32,384]{4,3,2,1,0:T(8,128)(2,1)}), bf16[8,4,2,32,384]{4,3,2,1,0:T(8,128)(2,1)}, u32[]{:S(2)}, u32[]{:S(2)}) async-start(bf16[8,4,2,32,384]{4,3,2,1,0:T(8,128)(2,1)} %broadcast_in_dim.11), calls=%async_computation.1 | async-start | bytes 3145728 | tf_op jit(solution)/shard_map/all_to_all | solution.py:43
  45.4 3.0 %collective-permute-start.5 = (bf16[8,2,64,384]{3,2,1,0:T(8,128)(2,1)}, bf16[8,2,64,384]{3,2,1,0:T(8,128)(2,1)S(1)}, u32[]{:S(2)}, u32[]{:S(2)}) collective-permute-start(bf16[8,2,64,384]{3,2,1,0:T(8,128)(2,1)} %bitcast.12.refs_7_), channel_id=1, source_target_pairs={{0,96},{32,0},{64,32},{96,64},{1,97},{33,1},{65,33},{97,65},{2,98}... | collective-permute-start | bytes 2359304 | tf_op jit(solution)/shard_map/ppermute | solution.py:39
  48.6 2.2 collective-permute-start.9
  50.8 29.3 %collective-permute-done.5.refs_8_ = bf16[8,2,64,384]{3,2,1,0:T(8,128)(2,1)S(1)} collective-permute-done((bf16[8,2,64,384]{3,2,1,0:T(8,128)(2,1)}, bf16[8,2,64,384]{3,2,1,0:T(8,128)(2,1)S(1)}, u32[]{:S(2)}, u32[]{:S(2)}) %collective-permute-start.5) | collective-permute-done | bytes 786464 | tf_op jit(solution)/shard_map/ppermute | solution.py:39
  80.1 3.3 %collective-permute-done.7.refs_10_ = bf16[8,2,64,384]{3,2,1,0:T(8,128)(2,1)S(1)} collective-permute-done((bf16[8,2,64,384]{3,2,1,0:T(8,128)(2,1)}, bf16[8,2,64,384]{3,2,1,0:T(8,128)(2,1)S(1)}, u32[]{:S(2)}, u32[]{:S(2)}) %collective-permute-start.7) | collective-permute-done | bytes 786464 | tf_op jit(solution)/shard_map/ppermute | solution.py:39
  87.7 3.7 %collective-permute-done.12.refs_11_ = bf16[8,2,64,384]{3,2,1,0:T(8,128)(2,1)S(1)} collective-permute-done((bf16[8,2,64,384]{3,2,1,0:T(8,128)(2,1)}, bf16[8,2,64,384]{3,2,1,0:T(8,128)(2,1)S(1)}, u32[]{:S(2)}, u32[]{:S(2)}) %collective-permute-start.12) | collective-permute-done | bytes 786464 | tf_op jit(solution)/shard_map/ppermute | solution.py:60
  92.4 27.6 %block.1 = (bf16[4,8,2,64,384]{4,3,2,1,0:T(8,128)(2,1)}, bf16[4,8,2,64,384]{4,3,2,1,0:T(8,128)(2,1)}, bf16[8,4,2,32,384]{4,3,2,1,0:T(8,128)(2,1)}, bf16[8,4,2,32...) custom-call(s32[2]{0:T(128)} %pad_add_fusion.where, ...), custom_call_target="tpu_custom_call" | custom-call | flops 12079595520 | bytes 25000000 | tf_op jit(solution)/shard_map/block/pallas_call | solution.py:286
  121.2 2.6 %collective-permute-start.17 = (bf16[128,1536]{1,0:T(8,128)(2,1)}, bf16[128,1536]{1,0:T(8,128)(2,1)S(1)}, u32[]{:S(2)}, u32[]{:S(2)}) collective-permute-start(bf16[128,1536]{1,0:T(8,128)(2,1)} %get-tuple-element.69), channel_id=1, source_target_pairs={{0,12},{4,0},{8,4},{12,8},{1,13},{5,1},{9,5},{13,9},{2,14},{6,2},{... | collective-permute-start | bytes 1179656 | tf_op jit(solution)/shard_map/ppermute | solution.py:35
  123.7 9.6 %collective-permute-done.16.refs_1_ = bf16[128,1536]{1,0:T(8,128)(2,1)S(1)} collective-permute-done((bf16[128,1536]{1,0:T(8,128)(2,1)}, bf16[128,1536]{1,0:T(8,128)(2,1)S(1)}, u32[]{:S(2)}, u32[]{:S(2)}) %collective-permute-start.16) | collective-permute-done | bytes 393248 | tf_op jit(solution)/shard_map/ppermute | solution.py:35
  142.0 7.3 %all-to-all-start.2 = ((bf16[8,4,2,32,384]{4,3,2,1,0:T(8,128)(2,1)}), bf16[8,4,2,32,384]{4,3,2,1,0:T(8,128)(2,1)S(1)}, u32[]{:S(2)}, u32[]{:S(2)}) async-start(bf16[8,4,2,32,384]{4,3,2,1,0:T(8,128)(2,1)} %get-tuple-element.89), calls=%async_computation.2 | async-start | bytes 3145728 | tf_op jit(solution)/shard_map/all_to_all | solution.py:43
  149.4 2.9 %collective-permute-start.19 = (bf16[8,2,64,384]{3,2,1,0:T(8,128)(2,1)}, bf16[8,2,64,384]{3,2,1,0:T(8,128)(2,1)S(1)}, u32[]{:S(2)}, u32[]{:S(2)}) collective-permute-start(bf16[8,2,64,384]{3,2,1,0:T(8,128)(2,1)} %copy-done.15), channel_id=1, source_target_pairs={{0,64},{32,96},{64,0},{96,32},{1,65},{33,97},{65,1},{97,33},{2,66}... | collective-permute-start | bytes 2359304 | tf_op jit(solution)/shard_map/ppermute | solution.py:39
  154.0 9.6 %collective-permute-done.21.refs_2_ = bf16[128,1536]{1,0:T(8,128)(2,1)S(1)} collective-permute-done((bf16[128,1536]{1,0:T(8,128)(2,1)S(1)}, bf16[128,1536]{1,0:T(8,128)(2,1)S(1)}, u32[]{:S(2)}, u32[]{:S(2)}) %collective-permute-start.21) | collective-permute-done | bytes 393248 | tf_op jit(solution)/shard_map/ppermute | solution.py:35
  167.0 4.3 %collective-permute-start.22 = (bf16[8,3,1536]{2,1,0:T(4,128)(2,1)S(1)}, bf16[8,3,1536]{2,1,0:T(4,128)(2,1)S(1)}, u32[]{:S(2)}, u32[]{:S(2)}) collective-permute-start(bf16[8,3,1536]{2,1,0:T(4,128)(2,1)S(1)} %get-tuple-element.84), channel_id=1, source_target_pairs={{0,1},{1,2},{2,3},{3,4},{4,5},{5,6},{6,7},{7,8},{8,9},{9,10},{10,1... | collective-permute-start | bytes 221192 | tf_op jit(solution)/shard_map/ppermute | solution.py:73
  172.8 13.4 %collective-permute-done.18.refs_1_ = bf16[8,2,64,384]{3,2,1,0:T(8,128)(2,1)S(1)} collective-permute-done((bf16[8,2,64,384]{3,2,1,0:T(8,128)(2,1)}, bf16[8,2,64,384]{3,2,1,0:T(8,128)(2,1)S(1)}, u32[]{:S(2)}, u32[]{:S(2)}) %collective-permute-start.18) | collective-permute-done | bytes 786464 | tf_op jit(solution)/shard_map/ppermute | solution.py:39
  190.2 5.0 %all-to-all-start.3 = ((bf16[8,2,64,384]{3,2,1,0:T(8,128)(2,1)}), bf16[8,2,64,384]{3,2,1,0:T(8,128)(2,1)S(1)}, u32[]{:S(2)}, u32[]{:S(2)}) async-start(bf16[8,2,64,384]{3,2,1,0:T(8,128)(2,1)} %sum_y.1), calls=%async_computation.3 | async-start | bytes 1572864 | tf_op jit(solution)/shard_map/all_to_all | solution.py:43
  197.6 5.8 %collective-permute-start.25 = (bf16[3,24,1536]{2,1,0:T(8,128)(2,1)S(1)}, bf16[3,24,1536]{2,1,0:T(8,128)(2,1)S(1)}, u32[]{:S(2)}, u32[]{:S(2)}) collective-permute-start(bf16[3,24,1536]{2,1,0:T(8,128)(2,1)S(1)} %get-tuple-element.97), channel_id=1, source_target_pairs={{16,0},{17,1},{18,2},{19,3},{20,4},{21,5},{22,6},{23,7},{24,8},{25... | collective-permute-start | bytes 663560 | tf_op jit(solution)/shard_map/ppermute | solution.py:73
  207.7 9.1 %collective-permute-done.24.up = bf16[3,24,1536]{2,1,0:T(8,128)(2,1)S(1)} collective-permute-done((bf16[3,24,1536]{2,1,0:T(8,128)(2,1)S(1)}, bf16[3,24,1536]{2,1,0:T(8,128)(2,1)S(1)}, u32[]{:S(2)}, u32[]{:S(2)}) %collective-permute-start.24) | collective-permute-done | bytes 221216 | tf_op jit(solution)/shard_map/ppermute | solution.py:73
  216.8 5.6 %convolution.1 = bf16[8,16,1536]{2,1,0:T(8,128)(2,1)} custom-call(bf16[8,16,1536]{2,1,0:T(8,128)(2,1)S(1)} %get-tuple-element.86.own, bf16[8,3,1536]{2,1,0:T(4,128)(2,1)S(1)} %collective-permute-done.22.left, bf16[8,3,1536]{2,1,0:T(4,128)(2,1)S(1)} %collective-permute-done.23.right, bf16[3,24,1536]{2,1,0:T(8,128)(2,1)S(1)} %collective-permute-done.24.up, ...), custom_call_target="tpu_custom_call" | custom-call | tf_op jit(solution)/shard_map/convolution/pallas_call | solution.py:185
  (132 shorter events, 43.8 us)
Async XLA Ops:
  3.6 32.2 %all-to-all-start = ((bf16[8,144,384]{2,1,0:T(8,128)(2,1)}), bf16[8,144,384]{2,1,0:T(8,128)(2,1)S(1)}, u32[]{:S(2)}, u32[]{:S(2)}) async-start(bf16[8,144,384]{2,1,0:T(8,128)(2,1)} %broadcast_in_dim.10), calls=%async_computation | async-start | bytes 1769472 | tf_op jit(solution)/shard_map/all_to_all | solution.py:43
  13.3 19.0 %collective-permute-start.3 = (bf16[256,1536]{1,0:T(8,128)(2,1)S(1)}, bf16[256,1536]{1,0:T(8,128)(2,1)S(1)}, u32[]{:S(2)}, u32[]{:S(2)}) collective-permute-start(bf16[256,1536]{1,0:T(8,128)(2,1)S(1)} %get-tuple-element.55.refs_1_), channel_id=1, source_target_pairs={{0,12},{4,0},{8,4},{12,8},{1,13},{5,1},{9,5},{13,9},{2,14},{6,2},{... | collective-permute-start | bytes 2359304 | tf_op jit(solution)/shard_map/ppermute | solution.py:35
  16.0 19.8 %collective-permute-start.4 = (bf16[256,1536]{1,0:T(8,128)(2,1)S(1)}, bf16[256,1536]{1,0:T(8,128)(2,1)}, u32[]{:S(2)}, u32[]{:S(2)}) collective-permute-start(bf16[256,1536]{1,0:T(8,128)(2,1)S(1)} %get-tuple-element.55.refs_1_), channel_id=1, source_target_pairs={{0,4},{4,8},{8,12},{12,0},{1,5},{5,9},{9,13},{13,1},{2,6},{6,10},{... | collective-permute-start | bytes 2359304 | tf_op jit(solution)/shard_map/ppermute | solution.py:35
  37.2 48.6 %all-to-all-start.1 = ((bf16[8,4,2,32,384]{4,3,2,1,0:T(8,128)(2,1)}), bf16[8,4,2,32,384]{4,3,2,1,0:T(8,128)(2,1)}, u32[]{:S(2)}, u32[]{:S(2)}) async-start(bf16[8,4,2,32,384]{4,3,2,1,0:T(8,128)(2,1)} %broadcast_in_dim.11), calls=%async_computation.1 | async-start | bytes 3145728 | tf_op jit(solution)/shard_map/all_to_all | solution.py:43
  45.4 34.7 %collective-permute-start.5 = (bf16[8,2,64,384]{3,2,1,0:T(8,128)(2,1)}, bf16[8,2,64,384]{3,2,1,0:T(8,128)(2,1)S(1)}, u32[]{:S(2)}, u32[]{:S(2)}) collective-permute-start(bf16[8,2,64,384]{3,2,1,0:T(8,128)(2,1)} %bitcast.12.refs_7_), channel_id=1, source_target_pairs={{0,96},{32,0},{64,32},{96,64},{1,97},{33,1},{65,33},{97,65},{2,98}... | collective-permute-start | bytes 2359304 | tf_op jit(solution)/shard_map/ppermute | solution.py:39
  48.4 34.9 %collective-permute-start.7 = (bf16[8,2,64,384]{3,2,1,0:T(8,128)(2,1)}, bf16[8,2,64,384]{3,2,1,0:T(8,128)(2,1)S(1)}, u32[]{:S(2)}, u32[]{:S(2)}) collective-permute-start(bf16[8,2,64,384]{3,2,1,0:T(8,128)(2,1)} %bitcast.12.refs_7_), channel_id=1, source_target_pairs={{0,32},{32,64},{64,96},{96,0},{1,33},{33,65},{65,97},{97,1},{2,34}... | collective-permute-start | bytes 2359304 | tf_op jit(solution)/shard_map/ppermute | solution.py:39
  48.4 35.0 %collective-permute-start.10 = (bf16[256,1536]{1,0:T(8,128)(2,1)S(1)}, bf16[256,1536]{1,0:T(8,128)(2,1)S(1)}, u32[]{:S(2)}, u32[]{:S(2)}) collective-permute-start(bf16[256,1536]{1,0:T(8,128)(2,1)S(1)} %get-tuple-element.55.refs_1_), channel_id=1, source_target_pairs={{0,8},{4,12},{8,0},{12,4},{1,9},{5,13},{9,1},{13,5},{2,10},{6,14},... | collective-permute-start | bytes 2359304 | tf_op jit(solution)/shard_map/ppermute | solution.py:35
  48.6 34.8 %collective-permute-start.9 = (bf16[8,2,64,384]{3,2,1,0:T(8,128)(2,1)}, bf16[8,2,64,384]{3,2,1,0:T(8,128)(2,1)S(1)}, u32[]{:S(2)}, u32[]{:S(2)}) collective-permute-start(bf16[8,2,64,384]{3,2,1,0:T(8,128)(2,1)} %bitcast.12.refs_7_), channel_id=1, source_target_pairs={{0,64},{32,96},{64,0},{96,32},{1,65},{33,97},{65,1},{97,33},{2,66}... | collective-permute-start | bytes 2359304 | tf_op jit(solution)/shard_map/ppermute | solution.py:39
  120.0 13.3 %collective-permute-start.14 = (bf16[4,8,2,64,384]{4,3,2,1,0:T(8,128)(2,1)}, bf16[4,8,2,64,384]{4,3,2,1,0:T(8,128)(2,1)S(1)}, u32[]{:S(2)}, u32[]{:S(2)}) collective-permute-start(bf16[4,8,2,64,384]{4,3,2,1,0:T(8,128)(2,1)} %get-tuple-element.66), channel_id=1, source_target_pairs={{0,16},{16,0},{1,17},{17,1},{2,18},{18,2},{3,19},{19,3},{4,20},{20... | collective-permute-start | bytes 9437192 | tf_op jit(solution)/shard_map/ppermute | solution.py:60
  120.3 13.0 %collective-permute-start.15 = (bf16[8,4,2,32,384]{4,3,2,1,0:T(8,128)(2,1)}, bf16[8,4,2,32,384]{4,3,2,1,0:T(8,128)(2,1)S(1)}, u32[]{:S(2)}, u32[]{:S(2)}) collective-permute-start(bf16[8,4,2,32,384]{4,3,2,1,0:T(8,128)(2,1)} %get-tuple-element.67), channel_id=1, source_target_pairs={{0,16},{16,0},{1,17},{17,1},{2,18},{18,2},{3,19},{19,3},{4,20},{20... | collective-permute-start | bytes 4718600 | tf_op jit(solution)/shard_map/ppermute | solution.py:60
  120.5 12.8 %collective-permute-start.16 = (bf16[128,1536]{1,0:T(8,128)(2,1)}, bf16[128,1536]{1,0:T(8,128)(2,1)S(1)}, u32[]{:S(2)}, u32[]{:S(2)}) collective-permute-start(bf16[128,1536]{1,0:T(8,128)(2,1)} %get-tuple-element.68), channel_id=1, source_target_pairs={{0,4},{4,8},{8,12},{12,0},{1,5},{5,9},{9,13},{13,1},{2,6},{6,10},{... | collective-permute-start | bytes 1179656 | tf_op jit(solution)/shard_map/ppermute | solution.py:35
  121.2 12.1 %collective-permute-start.17 = (bf16[128,1536]{1,0:T(8,128)(2,1)}, bf16[128,1536]{1,0:T(8,128)(2,1)S(1)}, u32[]{:S(2)}, u32[]{:S(2)}) collective-permute-start(bf16[128,1536]{1,0:T(8,128)(2,1)} %get-tuple-element.69), channel_id=1, source_target_pairs={{0,12},{4,0},{8,4},{12,8},{1,13},{5,1},{9,5},{13,9},{2,14},{6,2},{... | collective-permute-start | bytes 1179656 | tf_op jit(solution)/shard_map/ppermute | solution.py:35
  142.0 48.2 %all-to-all-start.2 = ((bf16[8,4,2,32,384]{4,3,2,1,0:T(8,128)(2,1)}), bf16[8,4,2,32,384]{4,3,2,1,0:T(8,128)(2,1)S(1)}, u32[]{:S(2)}, u32[]{:S(2)}) async-start(bf16[8,4,2,32,384]{4,3,2,1,0:T(8,128)(2,1)} %get-tuple-element.89), calls=%async_computation.2 | async-start | bytes 3145728 | tf_op jit(solution)/shard_map/all_to_all | solution.py:43
  149.4 36.7 %collective-permute-start.18 = (bf16[8,2,64,384]{3,2,1,0:T(8,128)(2,1)}, bf16[8,2,64,384]{3,2,1,0:T(8,128)(2,1)S(1)}, u32[]{:S(2)}, u32[]{:S(2)}) collective-permute-start(bf16[8,2,64,384]{3,2,1,0:T(8,128)(2,1)} %copy-done.16), channel_id=1, source_target_pairs={{0,32},{32,64},{64,96},{96,0},{1,33},{33,65},{65,97},{97,1},{2,34}... | collective-permute-start | bytes 2359304 | tf_op jit(solution)/shard_map/ppermute | solution.py:39
  149.4 36.7 %collective-permute-start.19 = (bf16[8,2,64,384]{3,2,1,0:T(8,128)(2,1)}, bf16[8,2,64,384]{3,2,1,0:T(8,128)(2,1)S(1)}, u32[]{:S(2)}, u32[]{:S(2)}) collective-permute-start(bf16[8,2,64,384]{3,2,1,0:T(8,128)(2,1)} %copy-done.15), channel_id=1, source_target_pairs={{0,64},{32,96},{64,0},{96,32},{1,65},{33,97},{65,1},{97,33},{2,66}... | collective-permute-start | bytes 2359304 | tf_op jit(solution)/shard_map/ppermute | solution.py:39
  152.2 34.5 %collective-permute-start.20 = (bf16[8,2,64,384]{3,2,1,0:T(8,128)(2,1)}, bf16[8,2,64,384]{3,2,1,0:T(8,128)(2,1)S(1)}, u32[]{:S(2)}, u32[]{:S(2)}) collective-permute-start(bf16[8,2,64,384]{3,2,1,0:T(8,128)(2,1)} %copy-done.14), channel_id=1, source_target_pairs={{0,96},{32,0},{64,32},{96,64},{1,97},{33,1},{65,33},{97,65},{2,98}... | collective-permute-start | bytes 2359304 | tf_op jit(solution)/shard_map/ppermute | solution.py:39
  167.0 21.1 %collective-permute-start.22 = (bf16[8,3,1536]{2,1,0:T(4,128)(2,1)S(1)}, bf16[8,3,1536]{2,1,0:T(4,128)(2,1)S(1)}, u32[]{:S(2)}, u32[]{:S(2)}) collective-permute-start(bf16[8,3,1536]{2,1,0:T(4,128)(2,1)S(1)} %get-tuple-element.84), channel_id=1, source_target_pairs={{0,1},{1,2},{2,3},{3,4},{4,5},{5,6},{6,7},{7,8},{8,9},{9,10},{10,1... | collective-permute-start | bytes 221192 | tf_op jit(solution)/shard_map/ppermute | solution.py:73
  171.2 16.8 %collective-permute-start.23 = (bf16[8,3,1536]{2,1,0:T(4,128)(2,1)S(1)}, bf16[8,3,1536]{2,1,0:T(4,128)(2,1)S(1)}, u32[]{:S(2)}, u32[]{:S(2)}) collective-permute-start(bf16[8,3,1536]{2,1,0:T(4,128)(2,1)S(1)} %get-tuple-element.85), channel_id=1, source_target_pairs={{1,0},{2,1},{3,2},{4,3},{5,4},{6,5},{7,6},{8,7},{9,8},{10,9},{11,1... | collective-permute-start | bytes 221192 | tf_op jit(solution)/shard_map/ppermute | solution.py:73
  190.2 32.2 %all-to-all-start.3 = ((bf16[8,2,64,384]{3,2,1,0:T(8,128)(2,1)}), bf16[8,2,64,384]{3,2,1,0:T(8,128)(2,1)S(1)}, u32[]{:S(2)}, u32[]{:S(2)}) async-start(bf16[8,2,64,384]{3,2,1,0:T(8,128)(2,1)} %sum_y.1), calls=%async_computation.3 | async-start | bytes 1572864 | tf_op jit(solution)/shard_map/all_to_all | solution.py:43
  195.6 21.2 %collective-permute-start.24 = (bf16[3,24,1536]{2,1,0:T(8,128)(2,1)S(1)}, bf16[3,24,1536]{2,1,0:T(8,128)(2,1)S(1)}, u32[]{:S(2)}, u32[]{:S(2)}) collective-permute-start(bf16[3,24,1536]{2,1,0:T(8,128)(2,1)S(1)} %get-tuple-element.96), channel_id=1, source_target_pairs={{0,16},{1,17},{2,18},{3,19},{4,20},{5,21},{6,22},{7,23},{8,24},{9,... | collective-permute-start | bytes 663560 | tf_op jit(solution)/shard_map/ppermute | solution.py:73
  197.6 19.2 %collective-permute-start.25 = (bf16[3,24,1536]{2,1,0:T(8,128)(2,1)S(1)}, bf16[3,24,1536]{2,1,0:T(8,128)(2,1)S(1)}, u32[]{:S(2)}, u32[]{:S(2)}) collective-permute-start(bf16[3,24,1536]{2,1,0:T(8,128)(2,1)S(1)} %get-tuple-element.97), channel_id=1, source_target_pairs={{16,0},{17,1},{18,2},{19,3},{20,4},{21,5},{22,6},{23,7},{24,8},{25... | collective-permute-start | bytes 663560 | tf_op jit(solution)/shard_map/ppermute | solution.py:73
  203.3 19.1 %collective-permute-start.26 = (bf16[2,32,384]{2,1,0:T(8,128)(2,1)S(1)}, bf16[2,32,384]{2,1,0:T(8,128)(2,1)S(1)}, u32[]{:S(2)}, u32[]{:S(2)}) collective-permute-start(bf16[2,32,384]{2,1,0:T(8,128)(2,1)S(1)} %get-tuple-element.101), channel_id=1, source_target_pairs={{0,32},{32,64},{64,96},{96,0},{1,33},{33,65},{65,97},{97,1},{2,34}... | collective-permute-start | bytes 147464 | tf_op jit(solution)/shard_map/ppermute | solution.py:39
  203.4 19.0 %collective-permute-start.27 = (bf16[2,32,384]{2,1,0:T(8,128)(2,1)S(1)}, bf16[2,32,384]{2,1,0:T(8,128)(2,1)S(1)}, u32[]{:S(2)}, u32[]{:S(2)}) collective-permute-start(bf16[2,32,384]{2,1,0:T(8,128)(2,1)S(1)} %get-tuple-element.102), channel_id=1, source_target_pairs={{0,64},{32,96},{64,0},{96,32},{1,65},{33,97},{65,1},{97,33},{2,66}... | collective-permute-start | bytes 147464 | tf_op jit(solution)/shard_map/ppermute | solution.py:39
  205.1 17.3 %collective-permute-start.28 = (bf16[2,32,384]{2,1,0:T(8,128)(2,1)S(1)}, bf16[2,32,384]{2,1,0:T(8,128)(2,1)S(1)}, u32[]{:S(2)}, u32[]{:S(2)}) collective-permute-start(bf16[2,32,384]{2,1,0:T(8,128)(2,1)S(1)} %get-tuple-element.103), channel_id=1, source_target_pairs={{0,96},{32,0},{64,32},{96,64},{1,97},{33,1},{65,33},{97,65},{2,98}... | collective-permute-start | bytes 147464 | tf_op jit(solution)/shard_map/ppermute | solution.py:39
  (39 other events, 263.4 us)

commit v3 on v2

--- a/solution.py
+++ b/solution.py
@@ -20,6 +20,7 @@
 NX, NY, NZ = 4, 4, 8
 CHAN, HIDDEN = 1536, 1536
 ROWS, COLS = 96, 384
+PLANES = 8
 AY, BY = 32, 64
 BLOCK = 128
 TOKENS = BLOCK * NX
@@ -200,132 +201,157 @@
     return pl.multiple_of(row, 32), slice(k % 4 * COLS, k % 4 * COLS + COLS)
 
 
-def compute_kernel(where, *refs):
-    n = 0
-
-    def take(count):
-        nonlocal n
-        n += count
-        return refs[n - count : n]
-
-    bias = take(1)[0]
-    tok = take(NX)
-    first = take(2)
-    second = [take(NY), take(NY)]
-    out_y = take(2)
-    out_z = take(2)
-    gn = take(NX)
-    w, xs, xt, acts, g = take(5)
+def own_row(j, c):
+    return pl.multiple_of((2 * j + c) * ROWS, 32)
+
+
+def token_kernel(where, *refs):
+    tok, (xs, mine, other, xt) = refs[:NX], refs[NX:]
+    c = where[1]
     for i in range(NX):
         rows = slice(i * BLOCK, (i + 1) * BLOCK)
         xs[0, rows, :] = tok[i][:BLOCK]
         xs[1, rows, :] = tok[i][BLOCK:]
+    for m in range(2):
+        for i in range(CHAN // 256):
+            xt[i * 256 : (i + 1) * 256, :] = xs[m, :, i * 256 : (i + 1) * 256].T
+        for out, core in ((mine, c), (other, 1 - c)):
+            for j in range(PLANES):
+                row = own_row(j, core)
+                row2 = pl.multiple_of(row + AY, 32)
+                out[m, j * AY : (j + 1) * AY, :] = xt[pl.ds(row, AY), :]
+                start = PLANES * AY + j * BY
+                out[m, start : start + BY, :] = xt[pl.ds(row2, BY), :]
+
+
+def tokens(where, tok):
+    half = jax.ShapeDtypeStruct((2, CHAN // 2, TOKENS), bf16)
+    return pl.pallas_call(
+        token_kernel,
+        out_shape=[jax.ShapeDtypeStruct((2, TOKENS, CHAN), bf16), half, half],
+        in_specs=[pl.BlockSpec(memory_space=pltpu.SMEM)] + vmem_specs(NX),
+        out_specs=vmem_specs(3),
+        scratch_shapes=[pltpu.VMEM((CHAN, TOKENS), bf16)],
+        compiler_params=pltpu.CompilerParams(vmem_limit_bytes=20 * 2**20),
+        cost_estimate=pl.CostEstimate(flops=0, bytes_accessed=12_000_000, transcendentals=0),
+        name="tokens",
+    )(where, *tok)
+
+
+def activation_kernel(where, *refs):
+    bias, xs = refs[:2]
+    first = refs[2:4]
+    second = refs[4 : 4 + NY], refs[4 + NY : 4 + 2 * NY]
+    act, pre_grad, w_in, w_out = refs[4 + 2 * NY :]
     for d in range(2):
         for k in range(NZ):
             for r in range(NY):
                 row, col = place(where, d, k, r)
-                for m in range(2):
-                    row2 = pl.multiple_of(row + AY, 32)
-                    w[m, pl.ds(row, AY), col] = first[d][k, r, m]
-                    w[m, pl.ds(row2, BY), col] = second[d][r][k, m]
-    for m in range(2):
-        for i in range(CHAN // 256):
-            xt[m, i * 256 : (i + 1) * 256, :] = xs[m, :, i * 256 : (i + 1) * 256].T
+                row2 = pl.multiple_of(row + AY, 32)
+                for m, w in ((0, w_in), (1, w_out)):
+                    w[pl.ds(row, AY), col] = first[d][k, r, m]
+                    w[pl.ds(row2, BY), col] = second[d][r][k, m]
 
     width = 256
 
-    def activations(i, _):
+    def step(i, _):
         cols = pl.ds(pl.multiple_of(i * width, width), width)
-        pre = jnp.dot(xs[0], w[0, :, cols], preferred_element_type=f32) + bias[:, cols]
-        back = jnp.dot(xs[1], w[1, :, cols], preferred_element_type=f32)
+        pre = jnp.dot(xs[0], w_in[:, cols], preferred_element_type=f32) + bias[:, cols]
+        back = jnp.dot(xs[1], w_out[:, cols], preferred_element_type=f32)
         cdf = 0.5 * (1.0 + lax.erf(pre * root_half))
         slope = cdf + pre * jnp.exp(-0.5 * pre * pre) * density_norm
-        act = (pre * cdf).astype(bf16)
-        acts[:, cols] = (back * slope).astype(bf16)
-        g[:, cols] = jnp.dot(xt[1], act, preferred_element_type=f32).astype(bf16)
+        act[:, cols] = (pre * cdf).astype(bf16)
+        pre_grad[:, cols] = (back * slope).astype(bf16)
         return 0
 
-    def flush(m):
-        for d in range(2):
-            for k in range(NZ):
-                for r in range(NY):
-                    row, col = place(where, d, k, r)
-                    row2 = pl.multiple_of(row + AY, 32)
-                    out_z[d][k, r, m] = g[pl.ds(row, AY), col]
-                    out_y[d][r, k, m] = g[pl.ds(row2, BY), col]
-
-    lax.fori_loop(0, HIDDEN // width, activations, 0)
-    flush(1)
-
-    def gradient_in(i, _):
-        cols = pl.ds(pl.multiple_of(i * width, width), width)
-        g[:, cols] = jnp.dot(xt[0], acts[:, cols], preferred_element_type=f32).astype(bf16)
-        return 0
-
-    lax.fori_loop(0, HIDDEN // width, gradient_in, 0)
-    flush(0)
-
-    def gradient_normed(i, _):
+    lax.fori_loop(0, HIDDEN // width, step, 0)
+
+
+def activations(where, bias, xs, first, second):
+    operands = [bias, xs, *first, *second[0], *second[1]]
+    out = jax.ShapeDtypeStruct((TOKENS, HIDDEN), bf16)
+    return pl.pallas_call(
+        activation_kernel,
+        out_shape=[out, out, jax.ShapeDtypeStruct((CHAN, HIDDEN), bf16)],
+        in_specs=[pl.BlockSpec(memory_space=pltpu.SMEM)] + vmem_specs(len(operands)),
+        out_specs=vmem_specs(3),
+        scratch_shapes=[pltpu.VMEM((CHAN, HIDDEN), bf16)],
+        compiler_params=pltpu.CompilerParams(vmem_limit_bytes=40 * 2**20),
+        cost_estimate=pl.CostEstimate(
+            flops=4 * TOKENS * CHAN * HIDDEN, bytes_accessed=25_000_000, transcendentals=0
+        ),
+        name="activations",
+    )(where, *operands)
+
+
+def normed_kernel(pre_grad, w_in, *outs):
+    width = 256
+
+    def step(i, _):
         cols = pl.ds(pl.multiple_of(i * width, width), width)
         part = lax.dot_general(
-            acts[...], w[0, cols, :], (((1,), (1,)), ((), ())), preferred_element_type=f32
+            pre_grad[...], w_in[cols, :], (((1,), (1,)), ((), ())), preferred_element_type=f32
         ).astype(bf16)
         for b in range(NX):
-            gn[b][:, cols] = part[b * BLOCK : (b + 1) * BLOCK]
+            outs[b][:, cols] = part[b * BLOCK : (b + 1) * BLOCK]
         return 0
 
-    lax.fori_loop(0, CHAN // width, gradient_normed, 0)
-
-
-def compute(where, bias, tok, first, second):
-    vmem = pl.BlockSpec(memory_space=pltpu.VMEM)
-    gy = jax.ShapeDtypeStruct((NY, NZ, 2, BY, COLS), bf16)
-    gz = jax.ShapeDtypeStruct((NZ, NY, 2, AY, COLS), bf16)
-    gn = jax.ShapeDtypeStruct((BLOCK, CHAN), bf16)
-    operands = [bias, *tok, *first, *second[0], *second[1]]
+    lax.fori_loop(0, CHAN // width, step, 0)
+
+
+def normed_gradient(pre_grad, w_in):
+    return pl.pallas_call(
+        normed_kernel,
+        out_shape=[jax.ShapeDtypeStruct((BLOCK, CHAN), bf16)] * NX,
+        in_specs=vmem_specs(2),
+        out_specs=vmem_specs(NX),
+        compiler_params=pltpu.CompilerParams(vmem_limit_bytes=20 * 2**20),
+        cost_estimate=pl.CostEstimate(
+            flops=2 * TOKENS * CHAN * HIDDEN, bytes_accessed=20_000_000, transcendentals=0
+        ),
+        name="normed_gradient",
+    )(pre_grad, w_in)
+
+
+def weight_kernel(where, mine, got, *refs):
+    sides, (ys, out_z, g) = (refs[0:2], refs[2:4]), (refs[4 : 4 + NY], *refs[4 + NY :])
+    width = 256
+    for m in range(2):
+        own, other = sides[m]
+
+        def step(i, _, m=m, own=own, other=other):
+            cols = pl.ds(pl.multiple_of(i * width, width), width)
+            value = jnp.dot(mine[m], own[:, cols], preferred_element_type=f32)
+            value = value + jnp.dot(got[m], other[:, cols], preferred_element_type=f32)
+            g[:, cols] = value.astype(bf16)
+            return 0
+
+        lax.fori_loop(0, HIDDEN // width, step, 0)
+        for k in range(NZ):
+            col = slice(k % 4 * COLS, k % 4 * COLS + COLS)
+            for r in range(NY):
+                j = k // 4 * NY + lax.rem(where[0] + r, NY)
+                row = pl.multiple_of(j * AY, 32)
+                row2 = pl.multiple_of(PLANES * AY + j * BY, 32)
+                out_z[k, r, m] = g[pl.ds(row, AY), col]
+                ys[r][k, m] = g[pl.ds(row2, BY), col]
+
+
+def weight_gradients(where, mine, got, pre_grad, other_pre_grad, act, other_act):
+    operands = [mine, got, pre_grad, other_pre_grad, act, other_act]
     out = pl.pallas_call(
-        compute_kernel,
-        out_shape=[gy, gy, gz, gz] + [gn] * NX,
-        in_specs=[pl.BlockSpec(memory_space=pltpu.SMEM)] + [vmem] * len(operands),
-        out_specs=[vmem] * (4 + NX),
-        scratch_shapes=[
-            pltpu.VMEM((2, CHAN, HIDDEN), bf16),
-            pltpu.VMEM((2, TOKENS, CHAN), bf16),
-            pltpu.VMEM((2, CHAN, TOKENS), bf16),
-            pltpu.VMEM((TOKENS, HIDDEN), bf16),
-            pltpu.VMEM((CHAN, HIDDEN), bf16),
-        ],
-        compiler_params=pltpu.CompilerParams(vmem_limit_bytes=60 * 2**20),
+        weight_kernel,
+        out_shape=[jax.ShapeDtypeStruct((NZ, 2, BY, COLS), bf16)] * NY
+        + [jax.ShapeDtypeStruct((NZ, NY, 2, AY, COLS), bf16)],
+        in_specs=[pl.BlockSpec(memory_space=pltpu.SMEM)] + vmem_specs(len(operands)),
+        out_specs=vmem_specs(NY + 1),
+        scratch_shapes=[pltpu.VMEM((CHAN // 2, HIDDEN), bf16)],
+        compiler_params=pltpu.CompilerParams(vmem_limit_bytes=32 * 2**20),
         cost_estimate=pl.CostEstimate(
-            flops=10 * TOKENS * CHAN * HIDDEN, bytes_accessed=25_000_000, transcendentals=0
+            flops=4 * TOKENS * CHAN * HIDDEN, bytes_accessed=30_000_000, transcendentals=0
         ),
-        name="block",
+        name="weight_gradients",
     )(where, *operands)
-    return out[0:2], out[2:4], out[4:]
-
-
-def add_kernel(*refs):
-    own_y, got_y, own_z, got_z = refs[:4]
-    ys, zs = refs[4 : 4 + NY], refs[4 + NY]
-    for r in range(NY):
-        for k in range(NZ):
-            ys[r][k] = (own_y[r, k].astype(f32) + got_y[r, k].astype(f32)).astype(bf16)
-    for k in range(NZ):
-        for r in range(NY):
-            zs[k, r] = (own_z[k, r].astype(f32) + got_z[k, r].astype(f32)).astype(bf16)
-
-
-def add_cores(own_y, got_y, own_z, got_z):
-    vmem = pl.BlockSpec(memory_space=pltpu.VMEM)
-    out = pl.pallas_call(
-        add_kernel,
-        out_shape=[jax.ShapeDtypeStruct(own_y.shape[1:], bf16)] * NY
-        + [jax.ShapeDtypeStruct(own_z.shape, bf16)],
-        in_specs=[vmem] * 4,
-        out_specs=[vmem] * (NY + 1),
-        compiler_params=pltpu.CompilerParams(vmem_limit_bytes=40 * 2**20),
-        name="add_cores",
-    )(own_y, got_y, own_z, got_z)
     return out[:NY], out[NY]
 
 
@@ -421,21 +447,25 @@
     second = [to_y(rest_z, -r) for r in range(NY)]
     first = gather_z(lead_y)
     swapped = [swap(v) for v in second[:2]] + [None, swap(second[3])]
-    first, swapped[1], swapped[3], second[2], tok[2] = lax.optimization_barrier(
-        (first, swapped[1], swapped[3], second[2], tok[2])
+    where = jnp.stack([lax.axis_index("y"), lax.axis_index("c")]).astype(jnp.int32)
+    tok[2], second[2] = lax.optimization_barrier((tok[2], second[2]))
+    xs, mine, other = tokens(where, tok)
+    first, swapped[1], swapped[3], xs = lax.optimization_barrier(
+        (first, swapped[1], swapped[3], xs)
     )
+    other = swap(other)
     swapped[2] = swap(second[2])
     second = [second, swapped]
     first = [first, swap(first)]
 
-    where = jnp.stack([lax.axis_index("y"), lax.axis_index("c")]).astype(jnp.int32)
-    grad_y, grad_z, part = compute(where, bias, tok, first, second)
-
+    act, pre_grad, w_all = activations(where, bias, xs, first, second)
+    other_act, other_pre_grad = swap(act), swap(pre_grad)
+    part = normed_gradient(pre_grad, w_all)
+    other_act, other_pre_grad, *part = lax.optimization_barrier(
+        (other_act, other_pre_grad, *part)
+    )
     part = [to_x(v, r) for r, v in enumerate(part)]
-    other_y, other_z, part[1], part[3] = lax.optimization_barrier(
-        (swap(grad_y[1]), swap(grad_z[1]), part[1], part[3])
-    )
-    ys, zs = add_cores(grad_y[0], other_y, grad_z[0], other_z)
+    ys, zs = weight_gradients(where, mine, other, pre_grad, other_pre_grad, act, other_act)
     ys = [to_y(v, r) for r, v in enumerate(ys)]
     own, first_cols, last_cols = layer_norm_backward(part, xhat, inverse, gain)
     left, right = to_tile(last_cols, 0, 1), to_tile(first_cols, 0, -1)

time: 225 us -> 216 us (0.960)
  waiting for transfers between devices: 95.4 us -> 83.7 us
  local copies, waits for them, and re-layouts: 20.5 us -> 23.1 us
  Pallas kernels: 38.1 us -> 35.8 us
    ppermute x12, waiting for transfers between devices: 51.1 us -> 37.9 us  [to_y(): return lax.ppermute(value, 'y', shift(NY, k)) if k else value]
    ppermute x6, waiting for transfers between devices: 28.8 us -> 32.1 us  [to_x(): return lax.ppermute(value, 'x', shift(NX, k)) if k else value]
    pallas_call x2 -> x4, Pallas kernels: 29.2 us -> 26.8 us  [the longest x1 11.8 us: activations(): pl.pallas_call(activation_kernel, out_shape=[out, out, jax.ShapeDtypeStru...]
    unnamed x62 -> x60, local copies, waits for them, and re-layouts: 15.8 us -> 18.1 us
  transfers between devices with their start and end apart: 33 -> 34, of which waited for: 16 -> 14; matrix products, arithmetic and copies ran while one was open for 1% -> 1% of each run, Pallas kernels for 4% -> 7%
where the time goes in v3:
time: 216 us; the launch traced here: 215 us
  waiting for transfers between devices  83.7 us (39%)
  starting transfers between devices  68.9 us (32%)
  Pallas kernels  35.8 us (17%)
  local copies, waits for them, and re-layouts  23.1 us (11%)
  other arithmetic  2.42 us (1%)
    ppermute x12, waiting for transfers between devices, to_y(): return lax.ppermute(value, 'y', shift(NY, k)) if k else value  37.9 us
    ppermute x6, waiting for transfers between devices, to_x(): return lax.ppermute(value, 'x', shift(NX, k)) if k else value  32.1 us
    all_to_all x4, starting transfers between devices, exchange_z(): return lax.all_to_all(value, Z, 0, 0, tiled=True)  30 us
    unnamed x60, local copies, waits for them, and re-layouts  18.1 us
    ppermute x12, starting transfers between devices, to_y(): return lax.ppermute(value, 'y', shift(NY, k)) if k else value  17.8 us
    ppermute x4, starting transfers between devices, to_tile(): return lax.ppermute(value, FINE, pairs)  13.2 us
    pallas_call x1, Pallas kernels, activations(): pl.pallas_call(activation_kernel, out_shape=[out, out, jax.ShapeDtypeStru...  11.8 us
    ppermute x4, waiting for transfers between devices, to_tile(): return lax.ppermute(value, FINE, pairs)  9.46 us
  transfers between devices with their start and end apart: 34, of which 14 were waited for; matrix products, arithmetic and copies ran while one was open for 1% of the time, Pallas kernels for 7%

profile of v3, /device:TPU:32, one launch (start us, length us, event | category | flops | bytes accessed | tf_op | source)
XLA Modules:
  0.0 214.9 jit_solution(3370832326185521981)
XLA Ops:
  3.6 8.6 %all-to-all-start = ((bf16[8,144,384]{2,1,0:T(8,128)(2,1)}), bf16[8,144,384]{2,1,0:T(8,128)(2,1)S(1)}, u32[]{:S(2)}, u32[]{:S(2)}) async-start(bf16[8,144,384]{2,1,0:T(8,128)(2,1)} %broadcast_in_dim.10), calls=%async_computation | async-start | bytes 1769472 | tf_op jit(solution)/shard_map/all_to_all | solution.py:44
  13.5 2.8 %collective-permute-start.3 = (bf16[256,1536]{1,0:T(8,128)(2,1)S(1)}, bf16[256,1536]{1,0:T(8,128)(2,1)S(1)}, u32[]{:S(2)}, u32[]{:S(2)}) collective-permute-start(bf16[256,1536]{1,0:T(8,128)(2,1)S(1)} %get-tuple-element.60.refs_0_), channel_id=1, source_target_pairs={{0,12},{4,0},{8,4},{12,8},{1,13},{5,1},{9,5},{13,9},{2,14},{6,2},{... | collective-permute-start | bytes 2359304 | tf_op jit(solution)/shard_map/ppermute | solution.py:36
  18.0 2.9 %collective-permute-start.1 = (bf16[2,32,384]{2,1,0:T(8,128)(2,1)S(1)}, bf16[2,32,384]{2,1,0:T(8,128)(2,1)S(1)}, u32[]{:S(2)}, u32[]{:S(2)}) collective-permute-start(bf16[2,32,384]{2,1,0:T(8,128)(2,1)S(1)} %pad_maximum_fusion.1), channel_id=1, source_target_pairs={{0,64},{32,96},{64,0},{96,32},{1,65},{33,97},{65,1},{97,33},{2,66}... | collective-permute-start | bytes 147464 | tf_op jit(solution)/shard_map/ppermute | solution.py:40
  25.0 7.5 %collective-permute-done.3.refs_1_ = bf16[256,1536]{1,0:T(8,128)(2,1)S(1)} collective-permute-done((bf16[256,1536]{1,0:T(8,128)(2,1)S(1)}, bf16[256,1536]{1,0:T(8,128)(2,1)S(1)}, u32[]{:S(2)}, u32[]{:S(2)}) %collective-permute-start.3) | collective-permute-done | bytes 786464 | tf_op jit(solution)/shard_map/ppermute | solution.py:36
  33.4 2.5 %collective-permute-done.4.refs_3_ = bf16[256,1536]{1,0:T(8,128)(2,1)S(1)} collective-permute-done((bf16[256,1536]{1,0:T(8,128)(2,1)S(1)}, bf16[256,1536]{1,0:T(8,128)(2,1)S(1)}, u32[]{:S(2)}, u32[]{:S(2)}) %collective-permute-start.4) | collective-permute-done | bytes 786464 | tf_op jit(solution)/shard_map/ppermute | solution.py:36
  38.3 7.2 %all-to-all-start.1 = ((bf16[8,4,2,32,384]{4,3,2,1,0:T(8,128)(2,1)}), bf16[8,4,2,32,384]{4,3,2,1,0:T(8,128)(2,1)S(1)}, u32[]{:S(2)}, u32[]{:S(2)}) async-start(bf16[8,4,2,32,384]{4,3,2,1,0:T(8,128)(2,1)} %broadcast_in_dim.11), calls=%async_computation.1 | async-start | bytes 3145728 | tf_op jit(solution)/shard_map/all_to_all | solution.py:44
  46.7 3.1 %collective-permute-start.8 = (bf16[8,2,64,384]{3,2,1,0:T(8,128)(2,1)S(1)}, bf16[8,2,64,384]{3,2,1,0:T(8,128)(2,1)}, u32[]{:S(2)}, u32[]{:S(2)}) collective-permute-start(bf16[8,2,64,384]{3,2,1,0:T(8,128)(2,1)S(1)} %bitcast.19), channel_id=1, source_target_pairs={{0,96},{32,0},{64,32},{96,64},{1,97},{33,1},{65,33},{97,65},{2,98}... | collective-permute-start | bytes 2359304 | tf_op jit(solution)/shard_map/ppermute | solution.py:40
  52.3 28.9 %collective-permute-done.8.refs_5_ = bf16[8,2,64,384]{3,2,1,0:T(8,128)(2,1)} collective-permute-done((bf16[8,2,64,384]{3,2,1,0:T(8,128)(2,1)S(1)}, bf16[8,2,64,384]{3,2,1,0:T(8,128)(2,1)}, u32[]{:S(2)}, u32[]{:S(2)}) %collective-permute-start.8) | collective-permute-done | bytes 786464 | tf_op jit(solution)/shard_map/ppermute | solution.py:40
  81.2 3.5 %collective-permute-done.10.refs_7_ = bf16[8,2,64,384]{3,2,1,0:T(8,128)(2,1)} collective-permute-done((bf16[8,2,64,384]{3,2,1,0:T(8,128)(2,1)S(1)}, bf16[8,2,64,384]{3,2,1,0:T(8,128)(2,1)}, u32[]{:S(2)}, u32[]{:S(2)}) %collective-permute-start.10) | collective-permute-done | bytes 786464 | tf_op jit(solution)/shard_map/ppermute | solution.py:40
  95.2 4.0 %collective-permute-done.13.refs_8_ = bf16[8,2,64,384]{3,2,1,0:T(8,128)(2,1)S(1)} collective-permute-done((bf16[8,2,64,384]{3,2,1,0:T(8,128)(2,1)S(1)}, bf16[8,2,64,384]{3,2,1,0:T(8,128)(2,1)S(1)}, u32[]{:S(2)}, u32[]{:S(2)}) %collective-permute-start.13) | collective-permute-done | bytes 786464 | tf_op jit(solution)/shard_map/ppermute | solution.py:61
  99.4 11.8 %activations.1 = (bf16[512,1536]{1,0:T(8,128)(2,1)S(1)}, bf16[512,1536]{1,0:T(8,128)(2,1)S(1)}, bf16[1536,1536]{1,0:T(8,128)(2,1)}) custom-call(s32[2]{0:T(128)S(1)} %pad_add_fusion.where, f32[1,1536]{1,0:T(1,128)S(1)} %bitcast.25, bf16[2,512,1536]{2,1,0:T(8,128)(2,1)} %copy-done.12, bf16[8,4,2,32,384]{4,3,2,1,0:T(8,128)(2,1)S(1)} %all-to-all-done.1.refs_2_, ...), custom_call_target="tpu_custom_call" | custom-call | flops 4831838208 | bytes 25000000 | tf_op jit(solution)/shard_map/activations/pallas_call | solution.py:273
  114.4 3.6 %normed_gradient.1 = (bf16[128,1536]{1,0:T(8,128)(2,1)S(1)}, bf16[128,1536]{1,0:T(8,128)(2,1)S(1)}, bf16[128,1536]{1,0:T(8,128)(2,1)S(1)}, bf16[128,1536]{1,0:T(8,128)(2,1)S(1)}) custom-call(bf16[512,1536]{1,0:T(8,128)(2,1)S(1)} %get-tuple-element.74.pre_grad.refs_0_, bf16[1536,1536]{1,0:T(8,128)(2,1)S(1)} %copy-done.22), custom_call_target="tpu_custom_call" | custom-call | flops 2415919104 | bytes 20000000 | tf_op jit(solution)/shard_map/normed_gradient/pallas_call | solution.py:303
  119.6 9.1 %weight_gradients.1 = (bf16[8,2,64,384]{3,2,1,0:T(8,128)(2,1)S(1)}, bf16[8,2,64,384]{3,2,1,0:T(8,128)(2,1)S(1)}, bf16[8,2,64,384]{3,2,1,0:T(8,128)(2,1)S(1)}, bf...) custom-call(s32[2]{0:T(128)S(1)} %pad_add_fusion.where, bf16[2,768,512]{2,1,0:T(8,128)(2,1)S(1)} %copy-done.14, ...), custom_call_target="tpu_custom_call" | custom-call | flops 4831838208 | bytes 30000000 | tf_op jit(solution)/shard_map/weight_gradients/pallas_call | solution.py:342
  132.3 7.3 %all-to-all-start.2 = ((bf16[8,4,2,32,384]{4,3,2,1,0:T(8,128)(2,1)}), bf16[8,4,2,32,384]{4,3,2,1,0:T(8,128)(2,1)S(1)}, u32[]{:S(2)}, u32[]{:S(2)}) async-start(bf16[8,4,2,32,384]{4,3,2,1,0:T(8,128)(2,1)} %get-tuple-element.99), calls=%async_computation.2 | async-start | bytes 3145728 | tf_op jit(solution)/shard_map/all_to_all | solution.py:44
  143.0 2.8 %collective-permute-start.21 = (bf16[128,1536]{1,0:T(8,128)(2,1)}, bf16[128,1536]{1,0:T(8,128)(2,1)S(1)}, u32[]{:S(2)}, u32[]{:S(2)}) collective-permute-start(bf16[128,1536]{1,0:T(8,128)(2,1)} %copy-done.20), channel_id=1, source_target_pairs={{0,8},{4,12},{8,0},{12,4},{1,9},{5,13},{9,1},{13,5},{2,10},{6,14},... | collective-permute-start | bytes 1179656 | tf_op jit(solution)/shard_map/ppermute | solution.py:36
  145.8 14.3 %collective-permute-done.20.refs_1_ = bf16[128,1536]{1,0:T(8,128)(2,1)S(1)} collective-permute-done((bf16[128,1536]{1,0:T(8,128)(2,1)}, bf16[128,1536]{1,0:T(8,128)(2,1)S(1)}, u32[]{:S(2)}, u32[]{:S(2)}) %collective-permute-start.20) | collective-permute-done | bytes 393248 | tf_op jit(solution)/shard_map/ppermute | solution.py:36
  160.1 7.8 %collective-permute-done.22.refs_3_ = bf16[128,1536]{1,0:T(8,128)(2,1)S(1)} collective-permute-done((bf16[128,1536]{1,0:T(8,128)(2,1)S(1)}, bf16[128,1536]{1,0:T(8,128)(2,1)S(1)}, u32[]{:S(2)}, u32[]{:S(2)}) %collective-permute-start.22) | collective-permute-done | bytes 393248 | tf_op jit(solution)/shard_map/ppermute | solution.py:36
  169.2 4.3 %collective-permute-start.23 = (bf16[8,3,1536]{2,1,0:T(4,128)(2,1)S(1)}, bf16[8,3,1536]{2,1,0:T(4,128)(2,1)S(1)}, u32[]{:S(2)}, u32[]{:S(2)}) collective-permute-start(bf16[8,3,1536]{2,1,0:T(4,128)(2,1)S(1)} %get-tuple-element.94), channel_id=1, source_target_pairs={{0,1},{1,2},{2,3},{3,4},{4,5},{5,6},{6,7},{7,8},{8,9},{9,10},{10,1... | collective-permute-start | bytes 221192 | tf_op jit(solution)/shard_map/ppermute | solution.py:74
  178.9 2.8 %collective-permute-done.24.right = bf16[8,3,1536]{2,1,0:T(4,128)(2,1)S(1)} collective-permute-done((bf16[8,3,1536]{2,1,0:T(4,128)(2,1)S(1)}, bf16[8,3,1536]{2,1,0:T(4,128)(2,1)S(1)}, u32[]{:S(2)}, u32[]{:S(2)}) %collective-permute-start.24) | collective-permute-done | bytes 73760 | tf_op jit(solution)/shard_map/ppermute | solution.py:74
  181.7 6.9 %all-to-all-start.3 = ((bf16[8,2,64,384]{3,2,1,0:T(8,128)(2,1)}), bf16[8,2,64,384]{3,2,1,0:T(8,128)(2,1)S(1)}, u32[]{:S(2)}, u32[]{:S(2)}) async-start(bf16[8,2,64,384]{3,2,1,0:T(8,128)(2,1)} %sum_y.1), calls=%async_computation.3 | async-start | bytes 1572864 | tf_op jit(solution)/shard_map/all_to_all | solution.py:44
  190.9 5.8 %collective-permute-start.26 = (bf16[3,24,1536]{2,1,0:T(8,128)(2,1)S(1)}, bf16[3,24,1536]{2,1,0:T(8,128)(2,1)S(1)}, u32[]{:S(2)}, u32[]{:S(2)}) collective-permute-start(bf16[3,24,1536]{2,1,0:T(8,128)(2,1)S(1)} %get-tuple-element.107), channel_id=1, source_target_pairs={{16,0},{17,1},{18,2},{19,3},{20,4},{21,5},{22,6},{23,7},{24,8},{25... | collective-permute-start | bytes 663560 | tf_op jit(solution)/shard_map/ppermute | solution.py:74
  196.8 3.1 %collective-permute-start.29 = (bf16[2,32,384]{2,1,0:T(8,128)(2,1)S(1)}, bf16[2,32,384]{2,1,0:T(8,128)(2,1)S(1)}, u32[]{:S(2)}, u32[]{:S(2)}) collective-permute-start(bf16[2,32,384]{2,1,0:T(8,128)(2,1)S(1)} %get-tuple-element.113), channel_id=1, source_target_pairs={{0,96},{32,0},{64,32},{96,64},{1,97},{33,1},{65,33},{97,65},{2,98}... | collective-permute-start | bytes 147464 | tf_op jit(solution)/shard_map/ppermute | solution.py:40
  201.0 6.7 %collective-permute-done.25.up = bf16[3,24,1536]{2,1,0:T(8,128)(2,1)S(1)} collective-permute-done((bf16[3,24,1536]{2,1,0:T(8,128)(2,1)S(1)}, bf16[3,24,1536]{2,1,0:T(8,128)(2,1)S(1)}, u32[]{:S(2)}, u32[]{:S(2)}) %collective-permute-start.25) | collective-permute-done | bytes 221216 | tf_op jit(solution)/shard_map/ppermute | solution.py:74
  207.7 5.6 %convolution.1 = bf16[8,16,1536]{2,1,0:T(8,128)(2,1)} custom-call(bf16[8,16,1536]{2,1,0:T(8,128)(2,1)S(1)} %get-tuple-element.96.own, bf16[8,3,1536]{2,1,0:T(4,128)(2,1)S(1)} %collective-permute-done.23.left, bf16[8,3,1536]{2,1,0:T(4,128)(2,1)S(1)} %collective-permute-done.24.right, bf16[3,24,1536]{2,1,0:T(8,128)(2,1)S(1)} %collective-permute-done.25.up, ...), custom_call_target="tpu_custom_call" | custom-call | tf_op jit(solution)/shard_map/convolution/pallas_call | solution.py:186
  (134 shorter events, 51.1 us)
Async XLA Ops:
  3.6 33.3 %all-to-all-start = ((bf16[8,144,384]{2,1,0:T(8,128)(2,1)}), bf16[8,144,384]{2,1,0:T(8,128)(2,1)S(1)}, u32[]{:S(2)}, u32[]{:S(2)}) async-start(bf16[8,144,384]{2,1,0:T(8,128)(2,1)} %broadcast_in_dim.10), calls=%async_computation | async-start | bytes 1769472 | tf_op jit(solution)/shard_map/all_to_all | solution.py:44
  13.5 19.0 %collective-permute-start.3 = (bf16[256,1536]{1,0:T(8,128)(2,1)S(1)}, bf16[256,1536]{1,0:T(8,128)(2,1)S(1)}, u32[]{:S(2)}, u32[]{:S(2)}) collective-permute-start(bf16[256,1536]{1,0:T(8,128)(2,1)S(1)} %get-tuple-element.60.refs_0_), channel_id=1, source_target_pairs={{0,12},{4,0},{8,4},{12,8},{1,13},{5,1},{9,5},{13,9},{2,14},{6,2},{... | collective-permute-start | bytes 2359304 | tf_op jit(solution)/shard_map/ppermute | solution.py:36
  16.3 19.7 %collective-permute-start.4 = (bf16[256,1536]{1,0:T(8,128)(2,1)S(1)}, bf16[256,1536]{1,0:T(8,128)(2,1)S(1)}, u32[]{:S(2)}, u32[]{:S(2)}) collective-permute-start(bf16[256,1536]{1,0:T(8,128)(2,1)S(1)} %get-tuple-element.60.refs_0_), channel_id=1, source_target_pairs={{0,4},{4,8},{8,12},{12,0},{1,5},{5,9},{9,13},{13,1},{2,6},{6,10},{... | collective-permute-start | bytes 2359304 | tf_op jit(solution)/shard_map/ppermute | solution.py:36
  38.3 55.0 %all-to-all-start.1 = ((bf16[8,4,2,32,384]{4,3,2,1,0:T(8,128)(2,1)}), bf16[8,4,2,32,384]{4,3,2,1,0:T(8,128)(2,1)S(1)}, u32[]{:S(2)}, u32[]{:S(2)}) async-start(bf16[8,4,2,32,384]{4,3,2,1,0:T(8,128)(2,1)} %broadcast_in_dim.11), calls=%async_computation.1 | async-start | bytes 3145728 | tf_op jit(solution)/shard_map/all_to_all | solution.py:44
  46.7 34.4 %collective-permute-start.8 = (bf16[8,2,64,384]{3,2,1,0:T(8,128)(2,1)S(1)}, bf16[8,2,64,384]{3,2,1,0:T(8,128)(2,1)}, u32[]{:S(2)}, u32[]{:S(2)}) collective-permute-start(bf16[8,2,64,384]{3,2,1,0:T(8,128)(2,1)S(1)} %bitcast.19), channel_id=1, source_target_pairs={{0,96},{32,0},{64,32},{96,64},{1,97},{33,1},{65,33},{97,65},{2,98}... | collective-permute-start | bytes 2359304 | tf_op jit(solution)/shard_map/ppermute | solution.py:40
  49.8 34.8 %collective-permute-start.10 = (bf16[8,2,64,384]{3,2,1,0:T(8,128)(2,1)S(1)}, bf16[8,2,64,384]{3,2,1,0:T(8,128)(2,1)}, u32[]{:S(2)}, u32[]{:S(2)}) collective-permute-start(bf16[8,2,64,384]{3,2,1,0:T(8,128)(2,1)S(1)} %bitcast.20), channel_id=1, source_target_pairs={{0,32},{32,64},{64,96},{96,0},{1,33},{33,65},{65,97},{97,1},{2,34}... | collective-permute-start | bytes 2359304 | tf_op jit(solution)/shard_map/ppermute | solution.py:40
  49.8 34.9 %collective-permute-start.5 = (bf16[256,1536]{1,0:T(8,128)(2,1)S(1)}, bf16[256,1536]{1,0:T(8,128)(2,1)}, u32[]{:S(2)}, u32[]{:S(2)}) collective-permute-start(bf16[256,1536]{1,0:T(8,128)(2,1)S(1)} %get-tuple-element.60.refs_0_), channel_id=1, source_target_pairs={{0,8},{4,12},{8,0},{12,4},{1,9},{5,13},{9,1},{13,5},{2,10},{6,14},... | collective-permute-start | bytes 2359304 | tf_op jit(solution)/shard_map/ppermute | solution.py:36
  50.1 34.7 %collective-permute-start.6 = (bf16[8,2,64,384]{3,2,1,0:T(8,128)(2,1)S(1)}, bf16[8,2,64,384]{3,2,1,0:T(8,128)(2,1)}, u32[]{:S(2)}, u32[]{:S(2)}) collective-permute-start(bf16[8,2,64,384]{3,2,1,0:T(8,128)(2,1)S(1)} %bitcast.21), channel_id=1, source_target_pairs={{0,64},{32,96},{64,0},{96,32},{1,65},{33,97},{65,1},{97,33},{2,66}... | collective-permute-start | bytes 2359304 | tf_op jit(solution)/shard_map/ppermute | solution.py:40
  81.2 12.1 %collective-permute-start.9 = (bf16[8,2,64,384]{3,2,1,0:T(8,128)(2,1)}, bf16[8,2,64,384]{3,2,1,0:T(8,128)(2,1)}, u32[]{:S(2)}, u32[]{:S(2)}) collective-permute-start(bf16[8,2,64,384]{3,2,1,0:T(8,128)(2,1)} %collective-permute-done.8.refs_5_), channel_id=1, source_target_pairs={{0,16},{16,0},{1,17},{17,1},{2,18},{18,2},{3,19},{19,3},{4,20},{20... | collective-permute-start | bytes 2359304 | tf_op jit(solution)/shard_map/ppermute | solution.py:61
  84.7 8.6 %collective-permute-start.11 = (bf16[8,2,64,384]{3,2,1,0:T(8,128)(2,1)}, bf16[8,2,64,384]{3,2,1,0:T(8,128)(2,1)}, u32[]{:S(2)}, u32[]{:S(2)}) collective-permute-start(bf16[8,2,64,384]{3,2,1,0:T(8,128)(2,1)} %collective-permute-done.10.refs_7_), channel_id=1, source_target_pairs={{0,16},{16,0},{1,17},{17,1},{2,18},{18,2},{3,19},{19,3},{4,20},{20... | collective-permute-start | bytes 2359304 | tf_op jit(solution)/shard_map/ppermute | solution.py:61
  111.2 8.4 %collective-permute-start.15 = (bf16[512,1536]{1,0:T(8,128)(2,1)S(1)}, bf16[512,1536]{1,0:T(8,128)(2,1)S(1)}, u32[]{:S(2)}, u32[]{:S(2)}) collective-permute-start(bf16[512,1536]{1,0:T(8,128)(2,1)S(1)} %get-tuple-element.75.refs_2_), channel_id=1, source_target_pairs={{0,16},{16,0},{1,17},{17,1},{2,18},{18,2},{3,19},{19,3},{4,20},{20... | collective-permute-start | bytes 4718600 | tf_op jit(solution)/shard_map/ppermute | solution.py:61
  132.3 49.4 %all-to-all-start.2 = ((bf16[8,4,2,32,384]{4,3,2,1,0:T(8,128)(2,1)}), bf16[8,4,2,32,384]{4,3,2,1,0:T(8,128)(2,1)S(1)}, u32[]{:S(2)}, u32[]{:S(2)}) async-start(bf16[8,4,2,32,384]{4,3,2,1,0:T(8,128)(2,1)} %get-tuple-element.99), calls=%async_computation.2 | async-start | bytes 3145728 | tf_op jit(solution)/shard_map/all_to_all | solution.py:44
  139.6 20.4 %collective-permute-start.20 = (bf16[128,1536]{1,0:T(8,128)(2,1)}, bf16[128,1536]{1,0:T(8,128)(2,1)S(1)}, u32[]{:S(2)}, u32[]{:S(2)}) collective-permute-start(bf16[128,1536]{1,0:T(8,128)(2,1)} %copy-done.21), channel_id=1, source_target_pairs={{0,4},{4,8},{8,12},{12,0},{1,5},{5,9},{9,13},{13,1},{2,6},{6,10},{... | collective-permute-start | bytes 1179656 | tf_op jit(solution)/shard_map/ppermute | solution.py:36
  139.6 37.4 %collective-permute-start.17 = (bf16[8,2,64,384]{3,2,1,0:T(8,128)(2,1)}, bf16[8,2,64,384]{3,2,1,0:T(8,128)(2,1)S(1)}, u32[]{:S(2)}, u32[]{:S(2)}) collective-permute-start(bf16[8,2,64,384]{3,2,1,0:T(8,128)(2,1)} %copy-done.19), channel_id=1, source_target_pairs={{0,32},{32,64},{64,96},{96,0},{1,33},{33,65},{65,97},{97,1},{2,34}... | collective-permute-start | bytes 2359304 | tf_op jit(solution)/shard_map/ppermute | solution.py:40
  139.7 37.3 %collective-permute-start.18 = (bf16[8,2,64,384]{3,2,1,0:T(8,128)(2,1)}, bf16[8,2,64,384]{3,2,1,0:T(8,128)(2,1)S(1)}, u32[]{:S(2)}, u32[]{:S(2)}) collective-permute-start(bf16[8,2,64,384]{3,2,1,0:T(8,128)(2,1)} %copy-done.18), channel_id=1, source_target_pairs={{0,64},{32,96},{64,0},{96,32},{1,65},{33,97},{65,1},{97,33},{2,66}... | collective-permute-start | bytes 2359304 | tf_op jit(solution)/shard_map/ppermute | solution.py:40
  141.6 36.0 %collective-permute-start.19 = (bf16[8,2,64,384]{3,2,1,0:T(8,128)(2,1)}, bf16[8,2,64,384]{3,2,1,0:T(8,128)(2,1)S(1)}, u32[]{:S(2)}, u32[]{:S(2)}) collective-permute-start(bf16[8,2,64,384]{3,2,1,0:T(8,128)(2,1)} %copy-done.17), channel_id=1, source_target_pairs={{0,96},{32,0},{64,32},{96,64},{1,97},{33,1},{65,33},{97,65},{2,98}... | collective-permute-start | bytes 2359304 | tf_op jit(solution)/shard_map/ppermute | solution.py:40
  143.0 17.1 %collective-permute-start.21 = (bf16[128,1536]{1,0:T(8,128)(2,1)}, bf16[128,1536]{1,0:T(8,128)(2,1)S(1)}, u32[]{:S(2)}, u32[]{:S(2)}) collective-permute-start(bf16[128,1536]{1,0:T(8,128)(2,1)} %copy-done.20), channel_id=1, source_target_pairs={{0,8},{4,12},{8,0},{12,4},{1,9},{5,13},{9,1},{13,5},{2,10},{6,14},... | collective-permute-start | bytes 1179656 | tf_op jit(solution)/shard_map/ppermute | solution.py:36
  169.2 9.7 %collective-permute-start.23 = (bf16[8,3,1536]{2,1,0:T(4,128)(2,1)S(1)}, bf16[8,3,1536]{2,1,0:T(4,128)(2,1)S(1)}, u32[]{:S(2)}, u32[]{:S(2)}) collective-permute-start(bf16[8,3,1536]{2,1,0:T(4,128)(2,1)S(1)} %get-tuple-element.94), channel_id=1, source_target_pairs={{0,1},{1,2},{2,3},{3,4},{4,5},{5,6},{6,7},{7,8},{8,9},{9,10},{10,1... | collective-permute-start | bytes 221192 | tf_op jit(solution)/shard_map/ppermute | solution.py:74
  181.7 31.6 %all-to-all-start.3 = ((bf16[8,2,64,384]{3,2,1,0:T(8,128)(2,1)}), bf16[8,2,64,384]{3,2,1,0:T(8,128)(2,1)S(1)}, u32[]{:S(2)}, u32[]{:S(2)}) async-start(bf16[8,2,64,384]{3,2,1,0:T(8,128)(2,1)} %sum_y.1), calls=%async_computation.3 | async-start | bytes 1572864 | tf_op jit(solution)/shard_map/all_to_all | solution.py:44
  189.0 18.7 %collective-permute-start.25 = (bf16[3,24,1536]{2,1,0:T(8,128)(2,1)S(1)}, bf16[3,24,1536]{2,1,0:T(8,128)(2,1)S(1)}, u32[]{:S(2)}, u32[]{:S(2)}) collective-permute-start(bf16[3,24,1536]{2,1,0:T(8,128)(2,1)S(1)} %get-tuple-element.106), channel_id=1, source_target_pairs={{0,16},{1,17},{2,18},{3,19},{4,20},{5,21},{6,22},{7,23},{8,24},{9,... | collective-permute-start | bytes 663560 | tf_op jit(solution)/shard_map/ppermute | solution.py:74
  190.9 16.8 %collective-permute-start.26 = (bf16[3,24,1536]{2,1,0:T(8,128)(2,1)S(1)}, bf16[3,24,1536]{2,1,0:T(8,128)(2,1)S(1)}, u32[]{:S(2)}, u32[]{:S(2)}) collective-permute-start(bf16[3,24,1536]{2,1,0:T(8,128)(2,1)S(1)} %get-tuple-element.107), channel_id=1, source_target_pairs={{16,0},{17,1},{18,2},{19,3},{20,4},{21,5},{22,6},{23,7},{24,8},{25... | collective-permute-start | bytes 663560 | tf_op jit(solution)/shard_map/ppermute | solution.py:74
  196.6 16.6 %collective-permute-start.27 = (bf16[2,32,384]{2,1,0:T(8,128)(2,1)S(1)}, bf16[2,32,384]{2,1,0:T(8,128)(2,1)S(1)}, u32[]{:S(2)}, u32[]{:S(2)}) collective-permute-start(bf16[2,32,384]{2,1,0:T(8,128)(2,1)S(1)} %get-tuple-element.111), channel_id=1, source_target_pairs={{0,32},{32,64},{64,96},{96,0},{1,33},{33,65},{65,97},{97,1},{2,34}... | collective-permute-start | bytes 147464 | tf_op jit(solution)/shard_map/ppermute | solution.py:40
  196.7 16.6 %collective-permute-start.28 = (bf16[2,32,384]{2,1,0:T(8,128)(2,1)S(1)}, bf16[2,32,384]{2,1,0:T(8,128)(2,1)S(1)}, u32[]{:S(2)}, u32[]{:S(2)}) collective-permute-start(bf16[2,32,384]{2,1,0:T(8,128)(2,1)S(1)} %get-tuple-element.112), channel_id=1, source_target_pairs={{0,64},{32,96},{64,0},{96,32},{1,65},{33,97},{65,1},{97,33},{2,66}... | collective-permute-start | bytes 147464 | tf_op jit(solution)/shard_map/ppermute | solution.py:40
  196.8 16.5 %collective-permute-start.29 = (bf16[2,32,384]{2,1,0:T(8,128)(2,1)S(1)}, bf16[2,32,384]{2,1,0:T(8,128)(2,1)S(1)}, u32[]{:S(2)}, u32[]{:S(2)}) collective-permute-start(bf16[2,32,384]{2,1,0:T(8,128)(2,1)S(1)} %get-tuple-element.113), channel_id=1, source_target_pairs={{0,96},{32,0},{64,32},{96,64},{1,97},{33,1},{65,33},{97,65},{2,98}... | collective-permute-start | bytes 147464 | tf_op jit(solution)/shard_map/ppermute | solution.py:40
  (39 other events, 272.1 us)

commit v4 on v3

--- a/solution.py
+++ b/solution.py
@@ -1,3 +1,4 @@
+import functools
 import math
 
 import jax
@@ -313,16 +314,18 @@
     )(pre_grad, w_in)
 
 
-def weight_kernel(where, mine, got, *refs):
-    sides, (ys, out_z, g) = (refs[0:2], refs[2:4]), (refs[4 : 4 + NY], *refs[4 + NY :])
+def weight_kernel(y_first, where, mine, got, *refs):
+    sides, outs, g = (refs[0:2], refs[2:4]), refs[4:-1], refs[-1]
+    rows = slice(PLANES * AY, CHAN // 2) if y_first else slice(0, PLANES * AY)
+    height = BY if y_first else AY
     width = 256
     for m in range(2):
         own, other = sides[m]
 
         def step(i, _, m=m, own=own, other=other):
             cols = pl.ds(pl.multiple_of(i * width, width), width)
-            value = jnp.dot(mine[m], own[:, cols], preferred_element_type=f32)
-            value = value + jnp.dot(got[m], other[:, cols], preferred_element_type=f32)
+            value = jnp.dot(mine[m, rows], own[:, cols], preferred_element_type=f32)
+            value = value + jnp.dot(got[m, rows], other[:, cols], preferred_element_type=f32)
             g[:, cols] = value.astype(bf16)
             return 0
 
@@ -331,28 +334,31 @@
             col = slice(k % 4 * COLS, k % 4 * COLS + COLS)
             for r in range(NY):
                 j = k // 4 * NY + lax.rem(where[0] + r, NY)
-                row = pl.multiple_of(j * AY, 32)
-                row2 = pl.multiple_of(PLANES * AY + j * BY, 32)
-                out_z[k, r, m] = g[pl.ds(row, AY), col]
-                ys[r][k, m] = g[pl.ds(row2, BY), col]
-
-
-def weight_gradients(where, mine, got, pre_grad, other_pre_grad, act, other_act):
-    operands = [mine, got, pre_grad, other_pre_grad, act, other_act]
-    out = pl.pallas_call(
-        weight_kernel,
-        out_shape=[jax.ShapeDtypeStruct((NZ, 2, BY, COLS), bf16)] * NY
-        + [jax.ShapeDtypeStruct((NZ, NY, 2, AY, COLS), bf16)],
+                piece = g[pl.ds(pl.multiple_of(j * height, 32), height), col]
+                if y_first:
+                    outs[r][k, m] = piece
+                else:
+                    outs[0][k, r, m] = piece
+
+
+def weight_gradients(y_first, where, *operands):
+    if y_first:
+        outs = [jax.ShapeDtypeStruct((NZ, 2, BY, COLS), bf16)] * NY
+    else:
+        outs = [jax.ShapeDtypeStruct((NZ, NY, 2, AY, COLS), bf16)]
+    height = PLANES * (BY if y_first else AY)
+    return pl.pallas_call(
+        functools.partial(weight_kernel, y_first),
+        out_shape=outs,
         in_specs=[pl.BlockSpec(memory_space=pltpu.SMEM)] + vmem_specs(len(operands)),
-        out_specs=vmem_specs(NY + 1),
-        scratch_shapes=[pltpu.VMEM((CHAN // 2, HIDDEN), bf16)],
-        compiler_params=pltpu.CompilerParams(vmem_limit_bytes=32 * 2**20),
+        out_specs=vmem_specs(len(outs)),
+        scratch_shapes=[pltpu.VMEM((height, HIDDEN), bf16)],
+        compiler_params=pltpu.CompilerParams(vmem_limit_bytes=28 * 2**20),
         cost_estimate=pl.CostEstimate(
-            flops=4 * TOKENS * CHAN * HIDDEN, bytes_accessed=30_000_000, transcendentals=0
+            flops=8 * TOKENS * height * HIDDEN, bytes_accessed=20_000_000, transcendentals=0
         ),
         name="weight_gradients",
     )(where, *operands)
-    return out[:NY], out[NY]
 
 
 def sum_y_kernel(*refs):
@@ -435,11 +441,13 @@
     token, xhat, inverse = layer_norm(
         conv_out.reshape(BLOCK, CHAN), out_grad.reshape(BLOCK, CHAN), gain, shift_row, scale
     )
-    tok = [to_x(token, -r) for r in range(NX)]
 
     shards = jnp.stack([w_in, w_out.T])
     lead, rest = shards[:, :AY], shards[:, AY:]
-    got = gather_z(jnp.concatenate([rest.reshape(2 * BY, COLS), bias_rows(b_in)]))
+    load = jnp.concatenate([rest.reshape(2 * BY, COLS), bias_rows(b_in)])
+    load, token = lax.optimization_barrier((load, token))
+    tok = [to_x(token, -r) for r in range(NX)]
+    got = gather_z(load)
     lead_y = jnp.stack([to_y(lead, -r) for r in range(NY)])
     got, lead_y, tok[1], tok[3] = lax.optimization_barrier((got, lead_y, tok[1], tok[3]))
     rest_z = got[:, : 2 * BY].reshape(NZ, 2, BY, COLS)
@@ -448,11 +456,10 @@
     first = gather_z(lead_y)
     swapped = [swap(v) for v in second[:2]] + [None, swap(second[3])]
     where = jnp.stack([lax.axis_index("y"), lax.axis_index("c")]).astype(jnp.int32)
-    tok[2], second[2] = lax.optimization_barrier((tok[2], second[2]))
+    first, swapped[1], swapped[3], second[2], tok[2] = lax.optimization_barrier(
+        (first, swapped[1], swapped[3], second[2], tok[2])
+    )
     xs, mine, other = tokens(where, tok)
-    first, swapped[1], swapped[3], xs = lax.optimization_barrier(
-        (first, swapped[1], swapped[3], xs)
-    )
     other = swap(other)
     swapped[2] = swap(second[2])
     second = [second, swapped]
@@ -465,7 +472,10 @@
         (other_act, other_pre_grad, *part)
     )
     part = [to_x(v, r) for r, v in enumerate(part)]
-    ys, zs = weight_gradients(where, mine, other, pre_grad, other_pre_grad, act, other_act)
+    operands = [mine, other, pre_grad, other_pre_grad, act, other_act]
+    zs = weight_gradients(False, where, *operands)[0]
+    *operands, zs = lax.optimization_barrier((*operands, zs))
+    ys = weight_gradients(True, where, *operands)
     ys = [to_y(v, r) for r, v in enumerate(ys)]
     own, first_cols, last_cols = layer_norm_backward(part, xhat, inverse, gain)
     left, right = to_tile(last_cols, 0, 1), to_tile(first_cols, 0, -1)

time: 216 us -> 228 us (1.056)
  local copies, waits for them, and re-layouts: 23.1 us -> 39 us
  waiting for transfers between devices: 83.7 us -> 78.1 us
    unnamed x60 -> x86, local copies, waits for them, and re-layouts: 18.1 us -> 32.3 us
    ppermute x6, waiting for transfers between devices: 32.1 us -> 26.3 us  [to_x(): return lax.ppermute(value, 'x', shift(NX, k)) if k else value]
    ppermute x12, waiting for transfers between devices: 37.9 us -> 42.4 us  [to_y(): return lax.ppermute(value, 'y', shift(NY, k)) if k else value]
    ppermute x8, waiting for transfers between devices: 4.22 us -> 0.02 us  [swap(): return lax.ppermute(value, 'c', shift(2, 1))]
    pallas_call x1 -> x2, Pallas kernels: 9.1 us -> 11.7 us  [weight_gradients(): pl.pallas_call(functools.partial(weight_kernel, y_first), out_shape=outs,...]
  transfers between devices with their start and end apart: 34 -> 34, of which waited for: 14 -> 12; matrix products, arithmetic and copies ran while one was open for 1% -> 1% of each run, Pallas kernels for 7% -> 8%
where the time goes in v4:
time: 228 us; the launch traced here: 227 us
  waiting for transfers between devices  78.1 us (34%)
  starting transfers between devices  69.4 us (30%)
  local copies, waits for them, and re-layouts  39 us (17%)
  Pallas kernels  37.8 us (17%)
    ppermute x12, waiting for transfers between devices, to_y(): return lax.ppermute(value, 'y', shift(NY, k)) if k else value  42.4 us
    unnamed x86, local copies, waits for them, and re-layouts  32.3 us
    all_to_all x4, starting transfers between devices, exchange_z(): return lax.all_to_all(value, Z, 0, 0, tiled=True)  30 us
    ppermute x6, waiting for transfers between devices, to_x(): return lax.ppermute(value, 'x', shift(NX, k)) if k else value  26.3 us
    ppermute x12, starting transfers between devices, to_y(): return lax.ppermute(value, 'y', shift(NY, k)) if k else value  17.7 us
    ppermute x4, starting transfers between devices, to_tile(): return lax.ppermute(value, FINE, pairs)  13.2 us
    pallas_call x1, Pallas kernels, activations(): pl.pallas_call(activation_kernel, out_shape=[out, out, jax.ShapeDtypeStru...  11.9 us
    pallas_call x2, Pallas kernels, weight_gradients(): pl.pallas_call(functools.partial(weight_kernel, y_first), out_shape=outs,...  11.7 us
  transfers between devices with their start and end apart: 34, of which 12 were waited for; matrix products, arithmetic and copies ran while one was open for 1% of the time, Pallas kernels for 8%

profile of v4, /device:TPU:32, one launch (start us, length us, event | category | flops | bytes accessed | tf_op | source)
XLA Modules:
  0.0 227.0 jit_solution(10967028175381220625)
XLA Ops:
  9.5 8.6 %all-to-all-start = ((bf16[8,144,384]{2,1,0:T(8,128)(2,1)}), bf16[8,144,384]{2,1,0:T(8,128)(2,1)S(1)}, u32[]{:S(2)}, u32[]{:S(2)}) async-start(bf16[8,144,384]{2,1,0:T(8,128)(2,1)} %broadcast_in_dim.10), calls=%async_computation | async-start | bytes 1769472 | tf_op jit(solution)/shard_map/all_to_all | solution.py:45
  18.0 2.8 %collective-permute-start.3 = (bf16[256,1536]{1,0:T(8,128)(2,1)S(1)}, bf16[256,1536]{1,0:T(8,128)(2,1)S(1)}, u32[]{:S(2)}, u32[]{:S(2)}) collective-permute-start(bf16[256,1536]{1,0:T(8,128)(2,1)S(1)} %get-tuple-element.68.refs_0_), channel_id=1, source_target_pairs={{0,12},{4,0},{8,4},{12,8},{1,13},{5,1},{9,5},{13,9},{2,14},{6,2},{... | collective-permute-start | bytes 2359304 | tf_op jit(solution)/shard_map/ppermute | solution.py:37
  22.5 2.9 %collective-permute-start.1 = (bf16[2,32,384]{2,1,0:T(8,128)(2,1)S(1)}, bf16[2,32,384]{2,1,0:T(8,128)(2,1)S(1)}, u32[]{:S(2)}, u32[]{:S(2)}) collective-permute-start(bf16[2,32,384]{2,1,0:T(8,128)(2,1)S(1)} %pad_maximum_fusion.1), channel_id=1, source_target_pairs={{0,64},{32,96},{64,0},{96,32},{1,65},{33,97},{65,1},{97,33},{2,66}... | collective-permute-start | bytes 147464 | tf_op jit(solution)/shard_map/ppermute | solution.py:41
  29.5 7.5 %collective-permute-done.3.refs_1_ = bf16[256,1536]{1,0:T(8,128)(2,1)S(1)} collective-permute-done((bf16[256,1536]{1,0:T(8,128)(2,1)S(1)}, bf16[256,1536]{1,0:T(8,128)(2,1)S(1)}, u32[]{:S(2)}, u32[]{:S(2)}) %collective-permute-start.3) | collective-permute-done | bytes 786464 | tf_op jit(solution)/shard_map/ppermute | solution.py:37
  37.9 2.5 %collective-permute-done.4.refs_3_ = bf16[256,1536]{1,0:T(8,128)(2,1)S(1)} collective-permute-done((bf16[256,1536]{1,0:T(8,128)(2,1)S(1)}, bf16[256,1536]{1,0:T(8,128)(2,1)S(1)}, u32[]{:S(2)}, u32[]{:S(2)}) %collective-permute-start.4) | collective-permute-done | bytes 786464 | tf_op jit(solution)/shard_map/ppermute | solution.py:37
  42.9 7.0 %all-to-all-start.1 = ((bf16[8,4,2,32,384]{4,3,2,1,0:T(8,128)(2,1)}), bf16[8,4,2,32,384]{4,3,2,1,0:T(8,128)(2,1)S(1)}, u32[]{:S(2)}, u32[]{:S(2)}) async-start(bf16[8,4,2,32,384]{4,3,2,1,0:T(8,128)(2,1)} %broadcast_in_dim.11), calls=%async_computation.1 | async-start | bytes 3145728 | tf_op jit(solution)/shard_map/all_to_all | solution.py:45
  50.9 3.0 %collective-permute-start.5 = (bf16[8,2,64,384]{3,2,1,0:T(8,128)(2,1)}, bf16[8,2,64,384]{3,2,1,0:T(8,128)(2,1)S(1)}, u32[]{:S(2)}, u32[]{:S(2)}) collective-permute-start(bf16[8,2,64,384]{3,2,1,0:T(8,128)(2,1)} %bitcast.12.refs_4_), channel_id=1, source_target_pairs={{0,96},{32,0},{64,32},{96,64},{1,97},{33,1},{65,33},{97,65},{2,98}... | collective-permute-start | bytes 2359304 | tf_op jit(solution)/shard_map/ppermute | solution.py:41
  56.3 29.2 %collective-permute-done.5.refs_5_ = bf16[8,2,64,384]{3,2,1,0:T(8,128)(2,1)S(1)} collective-permute-done((bf16[8,2,64,384]{3,2,1,0:T(8,128)(2,1)}, bf16[8,2,64,384]{3,2,1,0:T(8,128)(2,1)S(1)}, u32[]{:S(2)}, u32[]{:S(2)}) %collective-permute-start.5) | collective-permute-done | bytes 786464 | tf_op jit(solution)/shard_map/ppermute | solution.py:41
  101.5 11.9 %activations.1 = (bf16[512,1536]{1,0:T(8,128)(2,1)S(1)}, bf16[512,1536]{1,0:T(8,128)(2,1)S(1)}, bf16[1536,1536]{1,0:T(8,128)(2,1)}) custom-call(s32[2]{0:T(128)S(1)} %pad_add_fusion.where, f32[1,1536]{1,0:T(1,128)S(1)} %bitcast.20, bf16[2,512,1536]{2,1,0:T(8,128)(2,1)} %copy-done.25, bf16[8,4,2,32,384]{4,3,2,1,0:T(8,128)(2,1)S(1)} %all-to-all-done.1.refs_2_, ...), custom_call_target="tpu_custom_call" | custom-call | flops 4831838208 | bytes 25000000 | tf_op jit(solution)/shard_map/activations/pallas_call | solution.py:274
  114.0 2.8 %copy-done.39 = bf16[1536,1536]{1,0:T(8,128)(2,1)S(1)} copy-done((bf16[1536,1536]{1,0:T(8,128)(2,1)S(1)}, bf16[1536,1536]{1,0:T(8,128)(2,1)}, u32[]{:S(2)}) %copy-start.39) | copy-done | bytes 4718616
  116.8 3.6 %normed_gradient.1 = (bf16[128,1536]{1,0:T(8,128)(2,1)S(1)}, bf16[128,1536]{1,0:T(8,128)(2,1)S(1)}, bf16[128,1536]{1,0:T(8,128)(2,1)S(1)}, bf16[128,1536]{1,0:T(8,128)(2,1)S(1)}) custom-call(bf16[512,1536]{1,0:T(8,128)(2,1)S(1)} %get-tuple-element.93.pre_grad.refs_0_, bf16[1536,1536]{1,0:T(8,128)(2,1)S(1)} %copy-done.39), custom_call_target="tpu_custom_call" | custom-call | flops 2415919104 | bytes 20000000 | tf_op jit(solution)/shard_map/normed_gradient/pallas_call | solution.py:304
  122.7 5.5 %weight_gradients.2 = bf16[8,4,2,32,384]{4,3,2,1,0:T(8,128)(2,1)} custom-call(s32[2]{0:T(128)S(1)} %pad_add_fusion.where, bf16[2,768,512]{2,1,0:T(8,128)(2,1)S(1)} %get-tuple-element.91.mine, bf16[2,768,512]{2,1,0:T(8,128)(2,1)S(1)} %collective-permute-done.11.got, bf16[512,1536]{1,0:T(8,128)(2,1)S(1)} %get-tuple-element.93.pre_grad.refs_0_, ...), custom_call_target="tpu_custom_call" | custom-call | flops 1610612736 | bytes 20000000 | tf_op jit(solution)/shard_map/weight_gradients/pallas_call | solution.py:350
  131.7 7.2 %all-to-all-start.2 = ((bf16[8,4,2,32,384]{4,3,2,1,0:T(8,128)(2,1)}), bf16[8,4,2,32,384]{4,3,2,1,0:T(8,128)(2,1)S(1)}, u32[]{:S(2)}, u32[]{:S(2)}) async-start(bf16[8,4,2,32,384]{4,3,2,1,0:T(8,128)(2,1)} %weight_gradients.2), calls=%async_computation.2 | async-start | bytes 3145728 | tf_op jit(solution)/shard_map/all_to_all | solution.py:45
  145.9 6.1 %weight_gradients.3 = (bf16[8,2,64,384]{3,2,1,0:T(8,128)(2,1)S(1)}, bf16[8,2,64,384]{3,2,1,0:T(8,128)(2,1)S(1)}, bf16[8,2,64,384]{3,2,1,0:T(8,128)(2,1)S(1)}, bf16[8,2,64,384]{3,2,1,0:T(8,128)(2,1)S(1)}) custom-call(s32[2]{0:T(128)S(1)} %pad_add_fusion.where, bf16[2,768,512]{2,1,0:T(8,128)(2,1)S(1)} %get-tuple-element.91.mine, ...), custom_call_target="tpu_custom_call" | custom-call | flops 3221225472 | bytes 20000000 | tf_op jit(solution)/shard_map/weight_gradients/pallas_call | solution.py:350
  152.2 2.6 %collective-permute-start.18 = (bf16[8,2,64,384]{3,2,1,0:T(8,128)(2,1)S(1)}, bf16[8,2,64,384]{3,2,1,0:T(8,128)(2,1)S(1)}, u32[]{:S(2)}, u32[]{:S(2)}) collective-permute-start(bf16[8,2,64,384]{3,2,1,0:T(8,128)(2,1)S(1)} %get-tuple-element.99), channel_id=1, source_target_pairs={{0,64},{32,96},{64,0},{96,32},{1,65},{33,97},{65,1},{97,33},{2,66}... | collective-permute-start | bytes 2359304 | tf_op jit(solution)/shard_map/ppermute | solution.py:41
  155.4 2.9 %collective-permute-start.21 = (bf16[128,1536]{1,0:T(8,128)(2,1)S(1)}, bf16[128,1536]{1,0:T(8,128)(2,1)S(1)}, u32[]{:S(2)}, u32[]{:S(2)}) collective-permute-start(bf16[128,1536]{1,0:T(8,128)(2,1)S(1)} %copy-done.37), channel_id=1, source_target_pairs={{0,8},{4,12},{8,0},{12,4},{1,9},{5,13},{9,1},{13,5},{2,10},{6,14},... | collective-permute-start | bytes 1179656 | tf_op jit(solution)/shard_map/ppermute | solution.py:37
  159.3 7.5 %collective-permute-done.21.refs_2_ = bf16[128,1536]{1,0:T(8,128)(2,1)S(1)} collective-permute-done((bf16[128,1536]{1,0:T(8,128)(2,1)S(1)}, bf16[128,1536]{1,0:T(8,128)(2,1)S(1)}, u32[]{:S(2)}, u32[]{:S(2)}) %collective-permute-start.21) | collective-permute-done | bytes 393248 | tf_op jit(solution)/shard_map/ppermute | solution.py:37
  166.8 8.7 %collective-permute-done.22.refs_3_ = bf16[128,1536]{1,0:T(8,128)(2,1)S(1)} collective-permute-done((bf16[128,1536]{1,0:T(8,128)(2,1)S(1)}, bf16[128,1536]{1,0:T(8,128)(2,1)S(1)}, u32[]{:S(2)}, u32[]{:S(2)}) %collective-permute-start.22) | collective-permute-done | bytes 393248 | tf_op jit(solution)/shard_map/ppermute | solution.py:37
  176.1 4.3 %collective-permute-start.23 = (bf16[8,3,1536]{2,1,0:T(4,128)(2,1)S(1)}, bf16[8,3,1536]{2,1,0:T(4,128)(2,1)S(1)}, u32[]{:S(2)}, u32[]{:S(2)}) collective-permute-start(bf16[8,3,1536]{2,1,0:T(4,128)(2,1)S(1)} %get-tuple-element.108), channel_id=1, source_target_pairs={{0,1},{1,2},{2,3},{3,4},{4,5},{5,6},{6,7},{7,8},{8,9},{9,10},{10,1... | collective-permute-start | bytes 221192 | tf_op jit(solution)/shard_map/ppermute | solution.py:75
  181.7 7.4 %collective-permute-done.18.refs_2_ = bf16[8,2,64,384]{3,2,1,0:T(8,128)(2,1)S(1)} collective-permute-done((bf16[8,2,64,384]{3,2,1,0:T(8,128)(2,1)S(1)}, bf16[8,2,64,384]{3,2,1,0:T(8,128)(2,1)S(1)}, u32[]{:S(2)}, u32[]{:S(2)}) %collective-permute-start.18) | collective-permute-done | bytes 786464 | tf_op jit(solution)/shard_map/ppermute | solution.py:41
  191.0 7.2 %all-to-all-start.3 = ((bf16[8,2,64,384]{3,2,1,0:T(8,128)(2,1)}), bf16[8,2,64,384]{3,2,1,0:T(8,128)(2,1)S(1)}, u32[]{:S(2)}, u32[]{:S(2)}) async-start(bf16[8,2,64,384]{3,2,1,0:T(8,128)(2,1)} %sum_y.1), calls=%async_computation.3 | async-start | bytes 1572864 | tf_op jit(solution)/shard_map/all_to_all | solution.py:45
  200.5 5.8 %collective-permute-start.26 = (bf16[3,24,1536]{2,1,0:T(8,128)(2,1)S(1)}, bf16[3,24,1536]{2,1,0:T(8,128)(2,1)S(1)}, u32[]{:S(2)}, u32[]{:S(2)}) collective-permute-start(bf16[3,24,1536]{2,1,0:T(8,128)(2,1)S(1)} %get-tuple-element.121), channel_id=1, source_target_pairs={{16,0},{17,1},{18,2},{19,3},{20,4},{21,5},{22,6},{23,7},{24,8},{25... | collective-permute-start | bytes 663560 | tf_op jit(solution)/shard_map/ppermute | solution.py:75
  210.6 9.1 %collective-permute-done.25.up = bf16[3,24,1536]{2,1,0:T(8,128)(2,1)S(1)} collective-permute-done((bf16[3,24,1536]{2,1,0:T(8,128)(2,1)S(1)}, bf16[3,24,1536]{2,1,0:T(8,128)(2,1)S(1)}, u32[]{:S(2)}, u32[]{:S(2)}) %collective-permute-start.25) | collective-permute-done | bytes 221216 | tf_op jit(solution)/shard_map/ppermute | solution.py:75
  219.7 5.6 %convolution.1 = bf16[8,16,1536]{2,1,0:T(8,128)(2,1)} custom-call(bf16[8,16,1536]{2,1,0:T(8,128)(2,1)S(1)} %get-tuple-element.110.own, bf16[8,3,1536]{2,1,0:T(4,128)(2,1)S(1)} %collective-permute-done.23.left, bf16[8,3,1536]{2,1,0:T(4,128)(2,1)S(1)} %collective-permute-done.24.right, bf16[3,24,1536]{2,1,0:T(8,128)(2,1)S(1)} %collective-permute-done.25.up, ...), custom_call_target="tpu_custom_call" | custom-call | tf_op jit(solution)/shard_map/convolution/pallas_call | solution.py:187
  (161 shorter events, 64.1 us)
Async XLA Ops:
  9.5 32.1 %all-to-all-start = ((bf16[8,144,384]{2,1,0:T(8,128)(2,1)}), bf16[8,144,384]{2,1,0:T(8,128)(2,1)S(1)}, u32[]{:S(2)}, u32[]{:S(2)}) async-start(bf16[8,144,384]{2,1,0:T(8,128)(2,1)} %broadcast_in_dim.10), calls=%async_computation | async-start | bytes 1769472 | tf_op jit(solution)/shard_map/all_to_all | solution.py:45
  18.0 19.0 %collective-permute-start.3 = (bf16[256,1536]{1,0:T(8,128)(2,1)S(1)}, bf16[256,1536]{1,0:T(8,128)(2,1)S(1)}, u32[]{:S(2)}, u32[]{:S(2)}) collective-permute-start(bf16[256,1536]{1,0:T(8,128)(2,1)S(1)} %get-tuple-element.68.refs_0_), channel_id=1, source_target_pairs={{0,12},{4,0},{8,4},{12,8},{1,13},{5,1},{9,5},{13,9},{2,14},{6,2},{... | collective-permute-start | bytes 2359304 | tf_op jit(solution)/shard_map/ppermute | solution.py:37
  20.8 19.7 %collective-permute-start.4 = (bf16[256,1536]{1,0:T(8,128)(2,1)S(1)}, bf16[256,1536]{1,0:T(8,128)(2,1)S(1)}, u32[]{:S(2)}, u32[]{:S(2)}) collective-permute-start(bf16[256,1536]{1,0:T(8,128)(2,1)S(1)} %get-tuple-element.68.refs_0_), channel_id=1, source_target_pairs={{0,4},{4,8},{8,12},{12,0},{1,5},{5,9},{9,13},{13,1},{2,6},{6,10},{... | collective-permute-start | bytes 2359304 | tf_op jit(solution)/shard_map/ppermute | solution.py:37
  42.9 49.5 %all-to-all-start.1 = ((bf16[8,4,2,32,384]{4,3,2,1,0:T(8,128)(2,1)}), bf16[8,4,2,32,384]{4,3,2,1,0:T(8,128)(2,1)S(1)}, u32[]{:S(2)}, u32[]{:S(2)}) async-start(bf16[8,4,2,32,384]{4,3,2,1,0:T(8,128)(2,1)} %broadcast_in_dim.11), calls=%async_computation.1 | async-start | bytes 3145728 | tf_op jit(solution)/shard_map/all_to_all | solution.py:45
  50.9 34.7 %collective-permute-start.5 = (bf16[8,2,64,384]{3,2,1,0:T(8,128)(2,1)}, bf16[8,2,64,384]{3,2,1,0:T(8,128)(2,1)S(1)}, u32[]{:S(2)}, u32[]{:S(2)}) collective-permute-start(bf16[8,2,64,384]{3,2,1,0:T(8,128)(2,1)} %bitcast.12.refs_4_), channel_id=1, source_target_pairs={{0,96},{32,0},{64,32},{96,64},{1,97},{33,1},{65,33},{97,65},{2,98}... | collective-permute-start | bytes 2359304 | tf_op jit(solution)/shard_map/ppermute | solution.py:41
  53.9 34.9 %collective-permute-start.7 = (bf16[8,2,64,384]{3,2,1,0:T(8,128)(2,1)}, bf16[8,2,64,384]{3,2,1,0:T(8,128)(2,1)S(1)}, u32[]{:S(2)}, u32[]{:S(2)}) collective-permute-start(bf16[8,2,64,384]{3,2,1,0:T(8,128)(2,1)} %bitcast.12.refs_4_), channel_id=1, source_target_pairs={{0,32},{32,64},{64,96},{96,0},{1,33},{33,65},{65,97},{97,1},{2,34}... | collective-permute-start | bytes 2359304 | tf_op jit(solution)/shard_map/ppermute | solution.py:41
  53.9 35.8 %collective-permute-start.10 = (bf16[256,1536]{1,0:T(8,128)(2,1)S(1)}, bf16[256,1536]{1,0:T(8,128)(2,1)S(1)}, u32[]{:S(2)}, u32[]{:S(2)}) collective-permute-start(bf16[256,1536]{1,0:T(8,128)(2,1)S(1)} %get-tuple-element.68.refs_0_), channel_id=1, source_target_pairs={{0,8},{4,12},{8,0},{12,4},{1,9},{5,13},{9,1},{13,5},{2,10},{6,14},... | collective-permute-start | bytes 2359304 | tf_op jit(solution)/shard_map/ppermute | solution.py:37
  54.1 36.5 %collective-permute-start.9 = (bf16[8,2,64,384]{3,2,1,0:T(8,128)(2,1)}, bf16[8,2,64,384]{3,2,1,0:T(8,128)(2,1)}, u32[]{:S(2)}, u32[]{:S(2)}) collective-permute-start(bf16[8,2,64,384]{3,2,1,0:T(8,128)(2,1)} %bitcast.12.refs_4_), channel_id=1, source_target_pairs={{0,64},{32,96},{64,0},{96,32},{1,65},{33,97},{65,1},{97,33},{2,66}... | collective-permute-start | bytes 2359304 | tf_op jit(solution)/shard_map/ppermute | solution.py:41
  113.4 9.3 %collective-permute-start.15 = (bf16[512,1536]{1,0:T(8,128)(2,1)S(1)}, bf16[512,1536]{1,0:T(8,128)(2,1)S(1)}, u32[]{:S(2)}, u32[]{:S(2)}) collective-permute-start(bf16[512,1536]{1,0:T(8,128)(2,1)S(1)} %get-tuple-element.95.refs_2_), channel_id=1, source_target_pairs={{0,16},{16,0},{1,17},{17,1},{2,18},{18,2},{3,19},{19,3},{4,20},{20... | collective-permute-start | bytes 4718600 | tf_op jit(solution)/shard_map/ppermute | solution.py:62
  131.7 59.3 %all-to-all-start.2 = ((bf16[8,4,2,32,384]{4,3,2,1,0:T(8,128)(2,1)}), bf16[8,4,2,32,384]{4,3,2,1,0:T(8,128)(2,1)S(1)}, u32[]{:S(2)}, u32[]{:S(2)}) async-start(bf16[8,4,2,32,384]{4,3,2,1,0:T(8,128)(2,1)} %weight_gradients.2), calls=%async_computation.2 | async-start | bytes 3145728 | tf_op jit(solution)/shard_map/all_to_all | solution.py:45
  138.9 19.5 %collective-permute-start.20 = (bf16[128,1536]{1,0:T(8,128)(2,1)}, bf16[128,1536]{1,0:T(8,128)(2,1)S(1)}, u32[]{:S(2)}, u32[]{:S(2)}) collective-permute-start(bf16[128,1536]{1,0:T(8,128)(2,1)} %copy-done.38), channel_id=1, source_target_pairs={{0,4},{4,8},{8,12},{12,0},{1,5},{5,9},{9,13},{13,1},{2,6},{6,10},{... | collective-permute-start | bytes 1179656 | tf_op jit(solution)/shard_map/ppermute | solution.py:37
  152.1 29.6 %collective-permute-start.17 = (bf16[8,2,64,384]{3,2,1,0:T(8,128)(2,1)S(1)}, bf16[8,2,64,384]{3,2,1,0:T(8,128)(2,1)S(1)}, u32[]{:S(2)}, u32[]{:S(2)}) collective-permute-start(bf16[8,2,64,384]{3,2,1,0:T(8,128)(2,1)S(1)} %get-tuple-element.98), channel_id=1, source_target_pairs={{0,32},{32,64},{64,96},{96,0},{1,33},{33,65},{65,97},{97,1},{2,34}... | collective-permute-start | bytes 2359304 | tf_op jit(solution)/shard_map/ppermute | solution.py:41
  152.2 36.9 %collective-permute-start.18 = (bf16[8,2,64,384]{3,2,1,0:T(8,128)(2,1)S(1)}, bf16[8,2,64,384]{3,2,1,0:T(8,128)(2,1)S(1)}, u32[]{:S(2)}, u32[]{:S(2)}) collective-permute-start(bf16[8,2,64,384]{3,2,1,0:T(8,128)(2,1)S(1)} %get-tuple-element.99), channel_id=1, source_target_pairs={{0,64},{32,96},{64,0},{96,32},{1,65},{33,97},{65,1},{97,33},{2,66}... | collective-permute-start | bytes 2359304 | tf_op jit(solution)/shard_map/ppermute | solution.py:41
  154.8 34.9 %collective-permute-start.19 = (bf16[8,2,64,384]{3,2,1,0:T(8,128)(2,1)S(1)}, bf16[8,2,64,384]{3,2,1,0:T(8,128)(2,1)S(1)}, u32[]{:S(2)}, u32[]{:S(2)}) collective-permute-start(bf16[8,2,64,384]{3,2,1,0:T(8,128)(2,1)S(1)} %get-tuple-element.100), channel_id=1, source_target_pairs={{0,96},{32,0},{64,32},{96,64},{1,97},{33,1},{65,33},{97,65},{2,98}... | collective-permute-start | bytes 2359304 | tf_op jit(solution)/shard_map/ppermute | solution.py:41
  155.4 11.4 %collective-permute-start.21 = (bf16[128,1536]{1,0:T(8,128)(2,1)S(1)}, bf16[128,1536]{1,0:T(8,128)(2,1)S(1)}, u32[]{:S(2)}, u32[]{:S(2)}) collective-permute-start(bf16[128,1536]{1,0:T(8,128)(2,1)S(1)} %copy-done.37), channel_id=1, source_target_pairs={{0,8},{4,12},{8,0},{12,4},{1,9},{5,13},{9,1},{13,5},{2,10},{6,14},... | collective-permute-start | bytes 1179656 | tf_op jit(solution)/shard_map/ppermute | solution.py:37
  158.3 17.2 %collective-permute-start.22 = (bf16[128,1536]{1,0:T(8,128)(2,1)S(1)}, bf16[128,1536]{1,0:T(8,128)(2,1)S(1)}, u32[]{:S(2)}, u32[]{:S(2)}) collective-permute-start(bf16[128,1536]{1,0:T(8,128)(2,1)S(1)} %copy-done.35), channel_id=1, source_target_pairs={{0,12},{4,0},{8,4},{12,8},{1,13},{5,1},{9,5},{13,9},{2,14},{6,2},{... | collective-permute-start | bytes 1179656 | tf_op jit(solution)/shard_map/ppermute | solution.py:37
  176.1 14.9 %collective-permute-start.23 = (bf16[8,3,1536]{2,1,0:T(4,128)(2,1)S(1)}, bf16[8,3,1536]{2,1,0:T(4,128)(2,1)S(1)}, u32[]{:S(2)}, u32[]{:S(2)}) collective-permute-start(bf16[8,3,1536]{2,1,0:T(4,128)(2,1)S(1)} %get-tuple-element.108), channel_id=1, source_target_pairs={{0,1},{1,2},{2,3},{3,4},{4,5},{5,6},{6,7},{7,8},{8,9},{9,10},{10,1... | collective-permute-start | bytes 221192 | tf_op jit(solution)/shard_map/ppermute | solution.py:75
  180.4 10.6 %collective-permute-start.24 = (bf16[8,3,1536]{2,1,0:T(4,128)(2,1)S(1)}, bf16[8,3,1536]{2,1,0:T(4,128)(2,1)S(1)}, u32[]{:S(2)}, u32[]{:S(2)}) collective-permute-start(bf16[8,3,1536]{2,1,0:T(4,128)(2,1)S(1)} %get-tuple-element.109), channel_id=1, source_target_pairs={{1,0},{2,1},{3,2},{4,3},{5,4},{6,5},{7,6},{8,7},{9,8},{10,9},{11,1... | collective-permute-start | bytes 221192 | tf_op jit(solution)/shard_map/ppermute | solution.py:75
  191.0 34.4 %all-to-all-start.3 = ((bf16[8,2,64,384]{3,2,1,0:T(8,128)(2,1)}), bf16[8,2,64,384]{3,2,1,0:T(8,128)(2,1)S(1)}, u32[]{:S(2)}, u32[]{:S(2)}) async-start(bf16[8,2,64,384]{3,2,1,0:T(8,128)(2,1)} %sum_y.1), calls=%async_computation.3 | async-start | bytes 1572864 | tf_op jit(solution)/shard_map/all_to_all | solution.py:45
  198.6 21.2 %collective-permute-start.25 = (bf16[3,24,1536]{2,1,0:T(8,128)(2,1)S(1)}, bf16[3,24,1536]{2,1,0:T(8,128)(2,1)S(1)}, u32[]{:S(2)}, u32[]{:S(2)}) collective-permute-start(bf16[3,24,1536]{2,1,0:T(8,128)(2,1)S(1)} %get-tuple-element.120), channel_id=1, source_target_pairs={{0,16},{1,17},{2,18},{3,19},{4,20},{5,21},{6,22},{7,23},{8,24},{9,... | collective-permute-start | bytes 663560 | tf_op jit(solution)/shard_map/ppermute | solution.py:75
  200.5 19.2 %collective-permute-start.26 = (bf16[3,24,1536]{2,1,0:T(8,128)(2,1)S(1)}, bf16[3,24,1536]{2,1,0:T(8,128)(2,1)S(1)}, u32[]{:S(2)}, u32[]{:S(2)}) collective-permute-start(bf16[3,24,1536]{2,1,0:T(8,128)(2,1)S(1)} %get-tuple-element.121), channel_id=1, source_target_pairs={{16,0},{17,1},{18,2},{19,3},{20,4},{21,5},{22,6},{23,7},{24,8},{25... | collective-permute-start | bytes 663560 | tf_op jit(solution)/shard_map/ppermute | solution.py:75
  206.3 19.1 %collective-permute-start.27 = (bf16[2,32,384]{2,1,0:T(8,128)(2,1)S(1)}, bf16[2,32,384]{2,1,0:T(8,128)(2,1)S(1)}, u32[]{:S(2)}, u32[]{:S(2)}) collective-permute-start(bf16[2,32,384]{2,1,0:T(8,128)(2,1)S(1)} %get-tuple-element.125), channel_id=1, source_target_pairs={{0,32},{32,64},{64,96},{96,0},{1,33},{33,65},{65,97},{97,1},{2,34}... | collective-permute-start | bytes 147464 | tf_op jit(solution)/shard_map/ppermute | solution.py:41
  206.3 19.0 %collective-permute-start.28 = (bf16[2,32,384]{2,1,0:T(8,128)(2,1)S(1)}, bf16[2,32,384]{2,1,0:T(8,128)(2,1)S(1)}, u32[]{:S(2)}, u32[]{:S(2)}) collective-permute-start(bf16[2,32,384]{2,1,0:T(8,128)(2,1)S(1)} %get-tuple-element.126), channel_id=1, source_target_pairs={{0,64},{32,96},{64,0},{96,32},{1,65},{33,97},{65,1},{97,33},{2,66}... | collective-permute-start | bytes 147464 | tf_op jit(solution)/shard_map/ppermute | solution.py:41
  208.0 17.3 %collective-permute-start.29 = (bf16[2,32,384]{2,1,0:T(8,128)(2,1)S(1)}, bf16[2,32,384]{2,1,0:T(8,128)(2,1)S(1)}, u32[]{:S(2)}, u32[]{:S(2)}) collective-permute-start(bf16[2,32,384]{2,1,0:T(8,128)(2,1)S(1)} %get-tuple-element.127), channel_id=1, source_target_pairs={{0,96},{32,0},{64,32},{96,64},{1,97},{33,1},{65,33},{97,65},{2,98}... | collective-permute-start | bytes 147464 | tf_op jit(solution)/shard_map/ppermute | solution.py:41
  (52 other events, 303.8 us)

commit v5 on v3

--- a/solution.py
+++ b/solution.py
@@ -169,8 +169,7 @@
         column = pad[:, TAPS - 1 - col_tap : TAPS - 1 - col_tap + TILE_COLS, :]
         for row_tap in range(TAPS):
             start = TAPS - 1 - row_tap
-            n = row_tap * TAPS + col_tap
-            term = column[start : start + TILE_ROWS] * kernel[n : n + 1, :][None]
+            term = column[start : start + TILE_ROWS] * kernel[row_tap, col_tap : col_tap + 1, :][None]
             total = term if total is None else total + term
     out[...] = (grad[...].astype(f32) + total).astype(bf16)
 
@@ -206,13 +205,25 @@
 
 
 def token_kernel(where, *refs):
-    tok, (xs, mine, other, xt) = refs[:NX], refs[NX:]
+    tok, (xs, mine, other, xt, sems) = refs[:NX], refs[NX:]
     c = where[1]
-    for i in range(NX):
-        rows = slice(i * BLOCK, (i + 1) * BLOCK)
-        xs[0, rows, :] = tok[i][:BLOCK]
-        xs[1, rows, :] = tok[i][BLOCK:]
+    copies = [
+        [
+            pltpu.make_async_copy(
+                tok[i].at[pl.ds(m * BLOCK, BLOCK)],
+                xs.at[m, pl.ds(i * BLOCK, BLOCK)],
+                sems.at[m, i],
+            )
+            for i in range(NX)
+        ]
+        for m in range(2)
+    ]
     for m in range(2):
+        for i in range(NX):
+            copies[m][i].start()
+    for m in range(2):
+        for i in range(NX):
+            copies[m][i].wait()
         for i in range(CHAN // 256):
             xt[i * 256 : (i + 1) * 256, :] = xs[m, :, i * 256 : (i + 1) * 256].T
         for out, core in ((mine, c), (other, 1 - c)):
@@ -229,9 +240,10 @@
     return pl.pallas_call(
         token_kernel,
         out_shape=[jax.ShapeDtypeStruct((2, TOKENS, CHAN), bf16), half, half],
-        in_specs=[pl.BlockSpec(memory_space=pltpu.SMEM)] + vmem_specs(NX),
+        in_specs=[pl.BlockSpec(memory_space=pltpu.SMEM)]
+        + [pl.BlockSpec(memory_space=pl.ANY)] * NX,
         out_specs=vmem_specs(3),
-        scratch_shapes=[pltpu.VMEM((CHAN, TOKENS), bf16)],
+        scratch_shapes=[pltpu.VMEM((CHAN, TOKENS), bf16), pltpu.SemaphoreType.DMA((2, NX))],
         compiler_params=pltpu.CompilerParams(vmem_limit_bytes=20 * 2**20),
         cost_estimate=pl.CostEstimate(flops=0, bytes_accessed=12_000_000, transcendentals=0),
         name="tokens",
@@ -254,17 +266,22 @@
 
     width = 256
 
-    def step(i, _):
-        cols = pl.ds(pl.multiple_of(i * width, width), width)
+    def products(i):
+        cols = slice(i * width, (i + 1) * width)
         pre = jnp.dot(xs[0], w_in[:, cols], preferred_element_type=f32) + bias[:, cols]
-        back = jnp.dot(xs[1], w_out[:, cols], preferred_element_type=f32)
+        return pre, jnp.dot(xs[1], w_out[:, cols], preferred_element_type=f32)
+
+    count = HIDDEN // width
+    pre, back = products(0)
+    for i in range(count):
+        following = products(i + 1) if i + 1 < count else None
+        cols = slice(i * width, (i + 1) * width)
         cdf = 0.5 * (1.0 + lax.erf(pre * root_half))
         slope = cdf + pre * jnp.exp(-0.5 * pre * pre) * density_norm
         act[:, cols] = (pre * cdf).astype(bf16)
         pre_grad[:, cols] = (back * slope).astype(bf16)
-        return 0
-
-    lax.fori_loop(0, HIDDEN // width, step, 0)
+        if following is not None:
+            pre, back = following
 
 
 def activations(where, bias, xs, first, second):
@@ -285,26 +302,24 @@
 
 
 def normed_kernel(pre_grad, w_in, *outs):
+    part = lax.dot_general(
+        pre_grad[...], w_in[...], (((1,), (1,)), ((), ())), preferred_element_type=f32
+    ).astype(bf16)
+    for b in range(NX):
+        outs[b][...] = part[b * BLOCK : (b + 1) * BLOCK]
+
+
+def normed_gradient(pre_grad, w_in):
     width = 256
-
-    def step(i, _):
-        cols = pl.ds(pl.multiple_of(i * width, width), width)
-        part = lax.dot_general(
-            pre_grad[...], w_in[cols, :], (((1,), (1,)), ((), ())), preferred_element_type=f32
-        ).astype(bf16)
-        for b in range(NX):
-            outs[b][:, cols] = part[b * BLOCK : (b + 1) * BLOCK]
-        return 0
-
-    lax.fori_loop(0, CHAN // width, step, 0)
-
-
-def normed_gradient(pre_grad, w_in):
     return pl.pallas_call(
         normed_kernel,
+        grid=(CHAN // width,),
         out_shape=[jax.ShapeDtypeStruct((BLOCK, CHAN), bf16)] * NX,
-        in_specs=vmem_specs(2),
-        out_specs=vmem_specs(NX),
+        in_specs=[
+            pl.BlockSpec((TOKENS, HIDDEN), lambda i: (0, 0)),
+            pl.BlockSpec((width, HIDDEN), lambda i: (i, 0)),
+        ],
+        out_specs=[pl.BlockSpec((BLOCK, width), lambda i: (0, i))] * NX,
         compiler_params=pltpu.CompilerParams(vmem_limit_bytes=20 * 2**20),
         cost_estimate=pl.CostEstimate(
             flops=2 * TOKENS * CHAN * HIDDEN, bytes_accessed=20_000_000, transcendentals=0
@@ -448,11 +463,10 @@
     first = gather_z(lead_y)
     swapped = [swap(v) for v in second[:2]] + [None, swap(second[3])]
     where = jnp.stack([lax.axis_index("y"), lax.axis_index("c")]).astype(jnp.int32)
-    tok[2], second[2] = lax.optimization_barrier((tok[2], second[2]))
+    first, swapped[1], swapped[3], second[2], tok[2] = lax.optimization_barrier(
+        (first, swapped[1], swapped[3], second[2], tok[2])
+    )
     xs, mine, other = tokens(where, tok)
-    first, swapped[1], swapped[3], xs = lax.optimization_barrier(
-        (first, swapped[1], swapped[3], xs)
-    )
     other = swap(other)
     swapped[2] = swap(second[2])
     second = [second, swapped]
@@ -477,8 +491,7 @@
     up, down = to_tile(last_rows, 1, 0), to_tile(first_rows, -1, 0)
     zs = [to_y(v, r) for r, v in enumerate(zs)]
     ys = exchange_z(ys)
-    kernel = dw_kernel.reshape(TAPS * TAPS, CHAN)
-    grad_input = convolution(own, left, right, up, down, kernel, out_grad)
+    grad_input = convolution(own, left, right, up, down, dw_kernel, out_grad)
     grad_input, ys = lax.optimization_barrier((grad_input, ys))
     grad_in, grad_out = finish(zs, ys)
     return (grad_input, grad_in, grad_out)

time: 216 us -> 211 us (0.977)
  waiting for transfers between devices: 83.7 us -> 71.9 us
  starting transfers between devices: 68.9 us -> 73.6 us
  local copies, waits for them, and re-layouts: 23.1 us -> 27.3 us
    ppermute x6, waiting for transfers between devices: 32.1 us -> 23.8 us  [to_x(): return lax.ppermute(value, 'x', shift(NX, k)) if k else value]
    unnamed x60 -> x78, local copies, waits for them, and re-layouts: 18.1 us -> 23.3 us
    ppermute x8, waiting for transfers between devices: 4.22 us -> 0.02 us  [swap(): return lax.ppermute(value, 'c', shift(2, 1))]
    ppermute x6, starting transfers between devices: 5.84 us -> 8.92 us  [to_x(): return lax.ppermute(value, 'x', shift(NX, k)) if k else value]
    pallas_call x1, Pallas kernels: 11.8 us -> 9.17 us  [activations(): pl.pallas_call(activation_kernel, out_shape=[out, out, jax.ShapeDtypeStru...]
  transfers between devices with their start and end apart: 34 -> 34, of which waited for: 14 -> 12; matrix products, arithmetic and copies ran while one was open for 1% -> 1% of each run, Pallas kernels for 7% -> 7%
where the time goes in v5:
time: 211 us; the launch traced here: 210 us
  starting transfers between devices  73.6 us (35%)
  waiting for transfers between devices  71.9 us (34%)
  Pallas kernels  34.2 us (16%)
  local copies, waits for them, and re-layouts  27.3 us (13%)
  other arithmetic  2.42 us (1%)
    ppermute x12, waiting for transfers between devices, to_y(): return lax.ppermute(value, 'y', shift(NY, k)) if k else value  37.2 us
    all_to_all x4, starting transfers between devices, exchange_z(): return lax.all_to_all(value, Z, 0, 0, tiled=True)  29.9 us
    ppermute x6, waiting for transfers between devices, to_x(): return lax.ppermute(value, 'x', shift(NX, k)) if k else value  23.8 us
    unnamed x78, local copies, waits for them, and re-layouts  23.3 us
    ppermute x12, starting transfers between devices, to_y(): return lax.ppermute(value, 'y', shift(NY, k)) if k else value  19.8 us
    ppermute x4, starting transfers between devices, to_tile(): return lax.ppermute(value, FINE, pairs)  13.2 us
    ppermute x4, waiting for transfers between devices, to_tile(): return lax.ppermute(value, FINE, pairs)  10.4 us
    pallas_call x1, Pallas kernels, activations(): pl.pallas_call(activation_kernel, out_shape=[out, out, jax.ShapeDtypeStru...  9.17 us
  transfers between devices with their start and end apart: 34, of which 12 were waited for; matrix products, arithmetic and copies ran while one was open for 1% of the time, Pallas kernels for 7%

profile of v5, /device:TPU:32, one launch (start us, length us, event | category | flops | bytes accessed | tf_op | source)
XLA Modules:
  0.0 210.4 jit_solution(14427872722570623243)
XLA Ops:
  3.5 8.6 %all-to-all-start = ((bf16[8,144,384]{2,1,0:T(8,128)(2,1)}), bf16[8,144,384]{2,1,0:T(8,128)(2,1)S(1)}, u32[]{:S(2)}, u32[]{:S(2)}) async-start(bf16[8,144,384]{2,1,0:T(8,128)(2,1)} %broadcast_in_dim.10), calls=%async_computation | async-start | bytes 1769472 | tf_op jit(solution)/shard_map/all_to_all | solution.py:44
  16.7 3.1 %collective-permute-start = (bf16[2,32,384]{2,1,0:T(8,128)(2,1)S(1)}, bf16[2,32,384]{2,1,0:T(8,128)(2,1)S(1)}, u32[]{:S(2)}, u32[]{:S(2)}) collective-permute-start(bf16[2,32,384]{2,1,0:T(8,128)(2,1)S(1)} %pad_maximum_fusion.1), channel_id=1, source_target_pairs={{0,96},{32,0},{64,32},{96,64},{1,97},{33,1},{65,33},{97,65},{2,98}... | collective-permute-start | bytes 147464 | tf_op jit(solution)/shard_map/ppermute | solution.py:40
  21.6 3.9 %collective-permute-done.1 = bf16[2,32,384]{2,1,0:T(8,128)(2,1)S(1)} collective-permute-done((bf16[2,32,384]{2,1,0:T(8,128)(2,1)S(1)}, bf16[2,32,384]{2,1,0:T(8,128)(2,1)S(1)}, u32[]{:S(2)}, u32[]{:S(2)}) %collective-permute-start.1) | collective-permute-done | bytes 49184 | tf_op jit(solution)/shard_map/ppermute | solution.py:40
  26.0 7.4 %collective-permute-done.4.refs_3_ = bf16[256,1536]{1,0:T(8,128)(2,1)S(1)} collective-permute-done((bf16[256,1536]{1,0:T(8,128)(2,1)S(1)}, bf16[256,1536]{1,0:T(8,128)(2,1)S(1)}, u32[]{:S(2)}, u32[]{:S(2)}) %collective-permute-start.4) | collective-permute-done | bytes 786464 | tf_op jit(solution)/shard_map/ppermute | solution.py:36
  37.0 6.8 %all-to-all-start.1 = ((bf16[8,4,2,32,384]{4,3,2,1,0:T(8,128)(2,1)}), bf16[8,4,2,32,384]{4,3,2,1,0:T(8,128)(2,1)S(1)}, u32[]{:S(2)}, u32[]{:S(2)}) async-start(bf16[8,4,2,32,384]{4,3,2,1,0:T(8,128)(2,1)} %broadcast_in_dim.11), calls=%async_computation.1 | async-start | bytes 3145728 | tf_op jit(solution)/shard_map/all_to_all | solution.py:44
  52.2 13.5 %collective-permute-done.7.refs_7_ = bf16[8,2,64,384]{3,2,1,0:T(8,128)(2,1)S(1)} collective-permute-done((bf16[8,2,64,384]{3,2,1,0:T(8,128)(2,1)S(1)}, bf16[8,2,64,384]{3,2,1,0:T(8,128)(2,1)S(1)}, u32[]{:S(2)}, u32[]{:S(2)}) %collective-permute-start.7) | collective-permute-done | bytes 786464 | tf_op jit(solution)/shard_map/ppermute | solution.py:40
  66.6 13.3 %collective-permute-done.5.refs_5_ = bf16[8,2,64,384]{3,2,1,0:T(8,128)(2,1)S(1)} collective-permute-done((bf16[8,2,64,384]{3,2,1,0:T(8,128)(2,1)S(1)}, bf16[8,2,64,384]{3,2,1,0:T(8,128)(2,1)S(1)}, u32[]{:S(2)}, u32[]{:S(2)}) %collective-permute-start.5) | collective-permute-done | bytes 786464 | tf_op jit(solution)/shard_map/ppermute | solution.py:40
  89.7 3.2 %tokens.1 = (bf16[2,512,1536]{2,1,0:T(8,128)(2,1)S(1)}, bf16[2,768,512]{2,1,0:T(8,128)(2,1)S(1)}, bf16[2,768,512]{2,1,0:T(8,128)(2,1)S(1)}) custom-call(s32[2]{0:T(128)S(1)} %pad_add_fusion.where, bf16[256,1536]{1,0:T(8,128)(2,1)S(1)} %get-tuple-element.59.refs_0_, bf16[256,1536]{1,0:T(8,128)(2,1)S(1)} %copy-done.6, bf16[256,1536]{1,0:T(8,128)(2,1)S(1)} %copy-done.10, ...), custom_call_target="tpu_custom_call" | custom-call | bytes 12000000 | tf_op jit(solution)/shard_map/tokens/pallas_call | solution.py:240
  95.8 9.2 %activations.1 = (bf16[512,1536]{1,0:T(8,128)(2,1)S(1)}, bf16[512,1536]{1,0:T(8,128)(2,1)S(1)}, bf16[1536,1536]{1,0:T(8,128)(2,1)}) custom-call(s32[2]{0:T(128)S(1)} %pad_add_fusion.where, f32[1,1536]{1,0:T(1,128)S(1)} %bitcast.25, bf16[2,512,1536]{2,1,0:T(8,128)(2,1)} %copy-done.15, bf16[8,4,2,32,384]{4,3,2,1,0:T(8,128)(2,1)S(1)} %all-to-all-done.1.refs_2_, ...), custom_call_target="tpu_custom_call" | custom-call | flops 4831838208 | bytes 25000000 | tf_op jit(solution)/shard_map/activations/pallas_call | solution.py:290
  105.7 2.3 %copy-done.31 = bf16[1536,1536]{1,0:T(8,128)(2,1)S(1)} copy-done((bf16[1536,1536]{1,0:T(8,128)(2,1)S(1)}, bf16[1536,1536]{1,0:T(8,128)(2,1)}, u32[]{:S(2)}) %copy-start.31) | copy-done | bytes 4718616
  108.0 3.8 %normed_gradient.1 = (bf16[128,1536]{1,0:T(8,128)(2,1)S(1)}, bf16[128,1536]{1,0:T(8,128)(2,1)S(1)}, bf16[128,1536]{1,0:T(8,128)(2,1)S(1)}, bf16[128,1536]{1,0:T(8,128)(2,1)S(1)}) custom-call(bf16[512,1536]{1,0:T(8,128)(2,1)S(1)} %get-tuple-element.72.pre_grad.refs_0_, bf16[1536,1536]{1,0:T(8,128)(2,1)S(1)} %copy-done.31), custom_call_target="tpu_custom_call" | custom-call | flops 2415919104 | bytes 20000000 | tf_op jit(solution)/shard_map/normed_gradient/pallas_call | solution.py:314
  113.3 9.1 %weight_gradients.1 = (bf16[8,2,64,384]{3,2,1,0:T(8,128)(2,1)S(1)}, bf16[8,2,64,384]{3,2,1,0:T(8,128)(2,1)S(1)}, bf16[8,2,64,384]{3,2,1,0:T(8,128)(2,1)S(1)}, bf...) custom-call(s32[2]{0:T(128)S(1)} %pad_add_fusion.where, bf16[2,768,512]{2,1,0:T(8,128)(2,1)S(1)} %get-tuple-element.65.mine, ...), custom_call_target="tpu_custom_call" | custom-call | flops 4831838208 | bytes 30000000 | tf_op jit(solution)/shard_map/weight_gradients/pallas_call | solution.py:357
  125.9 7.3 %all-to-all-start.2 = ((bf16[8,4,2,32,384]{4,3,2,1,0:T(8,128)(2,1)}), bf16[8,4,2,32,384]{4,3,2,1,0:T(8,128)(2,1)S(1)}, u32[]{:S(2)}, u32[]{:S(2)}) async-start(bf16[8,4,2,32,384]{4,3,2,1,0:T(8,128)(2,1)} %get-tuple-element.97), calls=%async_computation.2 | async-start | bytes 3145728 | tf_op jit(solution)/shard_map/all_to_all | solution.py:44
  134.6 4.1 %collective-permute-start.18 = (bf16[8,2,64,384]{3,2,1,0:T(8,128)(2,1)}, bf16[8,2,64,384]{3,2,1,0:T(8,128)(2,1)S(1)}, u32[]{:S(2)}, u32[]{:S(2)}) collective-permute-start(bf16[8,2,64,384]{3,2,1,0:T(8,128)(2,1)} %copy-done.27), channel_id=1, source_target_pairs={{0,64},{32,96},{64,0},{96,32},{1,65},{33,97},{65,1},{97,33},{2,66}... | collective-permute-start | bytes 2359304 | tf_op jit(solution)/shard_map/ppermute | solution.py:40
  140.1 2.9 %collective-permute-start.21 = (bf16[128,1536]{1,0:T(8,128)(2,1)}, bf16[128,1536]{1,0:T(8,128)(2,1)S(1)}, u32[]{:S(2)}, u32[]{:S(2)}) collective-permute-start(bf16[128,1536]{1,0:T(8,128)(2,1)} %copy-done.29), channel_id=1, source_target_pairs={{0,8},{4,12},{8,0},{12,4},{1,9},{5,13},{9,1},{13,5},{2,10},{6,14},... | collective-permute-start | bytes 1179656 | tf_op jit(solution)/shard_map/ppermute | solution.py:36
  143.0 3.7 %collective-permute-done.20.refs_1_ = bf16[128,1536]{1,0:T(8,128)(2,1)S(1)} collective-permute-done((bf16[128,1536]{1,0:T(8,128)(2,1)}, bf16[128,1536]{1,0:T(8,128)(2,1)S(1)}, u32[]{:S(2)}, u32[]{:S(2)}) %collective-permute-start.20) | collective-permute-done | bytes 393248 | tf_op jit(solution)/shard_map/ppermute | solution.py:36
  147.3 6.8 %collective-permute-done.21.refs_2_ = bf16[128,1536]{1,0:T(8,128)(2,1)S(1)} collective-permute-done((bf16[128,1536]{1,0:T(8,128)(2,1)}, bf16[128,1536]{1,0:T(8,128)(2,1)S(1)}, u32[]{:S(2)}, u32[]{:S(2)}) %collective-permute-start.21) | collective-permute-done | bytes 393248 | tf_op jit(solution)/shard_map/ppermute | solution.py:36
  154.0 5.9 %collective-permute-done.22.refs_3_ = bf16[128,1536]{1,0:T(8,128)(2,1)S(1)} collective-permute-done((bf16[128,1536]{1,0:T(8,128)(2,1)S(1)}, bf16[128,1536]{1,0:T(8,128)(2,1)S(1)}, u32[]{:S(2)}, u32[]{:S(2)}) %collective-permute-start.22) | collective-permute-done | bytes 393248 | tf_op jit(solution)/shard_map/ppermute | solution.py:36
  161.4 4.3 %collective-permute-start.23 = (bf16[8,3,1536]{2,1,0:T(4,128)(2,1)S(1)}, bf16[8,3,1536]{2,1,0:T(4,128)(2,1)S(1)}, u32[]{:S(2)}, u32[]{:S(2)}) collective-permute-start(bf16[8,3,1536]{2,1,0:T(4,128)(2,1)S(1)} %get-tuple-element.92), channel_id=1, source_target_pairs={{0,1},{1,2},{2,3},{3,4},{4,5},{5,6},{6,7},{7,8},{8,9},{9,10},{10,1... | collective-permute-start | bytes 221192 | tf_op jit(solution)/shard_map/ppermute | solution.py:74
  167.0 5.9 %collective-permute-done.18.refs_2_ = bf16[8,2,64,384]{3,2,1,0:T(8,128)(2,1)S(1)} collective-permute-done((bf16[8,2,64,384]{3,2,1,0:T(8,128)(2,1)}, bf16[8,2,64,384]{3,2,1,0:T(8,128)(2,1)S(1)}, u32[]{:S(2)}, u32[]{:S(2)}) %collective-permute-start.18) | collective-permute-done | bytes 786464 | tf_op jit(solution)/shard_map/ppermute | solution.py:40
  174.2 7.2 %all-to-all-start.3 = ((bf16[8,2,64,384]{3,2,1,0:T(8,128)(2,1)}), bf16[8,2,64,384]{3,2,1,0:T(8,128)(2,1)S(1)}, u32[]{:S(2)}, u32[]{:S(2)}) async-start(bf16[8,2,64,384]{3,2,1,0:T(8,128)(2,1)} %sum_y.1), calls=%async_computation.3 | async-start | bytes 1572864 | tf_op jit(solution)/shard_map/all_to_all | solution.py:44
  183.7 5.8 %collective-permute-start.26 = (bf16[3,24,1536]{2,1,0:T(8,128)(2,1)S(1)}, bf16[3,24,1536]{2,1,0:T(8,128)(2,1)S(1)}, u32[]{:S(2)}, u32[]{:S(2)}) collective-permute-start(bf16[3,24,1536]{2,1,0:T(8,128)(2,1)S(1)} %get-tuple-element.105), channel_id=1, source_target_pairs={{16,0},{17,1},{18,2},{19,3},{20,4},{21,5},{22,6},{23,7},{24,8},{25... | collective-permute-start | bytes 663560 | tf_op jit(solution)/shard_map/ppermute | solution.py:74
  192.7 10.4 %collective-permute-done.25.up = bf16[3,24,1536]{2,1,0:T(8,128)(2,1)S(1)} collective-permute-done((bf16[3,24,1536]{2,1,0:T(8,128)(2,1)S(1)}, bf16[3,24,1536]{2,1,0:T(8,128)(2,1)S(1)}, u32[]{:S(2)}, u32[]{:S(2)}) %collective-permute-start.25) | collective-permute-done | bytes 221216 | tf_op jit(solution)/shard_map/ppermute | solution.py:74
  203.2 5.6 %convolution.1 = bf16[8,16,1536]{2,1,0:T(8,128)(2,1)} custom-call(bf16[8,16,1536]{2,1,0:T(8,128)(2,1)S(1)} %get-tuple-element.94.own, bf16[8,3,1536]{2,1,0:T(4,128)(2,1)S(1)} %collective-permute-done.23.left, bf16[8,3,1536]{2,1,0:T(4,128)(2,1)S(1)} %collective-permute-done.24.right, bf16[3,24,1536]{2,1,0:T(8,128)(2,1)S(1)} %collective-permute-done.25.up, ...), custom_call_target="tpu_custom_call" | custom-call | tf_op jit(solution)/shard_map/convolution/pallas_call | solution.py:185
  (151 shorter events, 55.4 us)
Async XLA Ops:
  3.5 32.1 %all-to-all-start = ((bf16[8,144,384]{2,1,0:T(8,128)(2,1)}), bf16[8,144,384]{2,1,0:T(8,128)(2,1)S(1)}, u32[]{:S(2)}, u32[]{:S(2)}) async-start(bf16[8,144,384]{2,1,0:T(8,128)(2,1)} %broadcast_in_dim.10), calls=%async_computation | async-start | bytes 1769472 | tf_op jit(solution)/shard_map/all_to_all | solution.py:44
  13.5 19.9 %collective-permute-start.4 = (bf16[256,1536]{1,0:T(8,128)(2,1)S(1)}, bf16[256,1536]{1,0:T(8,128)(2,1)S(1)}, u32[]{:S(2)}, u32[]{:S(2)}) collective-permute-start(bf16[256,1536]{1,0:T(8,128)(2,1)S(1)} %get-tuple-element.59.refs_0_), channel_id=1, source_target_pairs={{0,4},{4,8},{8,12},{12,0},{1,5},{5,9},{9,13},{13,1},{2,6},{6,10},{... | collective-permute-start | bytes 2359304 | tf_op jit(solution)/shard_map/ppermute | solution.py:36
  15.0 19.3 %collective-permute-start.3 = (bf16[256,1536]{1,0:T(8,128)(2,1)S(1)}, bf16[256,1536]{1,0:T(8,128)(2,1)S(1)}, u32[]{:S(2)}, u32[]{:S(2)}) collective-permute-start(bf16[256,1536]{1,0:T(8,128)(2,1)S(1)} %get-tuple-element.59.refs_0_), channel_id=1, source_target_pairs={{0,12},{4,0},{8,4},{12,8},{1,13},{5,1},{9,5},{13,9},{2,14},{6,2},{... | collective-permute-start | bytes 2359304 | tf_op jit(solution)/shard_map/ppermute | solution.py:36
  37.0 47.3 %all-to-all-start.1 = ((bf16[8,4,2,32,384]{4,3,2,1,0:T(8,128)(2,1)}), bf16[8,4,2,32,384]{4,3,2,1,0:T(8,128)(2,1)S(1)}, u32[]{:S(2)}, u32[]{:S(2)}) async-start(bf16[8,4,2,32,384]{4,3,2,1,0:T(8,128)(2,1)} %broadcast_in_dim.11), calls=%async_computation.1 | async-start | bytes 3145728 | tf_op jit(solution)/shard_map/all_to_all | solution.py:44
  45.1 20.6 %collective-permute-start.7 = (bf16[8,2,64,384]{3,2,1,0:T(8,128)(2,1)S(1)}, bf16[8,2,64,384]{3,2,1,0:T(8,128)(2,1)S(1)}, u32[]{:S(2)}, u32[]{:S(2)}) collective-permute-start(bf16[8,2,64,384]{3,2,1,0:T(8,128)(2,1)S(1)} %bitcast.19), channel_id=1, source_target_pairs={{0,32},{32,64},{64,96},{96,0},{1,33},{33,65},{65,97},{97,1},{2,34}... | collective-permute-start | bytes 2359304 | tf_op jit(solution)/shard_map/ppermute | solution.py:40
  46.7 33.2 %collective-permute-start.5 = (bf16[8,2,64,384]{3,2,1,0:T(8,128)(2,1)S(1)}, bf16[8,2,64,384]{3,2,1,0:T(8,128)(2,1)S(1)}, u32[]{:S(2)}, u32[]{:S(2)}) collective-permute-start(bf16[8,2,64,384]{3,2,1,0:T(8,128)(2,1)S(1)} %bitcast.20), channel_id=1, source_target_pairs={{0,96},{32,0},{64,32},{96,64},{1,97},{33,1},{65,33},{97,65},{2,98}... | collective-permute-start | bytes 2359304 | tf_op jit(solution)/shard_map/ppermute | solution.py:40
  48.4 32.4 %collective-permute-start.10 = (bf16[256,1536]{1,0:T(8,128)(2,1)S(1)}, bf16[256,1536]{1,0:T(8,128)(2,1)S(1)}, u32[]{:S(2)}, u32[]{:S(2)}) collective-permute-start(bf16[256,1536]{1,0:T(8,128)(2,1)S(1)} %get-tuple-element.59.refs_0_), channel_id=1, source_target_pairs={{0,8},{4,12},{8,0},{12,4},{1,9},{5,13},{9,1},{13,5},{2,10},{6,14},... | collective-permute-start | bytes 2359304 | tf_op jit(solution)/shard_map/ppermute | solution.py:36
  50.2 31.5 %collective-permute-start.9 = (bf16[8,2,64,384]{3,2,1,0:T(8,128)(2,1)S(1)}, bf16[8,2,64,384]{3,2,1,0:T(8,128)(2,1)S(1)}, u32[]{:S(2)}, u32[]{:S(2)}) collective-permute-start(bf16[8,2,64,384]{3,2,1,0:T(8,128)(2,1)S(1)} %bitcast.21), channel_id=1, source_target_pairs={{0,64},{32,96},{64,0},{96,32},{1,65},{33,97},{65,1},{97,33},{2,66}... | collective-permute-start | bytes 2359304 | tf_op jit(solution)/shard_map/ppermute | solution.py:40
  65.7 16.0 %collective-permute-start.8 = (bf16[8,2,64,384]{3,2,1,0:T(8,128)(2,1)S(1)}, bf16[8,2,64,384]{3,2,1,0:T(8,128)(2,1)S(1)}, u32[]{:S(2)}, u32[]{:S(2)}) collective-permute-start(bf16[8,2,64,384]{3,2,1,0:T(8,128)(2,1)S(1)} %collective-permute-done.7.refs_7_), channel_id=1, source_target_pairs={{0,16},{16,0},{1,17},{17,1},{2,18},{18,2},{3,19},{19,3},{4,20},{20... | collective-permute-start | bytes 2359304 | tf_op jit(solution)/shard_map/ppermute | solution.py:61
  84.4 10.2 %collective-permute-start.12 = (bf16[8,4,2,32,384]{4,3,2,1,0:T(8,128)(2,1)S(1)}, bf16[8,4,2,32,384]{4,3,2,1,0:T(8,128)(2,1)}, u32[]{:S(2)}, u32[]{:S(2)}) collective-permute-start(bf16[8,4,2,32,384]{4,3,2,1,0:T(8,128)(2,1)S(1)} %all-to-all-done.1.refs_2_), channel_id=1, source_target_pairs={{0,16},{16,0},{1,17},{17,1},{2,18},{18,2},{3,19},{19,3},{4,20},{20... | collective-permute-start | bytes 4718600 | tf_op jit(solution)/shard_map/ppermute | solution.py:61
  125.9 48.2 %all-to-all-start.2 = ((bf16[8,4,2,32,384]{4,3,2,1,0:T(8,128)(2,1)}), bf16[8,4,2,32,384]{4,3,2,1,0:T(8,128)(2,1)S(1)}, u32[]{:S(2)}, u32[]{:S(2)}) async-start(bf16[8,4,2,32,384]{4,3,2,1,0:T(8,128)(2,1)} %get-tuple-element.97), calls=%async_computation.2 | async-start | bytes 3145728 | tf_op jit(solution)/shard_map/all_to_all | solution.py:44
  133.3 13.4 %collective-permute-start.20 = (bf16[128,1536]{1,0:T(8,128)(2,1)}, bf16[128,1536]{1,0:T(8,128)(2,1)S(1)}, u32[]{:S(2)}, u32[]{:S(2)}) collective-permute-start(bf16[128,1536]{1,0:T(8,128)(2,1)} %copy-done.30), channel_id=1, source_target_pairs={{0,4},{4,8},{8,12},{12,0},{1,5},{5,9},{9,13},{13,1},{2,6},{6,10},{... | collective-permute-start | bytes 1179656 | tf_op jit(solution)/shard_map/ppermute | solution.py:36
  133.6 33.4 %collective-permute-start.17 = (bf16[8,2,64,384]{3,2,1,0:T(8,128)(2,1)}, bf16[8,2,64,384]{3,2,1,0:T(8,128)(2,1)S(1)}, u32[]{:S(2)}, u32[]{:S(2)}) collective-permute-start(bf16[8,2,64,384]{3,2,1,0:T(8,128)(2,1)} %copy-done.28), channel_id=1, source_target_pairs={{0,32},{32,64},{64,96},{96,0},{1,33},{33,65},{65,97},{97,1},{2,34}... | collective-permute-start | bytes 2359304 | tf_op jit(solution)/shard_map/ppermute | solution.py:40
  134.6 38.2 %collective-permute-start.18 = (bf16[8,2,64,384]{3,2,1,0:T(8,128)(2,1)}, bf16[8,2,64,384]{3,2,1,0:T(8,128)(2,1)S(1)}, u32[]{:S(2)}, u32[]{:S(2)}) collective-permute-start(bf16[8,2,64,384]{3,2,1,0:T(8,128)(2,1)} %copy-done.27), channel_id=1, source_target_pairs={{0,64},{32,96},{64,0},{96,32},{1,65},{33,97},{65,1},{97,33},{2,66}... | collective-permute-start | bytes 2359304 | tf_op jit(solution)/shard_map/ppermute | solution.py:40
  138.7 34.1 %collective-permute-start.19 = (bf16[8,2,64,384]{3,2,1,0:T(8,128)(2,1)}, bf16[8,2,64,384]{3,2,1,0:T(8,128)(2,1)S(1)}, u32[]{:S(2)}, u32[]{:S(2)}) collective-permute-start(bf16[8,2,64,384]{3,2,1,0:T(8,128)(2,1)} %copy-done.26), channel_id=1, source_target_pairs={{0,96},{32,0},{64,32},{96,64},{1,97},{33,1},{65,33},{97,65},{2,98}... | collective-permute-start | bytes 2359304 | tf_op jit(solution)/shard_map/ppermute | solution.py:40
  140.1 13.9 %collective-permute-start.21 = (bf16[128,1536]{1,0:T(8,128)(2,1)}, bf16[128,1536]{1,0:T(8,128)(2,1)S(1)}, u32[]{:S(2)}, u32[]{:S(2)}) collective-permute-start(bf16[128,1536]{1,0:T(8,128)(2,1)} %copy-done.29), channel_id=1, source_target_pairs={{0,8},{4,12},{8,0},{12,4},{1,9},{5,13},{9,1},{13,5},{2,10},{6,14},... | collective-permute-start | bytes 1179656 | tf_op jit(solution)/shard_map/ppermute | solution.py:36
  146.7 13.3 %collective-permute-start.22 = (bf16[128,1536]{1,0:T(8,128)(2,1)S(1)}, bf16[128,1536]{1,0:T(8,128)(2,1)S(1)}, u32[]{:S(2)}, u32[]{:S(2)}) collective-permute-start(bf16[128,1536]{1,0:T(8,128)(2,1)S(1)} %get-tuple-element.88), channel_id=1, source_target_pairs={{0,12},{4,0},{8,4},{12,8},{1,13},{5,1},{9,5},{13,9},{2,14},{6,2},{... | collective-permute-start | bytes 1179656 | tf_op jit(solution)/shard_map/ppermute | solution.py:36
  161.4 12.8 %collective-permute-start.23 = (bf16[8,3,1536]{2,1,0:T(4,128)(2,1)S(1)}, bf16[8,3,1536]{2,1,0:T(4,128)(2,1)S(1)}, u32[]{:S(2)}, u32[]{:S(2)}) collective-permute-start(bf16[8,3,1536]{2,1,0:T(4,128)(2,1)S(1)} %get-tuple-element.92), channel_id=1, source_target_pairs={{0,1},{1,2},{2,3},{3,4},{4,5},{5,6},{6,7},{7,8},{8,9},{9,10},{10,1... | collective-permute-start | bytes 221192 | tf_op jit(solution)/shard_map/ppermute | solution.py:74
  174.2 34.6 %all-to-all-start.3 = ((bf16[8,2,64,384]{3,2,1,0:T(8,128)(2,1)}), bf16[8,2,64,384]{3,2,1,0:T(8,128)(2,1)S(1)}, u32[]{:S(2)}, u32[]{:S(2)}) async-start(bf16[8,2,64,384]{3,2,1,0:T(8,128)(2,1)} %sum_y.1), calls=%async_computation.3 | async-start | bytes 1572864 | tf_op jit(solution)/shard_map/all_to_all | solution.py:44
  181.7 21.4 %collective-permute-start.25 = (bf16[3,24,1536]{2,1,0:T(8,128)(2,1)S(1)}, bf16[3,24,1536]{2,1,0:T(8,128)(2,1)S(1)}, u32[]{:S(2)}, u32[]{:S(2)}) collective-permute-start(bf16[3,24,1536]{2,1,0:T(8,128)(2,1)S(1)} %get-tuple-element.104), channel_id=1, source_target_pairs={{0,16},{1,17},{2,18},{3,19},{4,20},{5,21},{6,22},{7,23},{8,24},{9,... | collective-permute-start | bytes 663560 | tf_op jit(solution)/shard_map/ppermute | solution.py:74
  183.7 19.5 %collective-permute-start.26 = (bf16[3,24,1536]{2,1,0:T(8,128)(2,1)S(1)}, bf16[3,24,1536]{2,1,0:T(8,128)(2,1)S(1)}, u32[]{:S(2)}, u32[]{:S(2)}) collective-permute-start(bf16[3,24,1536]{2,1,0:T(8,128)(2,1)S(1)} %get-tuple-element.105), channel_id=1, source_target_pairs={{16,0},{17,1},{18,2},{19,3},{20,4},{21,5},{22,6},{23,7},{24,8},{25... | collective-permute-start | bytes 663560 | tf_op jit(solution)/shard_map/ppermute | solution.py:74
  189.4 19.4 %collective-permute-start.27 = (bf16[2,32,384]{2,1,0:T(8,128)(2,1)S(1)}, bf16[2,32,384]{2,1,0:T(8,128)(2,1)S(1)}, u32[]{:S(2)}, u32[]{:S(2)}) collective-permute-start(bf16[2,32,384]{2,1,0:T(8,128)(2,1)S(1)} %get-tuple-element.109), channel_id=1, source_target_pairs={{0,32},{32,64},{64,96},{96,0},{1,33},{33,65},{65,97},{97,1},{2,34}... | collective-permute-start | bytes 147464 | tf_op jit(solution)/shard_map/ppermute | solution.py:40
  189.5 19.3 %collective-permute-start.28 = (bf16[2,32,384]{2,1,0:T(8,128)(2,1)S(1)}, bf16[2,32,384]{2,1,0:T(8,128)(2,1)S(1)}, u32[]{:S(2)}, u32[]{:S(2)}) collective-permute-start(bf16[2,32,384]{2,1,0:T(8,128)(2,1)S(1)} %get-tuple-element.110), channel_id=1, source_target_pairs={{0,64},{32,96},{64,0},{96,32},{1,65},{33,97},{65,1},{97,33},{2,66}... | collective-permute-start | bytes 147464 | tf_op jit(solution)/shard_map/ppermute | solution.py:40
  191.2 17.6 %collective-permute-start.29 = (bf16[2,32,384]{2,1,0:T(8,128)(2,1)S(1)}, bf16[2,32,384]{2,1,0:T(8,128)(2,1)S(1)}, u32[]{:S(2)}, u32[]{:S(2)}) collective-permute-start(bf16[2,32,384]{2,1,0:T(8,128)(2,1)S(1)} %get-tuple-element.111), channel_id=1, source_target_pairs={{0,96},{32,0},{64,32},{96,64},{1,97},{33,1},{65,33},{97,65},{2,98}... | collective-permute-start | bytes 147464 | tf_op jit(solution)/shard_map/ppermute | solution.py:40
  (48 other events, 310.9 us)

commit v6 on v5

--- a/solution.py
+++ b/solution.py
@@ -254,15 +254,28 @@
     bias, xs = refs[:2]
     first = refs[2:4]
     second = refs[4 : 4 + NY], refs[4 + NY : 4 + 2 * NY]
-    act, pre_grad, w_in, w_out = refs[4 + 2 * NY :]
+    act, pre_grad, w_in, w_out, held, sems = refs[4 + 2 * NY :]
+    copies = [
+        [pltpu.make_async_copy(second[d][r], held.at[d, r], sems.at[d, r]) for r in range(NY)]
+        for d in range(2)
+    ]
+    for d in range(2):
+        for r in range(NY):
+            copies[d][r].start()
     for d in range(2):
         for k in range(NZ):
             for r in range(NY):
                 row, col = place(where, d, k, r)
+                for m, w in ((0, w_in), (1, w_out)):
+                    w[pl.ds(row, AY), col] = first[d][k, r, m]
+    for d in range(2):
+        for r in range(NY):
+            copies[d][r].wait()
+            for k in range(NZ):
+                row, col = place(where, d, k, r)
                 row2 = pl.multiple_of(row + AY, 32)
                 for m, w in ((0, w_in), (1, w_out)):
-                    w[pl.ds(row, AY), col] = first[d][k, r, m]
-                    w[pl.ds(row2, BY), col] = second[d][r][k, m]
+                    w[pl.ds(row2, BY), col] = held[d, r, k, m]
 
     width = 256
 
@@ -290,9 +303,15 @@
     return pl.pallas_call(
         activation_kernel,
         out_shape=[out, out, jax.ShapeDtypeStruct((CHAN, HIDDEN), bf16)],
-        in_specs=[pl.BlockSpec(memory_space=pltpu.SMEM)] + vmem_specs(len(operands)),
+        in_specs=[pl.BlockSpec(memory_space=pltpu.SMEM)]
+        + vmem_specs(4)
+        + [pl.BlockSpec(memory_space=pl.ANY)] * (2 * NY),
         out_specs=vmem_specs(3),
-        scratch_shapes=[pltpu.VMEM((CHAN, HIDDEN), bf16)],
+        scratch_shapes=[
+            pltpu.VMEM((CHAN, HIDDEN), bf16),
+            pltpu.VMEM((2, NY, NZ, 2, BY, COLS), bf16),
+            pltpu.SemaphoreType.DMA((2, NY)),
+        ],
         compiler_params=pltpu.CompilerParams(vmem_limit_bytes=40 * 2**20),
         cost_estimate=pl.CostEstimate(
             flops=4 * TOKENS * CHAN * HIDDEN, bytes_accessed=25_000_000, transcendentals=0
@@ -329,7 +348,16 @@
 
 
 def weight_kernel(where, mine, got, *refs):
-    sides, (ys, out_z, g) = (refs[0:2], refs[2:4]), (refs[4 : 4 + NY], *refs[4 + NY :])
+    sides, (ys, out_z, g) = (refs[0:2], refs[2:4]), (refs[4 : 4 + NY], *refs[4 + NY : 6 + NY])
+    held_y, held_z, sems = refs[6 + NY :]
+    copies = [
+        [
+            pltpu.make_async_copy(held_y.at[m, r], ys[r].at[:, m], sems.at[m, r])
+            for r in range(NY)
+        ]
+        + [pltpu.make_async_copy(held_z.at[m], out_z.at[:, :, m], sems.at[m, NY])]
+        for m in range(2)
+    ]
     width = 256
     for m in range(2):
         own, other = sides[m]
@@ -348,8 +376,13 @@
                 j = k // 4 * NY + lax.rem(where[0] + r, NY)
                 row = pl.multiple_of(j * AY, 32)
                 row2 = pl.multiple_of(PLANES * AY + j * BY, 32)
-                out_z[k, r, m] = g[pl.ds(row, AY), col]
-                ys[r][k, m] = g[pl.ds(row2, BY), col]
+                held_z[m, k, r] = g[pl.ds(row, AY), col]
+                held_y[m, r, k] = g[pl.ds(row2, BY), col]
+        for copy in copies[m]:
+            copy.start()
+    for m in range(2):
+        for copy in copies[m]:
+            copy.wait()
 
 
 def weight_gradients(where, mine, got, pre_grad, other_pre_grad, act, other_act):
@@ -359,8 +392,13 @@
         out_shape=[jax.ShapeDtypeStruct((NZ, 2, BY, COLS), bf16)] * NY
         + [jax.ShapeDtypeStruct((NZ, NY, 2, AY, COLS), bf16)],
         in_specs=[pl.BlockSpec(memory_space=pltpu.SMEM)] + vmem_specs(len(operands)),
-        out_specs=vmem_specs(NY + 1),
-        scratch_shapes=[pltpu.VMEM((CHAN // 2, HIDDEN), bf16)],
+        out_specs=[pl.BlockSpec(memory_space=pltpu.HBM)] * (NY + 1),
+        scratch_shapes=[
+            pltpu.VMEM((CHAN // 2, HIDDEN), bf16),
+            pltpu.VMEM((2, NY, NZ, BY, COLS), bf16),
+            pltpu.VMEM((2, NZ, NY, AY, COLS), bf16),
+            pltpu.SemaphoreType.DMA((2, NY + 1)),
+        ],
         compiler_params=pltpu.CompilerParams(vmem_limit_bytes=32 * 2**20),
         cost_estimate=pl.CostEstimate(
             flops=4 * TOKENS * CHAN * HIDDEN, bytes_accessed=30_000_000, transcendentals=0
@@ -480,15 +518,16 @@
     )
     part = [to_x(v, r) for r, v in enumerate(part)]
     ys, zs = weight_gradients(where, mine, other, pre_grad, other_pre_grad, act, other_act)
+    zs, part[1], part[3] = lax.optimization_barrier((zs, part[1], part[3]))
     ys = [to_y(v, r) for r, v in enumerate(ys)]
     own, first_cols, last_cols = layer_norm_backward(part, xhat, inverse, gain)
     left, right = to_tile(last_cols, 0, 1), to_tile(first_cols, 0, -1)
-    ys = sum_y(ys)
-    ys, own, left, right = lax.optimization_barrier((ys, own, left, right))
-    zs = sum_z(exchange_z(zs))
-    left, right, *zs = lax.optimization_barrier((left, right, *zs))
     first_rows, last_rows = edges(own, left, right)
     up, down = to_tile(last_rows, 1, 0), to_tile(first_rows, -1, 0)
+    ys = sum_y(ys)
+    ys, up, down = lax.optimization_barrier((ys, up, down))
+    zs = sum_z(exchange_z(zs))
+    own, *zs = lax.optimization_barrier((own, *zs))
     zs = [to_y(v, r) for r, v in enumerate(zs)]
     ys = exchange_z(ys)
     grad_input = convolution(own, left, right, up, down, dw_kernel, out_grad)

time: 211 us -> 219 us (1.038)
  local copies, waits for them, and re-layouts: 27.3 us -> 30.8 us
    all_to_all x4, waiting for transfers between devices: 0.45 us -> 11 us  [exchange_z(): return lax.all_to_all(value, Z, 0, 0, tiled=True)]
    ppermute x6, waiting for transfers between devices: 23.8 us -> 17.7 us  [to_x(): return lax.ppermute(value, 'x', shift(NX, k)) if k else value]
    ppermute x12, waiting for transfers between devices: 37.2 us -> 31.3 us  [to_y(): return lax.ppermute(value, 'y', shift(NY, k)) if k else value]
    unnamed x78 -> x92, local copies, waits for them, and re-layouts: 23.3 us -> 26.9 us
    ppermute x4, waiting for transfers between devices: 10.4 us -> 13.3 us  [to_tile(): return lax.ppermute(value, FINE, pairs)]
  transfers between devices with their start and end apart: 34 -> 34, of which waited for: 12 -> 13; matrix products, arithmetic and copies ran while one was open for 1% -> 1% of each run, Pallas kernels for 7% -> 11%
where the time goes in v6:
time: 219 us; the launch traced here: 218 us
  starting transfers between devices  75.2 us (34%)
  waiting for transfers between devices  73.3 us (33%)
  Pallas kernels  34.9 us (16%)
  local copies, waits for them, and re-layouts  30.8 us (14%)
  other arithmetic  2.42 us (1%)
    ppermute x12, waiting for transfers between devices, to_y(): return lax.ppermute(value, 'y', shift(NY, k)) if k else value  31.3 us
    all_to_all x4, starting transfers between devices, exchange_z(): return lax.all_to_all(value, Z, 0, 0, tiled=True)  30.1 us
    unnamed x92, local copies, waits for them, and re-layouts  26.9 us
    ppermute x12, starting transfers between devices, to_y(): return lax.ppermute(value, 'y', shift(NY, k)) if k else value  20.6 us
    ppermute x6, waiting for transfers between devices, to_x(): return lax.ppermute(value, 'x', shift(NX, k)) if k else value  17.7 us
    ppermute x4, starting transfers between devices, to_tile(): return lax.ppermute(value, FINE, pairs)  13.8 us
    ppermute x4, waiting for transfers between devices, to_tile(): return lax.ppermute(value, FINE, pairs)  13.3 us
    all_to_all x4, waiting for transfers between devices, exchange_z(): return lax.all_to_all(value, Z, 0, 0, tiled=True)  11 us
  transfers between devices with their start and end apart: 34, of which 13 were waited for; matrix products, arithmetic and copies ran while one was open for 1% of the time, Pallas kernels for 11%

profile of v6, /device:TPU:32, one launch (start us, length us, event | category | flops | bytes accessed | tf_op | source)
XLA Modules:
  0.0 217.6 jit_solution(11457762497591085374)
XLA Ops:
  3.5 8.6 %all-to-all-start = ((bf16[8,144,384]{2,1,0:T(8,128)(2,1)}), bf16[8,144,384]{2,1,0:T(8,128)(2,1)S(1)}, u32[]{:S(2)}, u32[]{:S(2)}) async-start(bf16[8,144,384]{2,1,0:T(8,128)(2,1)} %broadcast_in_dim.10), calls=%async_computation | async-start | bytes 1769472 | tf_op jit(solution)/shard_map/all_to_all | solution.py:44
  16.7 3.1 %collective-permute-start = (bf16[2,32,384]{2,1,0:T(8,128)(2,1)S(1)}, bf16[2,32,384]{2,1,0:T(8,128)(2,1)S(1)}, u32[]{:S(2)}, u32[]{:S(2)}) collective-permute-start(bf16[2,32,384]{2,1,0:T(8,128)(2,1)S(1)} %pad_maximum_fusion.1), channel_id=1, source_target_pairs={{0,96},{32,0},{64,32},{96,64},{1,97},{33,1},{65,33},{97,65},{2,98}... | collective-permute-start | bytes 147464 | tf_op jit(solution)/shard_map/ppermute | solution.py:40
  21.6 3.9 %collective-permute-done.1 = bf16[2,32,384]{2,1,0:T(8,128)(2,1)S(1)} collective-permute-done((bf16[2,32,384]{2,1,0:T(8,128)(2,1)S(1)}, bf16[2,32,384]{2,1,0:T(8,128)(2,1)S(1)}, u32[]{:S(2)}, u32[]{:S(2)}) %collective-permute-start.1) | collective-permute-done | bytes 49184 | tf_op jit(solution)/shard_map/ppermute | solution.py:40
  26.0 7.4 %collective-permute-done.4.refs_3_ = bf16[256,1536]{1,0:T(8,128)(2,1)S(1)} collective-permute-done((bf16[256,1536]{1,0:T(8,128)(2,1)S(1)}, bf16[256,1536]{1,0:T(8,128)(2,1)S(1)}, u32[]{:S(2)}, u32[]{:S(2)}) %collective-permute-start.4) | collective-permute-done | bytes 786464 | tf_op jit(solution)/shard_map/ppermute | solution.py:36
  37.0 6.8 %all-to-all-start.1 = ((bf16[8,4,2,32,384]{4,3,2,1,0:T(8,128)(2,1)}), bf16[8,4,2,32,384]{4,3,2,1,0:T(8,128)(2,1)S(1)}, u32[]{:S(2)}, u32[]{:S(2)}) async-start(bf16[8,4,2,32,384]{4,3,2,1,0:T(8,128)(2,1)} %broadcast_in_dim.11), calls=%async_computation.1 | async-start | bytes 3145728 | tf_op jit(solution)/shard_map/all_to_all | solution.py:44
  50.2 2.0 collective-permute-start.9
  52.2 13.5 %collective-permute-done.7.refs_7_ = bf16[8,2,64,384]{3,2,1,0:T(8,128)(2,1)S(1)} collective-permute-done((bf16[8,2,64,384]{3,2,1,0:T(8,128)(2,1)S(1)}, bf16[8,2,64,384]{3,2,1,0:T(8,128)(2,1)S(1)}, u32[]{:S(2)}, u32[]{:S(2)}) %collective-permute-start.7) | collective-permute-done | bytes 786464 | tf_op jit(solution)/shard_map/ppermute | solution.py:40
  66.6 13.2 %collective-permute-done.5.refs_5_ = bf16[8,2,64,384]{3,2,1,0:T(8,128)(2,1)S(1)} collective-permute-done((bf16[8,2,64,384]{3,2,1,0:T(8,128)(2,1)S(1)}, bf16[8,2,64,384]{3,2,1,0:T(8,128)(2,1)S(1)}, u32[]{:S(2)}, u32[]{:S(2)}) %collective-permute-start.5) | collective-permute-done | bytes 786464 | tf_op jit(solution)/shard_map/ppermute | solution.py:40
  89.7 3.2 %tokens.1 = (bf16[2,512,1536]{2,1,0:T(8,128)(2,1)S(1)}, bf16[2,768,512]{2,1,0:T(8,128)(2,1)S(1)}, bf16[2,768,512]{2,1,0:T(8,128)(2,1)S(1)}) custom-call(s32[2]{0:T(128)S(1)} %pad_add_fusion.where, bf16[256,1536]{1,0:T(8,128)(2,1)S(1)} %get-tuple-element.60.refs_0_, bf16[256,1536]{1,0:T(8,128)(2,1)S(1)} %copy-done.6, bf16[256,1536]{1,0:T(8,128)(2,1)S(1)} %copy-done.10, ...), custom_call_target="tpu_custom_call" | custom-call | bytes 12000000 | tf_op jit(solution)/shard_map/tokens/pallas_call | solution.py:240
  95.8 9.6 %activations.1 = (bf16[512,1536]{1,0:T(8,128)(2,1)S(1)}, bf16[512,1536]{1,0:T(8,128)(2,1)S(1)}, bf16[1536,1536]{1,0:T(8,128)(2,1)}) custom-call(s32[2]{0:T(128)S(1)} %pad_add_fusion.where, f32[1,1536]{1,0:T(1,128)S(1)} %bitcast.25, bf16[2,512,1536]{2,1,0:T(8,128)(2,1)} %copy-done.23, bf16[8,4,2,32,384]{4,3,2,1,0:T(8,128)(2,1)S(1)} %all-to-all-done.1.refs_2_, ...), custom_call_target="tpu_custom_call" | custom-call | flops 4831838208 | bytes 25000000 | tf_op jit(solution)/shard_map/activations/pallas_call | solution.py:303
  106.2 2.3 %copy-done.38 = bf16[1536,1536]{1,0:T(8,128)(2,1)S(1)} copy-done((bf16[1536,1536]{1,0:T(8,128)(2,1)S(1)}, bf16[1536,1536]{1,0:T(8,128)(2,1)}, u32[]{:S(2)}) %copy-start.38) | copy-done | bytes 4718616
  108.5 3.8 %normed_gradient.1 = (bf16[128,1536]{1,0:T(8,128)(2,1)S(1)}, bf16[128,1536]{1,0:T(8,128)(2,1)S(1)}, bf16[128,1536]{1,0:T(8,128)(2,1)S(1)}, bf16[128,1536]{1,0:T(8,128)(2,1)S(1)}) custom-call(bf16[512,1536]{1,0:T(8,128)(2,1)S(1)} %get-tuple-element.72.pre_grad.refs_0_, bf16[1536,1536]{1,0:T(8,128)(2,1)S(1)} %copy-done.38), custom_call_target="tpu_custom_call" | custom-call | flops 2415919104 | bytes 20000000 | tf_op jit(solution)/shard_map/normed_gradient/pallas_call | solution.py:333
  113.4 2.9 %collective-permute-start.18 = (bf16[128,1536]{1,0:T(8,128)(2,1)S(1)}, bf16[128,1536]{1,0:T(8,128)(2,1)S(1)}, u32[]{:S(2)}, u32[]{:S(2)}) collective-permute-start(bf16[128,1536]{1,0:T(8,128)(2,1)S(1)} %get-tuple-element.85), channel_id=1, source_target_pairs={{0,12},{4,0},{8,4},{12,8},{1,13},{5,1},{9,5},{13,9},{2,14},{6,2},{... | collective-permute-start | bytes 1179656 | tf_op jit(solution)/shard_map/ppermute | solution.py:36
  116.3 9.2 %weight_gradients.1 = (bf16[8,2,64,384]{3,2,1,0:T(8,128)(2,1)S(1)}, bf16[8,2,64,384]{3,2,1,0:T(8,128)(2,1)S(1)}, bf16[8,2,64,384]{3,2,1,0:T(8,128)(2,1)S(1)}, bf...) custom-call(s32[2]{0:T(128)S(1)} %pad_add_fusion.where, bf16[2,768,512]{2,1,0:T(8,128)(2,1)S(1)} %get-tuple-element.79.mine, ...), custom_call_target="tpu_custom_call" | custom-call | flops 4831838208 | bytes 30000000 | tf_op jit(solution)/shard_map/weight_gradients/pallas_call | solution.py:390
  130.0 7.3 %all-to-all-start.2 = ((bf16[8,4,2,32,384]{4,3,2,1,0:T(8,128)(2,1)}), bf16[8,4,2,32,384]{4,3,2,1,0:T(8,128)(2,1)S(1)}, u32[]{:S(2)}, u32[]{:S(2)}) async-start(bf16[8,4,2,32,384]{4,3,2,1,0:T(8,128)(2,1)} %get-tuple-element.92), calls=%async_computation.2 | async-start | bytes 3145728 | tf_op jit(solution)/shard_map/all_to_all | solution.py:44
  138.3 4.1 %collective-permute-start.23 = (bf16[8,2,64,384]{3,2,1,0:T(8,128)(2,1)}, bf16[8,2,64,384]{3,2,1,0:T(8,128)(2,1)S(1)}, u32[]{:S(2)}, u32[]{:S(2)}) collective-permute-start(bf16[8,2,64,384]{3,2,1,0:T(8,128)(2,1)} %copy-done.31), channel_id=1, source_target_pairs={{0,64},{32,96},{64,0},{96,32},{1,65},{33,97},{65,1},{97,33},{2,66}... | collective-permute-start | bytes 2359304 | tf_op jit(solution)/shard_map/ppermute | solution.py:40
  144.4 10.3 %collective-permute-done.19.refs_2_ = bf16[128,1536]{1,0:T(8,128)(2,1)S(1)} collective-permute-done((bf16[128,1536]{1,0:T(8,128)(2,1)}, bf16[128,1536]{1,0:T(8,128)(2,1)S(1)}, u32[]{:S(2)}, u32[]{:S(2)}) %collective-permute-start.19) | collective-permute-done | bytes 393248 | tf_op jit(solution)/shard_map/ppermute | solution.py:36
  158.1 4.3 %collective-permute-start.20 = (bf16[8,3,1536]{2,1,0:T(4,128)(2,1)S(1)}, bf16[8,3,1536]{2,1,0:T(4,128)(2,1)S(1)}, u32[]{:S(2)}, u32[]{:S(2)}) collective-permute-start(bf16[8,3,1536]{2,1,0:T(4,128)(2,1)S(1)} %get-tuple-element.98), channel_id=1, source_target_pairs={{0,1},{1,2},{2,3},{3,4},{4,5},{5,6},{6,7},{7,8},{8,9},{9,10},{10,1... | collective-permute-start | bytes 221192 | tf_op jit(solution)/shard_map/ppermute | solution.py:74
  163.7 11.3 %collective-permute-done.20.left = bf16[8,3,1536]{2,1,0:T(4,128)(2,1)S(1)} collective-permute-done((bf16[8,3,1536]{2,1,0:T(4,128)(2,1)S(1)}, bf16[8,3,1536]{2,1,0:T(4,128)(2,1)S(1)}, u32[]{:S(2)}, u32[]{:S(2)}) %collective-permute-start.20) | collective-permute-done | bytes 73760 | tf_op jit(solution)/shard_map/ppermute | solution.py:74
  177.6 6.3 %collective-permute-start.26 = (bf16[3,24,1536]{2,1,0:T(8,128)(2,1)S(1)}, bf16[3,24,1536]{2,1,0:T(8,128)(2,1)S(1)}, u32[]{:S(2)}, u32[]{:S(2)}) collective-permute-start(bf16[3,24,1536]{2,1,0:T(8,128)(2,1)S(1)} %get-tuple-element.105), channel_id=1, source_target_pairs={{16,0},{17,1},{18,2},{19,3},{20,4},{21,5},{22,6},{23,7},{24,8},{25... | collective-permute-start | bytes 663560 | tf_op jit(solution)/shard_map/ppermute | solution.py:74
  188.1 7.4 %all-to-all-start.3 = ((bf16[8,2,64,384]{3,2,1,0:T(8,128)(2,1)}), bf16[8,2,64,384]{3,2,1,0:T(8,128)(2,1)S(1)}, u32[]{:S(2)}, u32[]{:S(2)}) async-start(bf16[8,2,64,384]{3,2,1,0:T(8,128)(2,1)} %sum_y.1), calls=%async_computation.3 | async-start | bytes 1572864 | tf_op jit(solution)/shard_map/all_to_all | solution.py:44
  195.8 3.0 %collective-permute-start.28 = (bf16[2,32,384]{2,1,0:T(8,128)(2,1)S(1)}, bf16[2,32,384]{2,1,0:T(8,128)(2,1)S(1)}, u32[]{:S(2)}, u32[]{:S(2)}) collective-permute-start(bf16[2,32,384]{2,1,0:T(8,128)(2,1)S(1)} %get-tuple-element.112), channel_id=1, source_target_pairs={{0,64},{32,96},{64,0},{96,32},{1,65},{33,97},{65,1},{97,33},{2,66}... | collective-permute-start | bytes 147464 | tf_op jit(solution)/shard_map/ppermute | solution.py:40
  199.8 5.6 %convolution.1 = bf16[8,16,1536]{2,1,0:T(8,128)(2,1)} custom-call(bf16[8,16,1536]{2,1,0:T(8,128)(2,1)S(1)} %get-tuple-element.97.own, bf16[8,3,1536]{2,1,0:T(4,128)(2,1)S(1)} %collective-permute-done.20.left, bf16[8,3,1536]{2,1,0:T(4,128)(2,1)S(1)} %collective-permute-done.21.right, bf16[3,24,1536]{2,1,0:T(8,128)(2,1)S(1)} %copy-done.18, ...), custom_call_target="tpu_custom_call" | custom-call | tf_op jit(solution)/shard_map/convolution/pallas_call | solution.py:185
  205.5 10.6 %all-to-all-done.3.refs_4_ = bf16[8,2,64,384]{3,2,1,0:T(8,128)(2,1)S(1)} async-done(((bf16[8,2,64,384]{3,2,1,0:T(8,128)(2,1)}), bf16[8,2,64,384]{3,2,1,0:T(8,128)(2,1)S(1)}, u32[]{:S(2)}, u32[]{:S(2)}) %all-to-all-start.3) | async-done | bytes 786464 | tf_op jit(solution)/shard_map/all_to_all | solution.py:44
  (165 shorter events, 56.6 us)
Async XLA Ops:
  3.5 32.1 %all-to-all-start = ((bf16[8,144,384]{2,1,0:T(8,128)(2,1)}), bf16[8,144,384]{2,1,0:T(8,128)(2,1)S(1)}, u32[]{:S(2)}, u32[]{:S(2)}) async-start(bf16[8,144,384]{2,1,0:T(8,128)(2,1)} %broadcast_in_dim.10), calls=%async_computation | async-start | bytes 1769472 | tf_op jit(solution)/shard_map/all_to_all | solution.py:44
  13.5 19.9 %collective-permute-start.4 = (bf16[256,1536]{1,0:T(8,128)(2,1)S(1)}, bf16[256,1536]{1,0:T(8,128)(2,1)S(1)}, u32[]{:S(2)}, u32[]{:S(2)}) collective-permute-start(bf16[256,1536]{1,0:T(8,128)(2,1)S(1)} %get-tuple-element.60.refs_0_), channel_id=1, source_target_pairs={{0,4},{4,8},{8,12},{12,0},{1,5},{5,9},{9,13},{13,1},{2,6},{6,10},{... | collective-permute-start | bytes 2359304 | tf_op jit(solution)/shard_map/ppermute | solution.py:36
  15.0 19.4 %collective-permute-start.3 = (bf16[256,1536]{1,0:T(8,128)(2,1)S(1)}, bf16[256,1536]{1,0:T(8,128)(2,1)S(1)}, u32[]{:S(2)}, u32[]{:S(2)}) collective-permute-start(bf16[256,1536]{1,0:T(8,128)(2,1)S(1)} %get-tuple-element.60.refs_0_), channel_id=1, source_target_pairs={{0,12},{4,0},{8,4},{12,8},{1,13},{5,1},{9,5},{13,9},{2,14},{6,2},{... | collective-permute-start | bytes 2359304 | tf_op jit(solution)/shard_map/ppermute | solution.py:36
  37.0 47.4 %all-to-all-start.1 = ((bf16[8,4,2,32,384]{4,3,2,1,0:T(8,128)(2,1)}), bf16[8,4,2,32,384]{4,3,2,1,0:T(8,128)(2,1)S(1)}, u32[]{:S(2)}, u32[]{:S(2)}) async-start(bf16[8,4,2,32,384]{4,3,2,1,0:T(8,128)(2,1)} %broadcast_in_dim.11), calls=%async_computation.1 | async-start | bytes 3145728 | tf_op jit(solution)/shard_map/all_to_all | solution.py:44
  45.1 20.6 %collective-permute-start.7 = (bf16[8,2,64,384]{3,2,1,0:T(8,128)(2,1)S(1)}, bf16[8,2,64,384]{3,2,1,0:T(8,128)(2,1)S(1)}, u32[]{:S(2)}, u32[]{:S(2)}) collective-permute-start(bf16[8,2,64,384]{3,2,1,0:T(8,128)(2,1)S(1)} %bitcast.19), channel_id=1, source_target_pairs={{0,32},{32,64},{64,96},{96,0},{1,33},{33,65},{65,97},{97,1},{2,34}... | collective-permute-start | bytes 2359304 | tf_op jit(solution)/shard_map/ppermute | solution.py:40
  46.7 33.2 %collective-permute-start.5 = (bf16[8,2,64,384]{3,2,1,0:T(8,128)(2,1)S(1)}, bf16[8,2,64,384]{3,2,1,0:T(8,128)(2,1)S(1)}, u32[]{:S(2)}, u32[]{:S(2)}) collective-permute-start(bf16[8,2,64,384]{3,2,1,0:T(8,128)(2,1)S(1)} %bitcast.20), channel_id=1, source_target_pairs={{0,96},{32,0},{64,32},{96,64},{1,97},{33,1},{65,33},{97,65},{2,98}... | collective-permute-start | bytes 2359304 | tf_op jit(solution)/shard_map/ppermute | solution.py:40
  48.4 32.4 %collective-permute-start.10 = (bf16[256,1536]{1,0:T(8,128)(2,1)S(1)}, bf16[256,1536]{1,0:T(8,128)(2,1)S(1)}, u32[]{:S(2)}, u32[]{:S(2)}) collective-permute-start(bf16[256,1536]{1,0:T(8,128)(2,1)S(1)} %get-tuple-element.60.refs_0_), channel_id=1, source_target_pairs={{0,8},{4,12},{8,0},{12,4},{1,9},{5,13},{9,1},{13,5},{2,10},{6,14},... | collective-permute-start | bytes 2359304 | tf_op jit(solution)/shard_map/ppermute | solution.py:36
  50.2 31.5 %collective-permute-start.9 = (bf16[8,2,64,384]{3,2,1,0:T(8,128)(2,1)S(1)}, bf16[8,2,64,384]{3,2,1,0:T(8,128)(2,1)S(1)}, u32[]{:S(2)}, u32[]{:S(2)}) collective-permute-start(bf16[8,2,64,384]{3,2,1,0:T(8,128)(2,1)S(1)} %bitcast.21), channel_id=1, source_target_pairs={{0,64},{32,96},{64,0},{96,32},{1,65},{33,97},{65,1},{97,33},{2,66}... | collective-permute-start | bytes 2359304 | tf_op jit(solution)/shard_map/ppermute | solution.py:40
  65.7 16.0 %collective-permute-start.8 = (bf16[8,2,64,384]{3,2,1,0:T(8,128)(2,1)S(1)}, bf16[8,2,64,384]{3,2,1,0:T(8,128)(2,1)S(1)}, u32[]{:S(2)}, u32[]{:S(2)}) collective-permute-start(bf16[8,2,64,384]{3,2,1,0:T(8,128)(2,1)S(1)} %collective-permute-done.7.refs_7_), channel_id=1, source_target_pairs={{0,16},{16,0},{1,17},{17,1},{2,18},{18,2},{3,19},{19,3},{4,20},{20... | collective-permute-start | bytes 2359304 | tf_op jit(solution)/shard_map/ppermute | solution.py:61
  84.4 10.2 %collective-permute-start.11 = (bf16[8,4,2,32,384]{4,3,2,1,0:T(8,128)(2,1)S(1)}, bf16[8,4,2,32,384]{4,3,2,1,0:T(8,128)(2,1)}, u32[]{:S(2)}, u32[]{:S(2)}) collective-permute-start(bf16[8,4,2,32,384]{4,3,2,1,0:T(8,128)(2,1)S(1)} %all-to-all-done.1.refs_2_), channel_id=1, source_target_pairs={{0,16},{16,0},{1,17},{17,1},{2,18},{18,2},{3,19},{19,3},{4,20},{20... | collective-permute-start | bytes 4718600 | tf_op jit(solution)/shard_map/ppermute | solution.py:61
  106.1 10.2 %collective-permute-start.16 = (bf16[2,768,512]{2,1,0:T(8,128)(2,1)S(1)}, bf16[2,768,512]{2,1,0:T(8,128)(2,1)S(1)}, u32[]{:S(2)}, u32[]{:S(2)}) collective-permute-start(bf16[2,768,512]{2,1,0:T(8,128)(2,1)S(1)} %get-tuple-element.80), channel_id=1, source_target_pairs={{0,16},{16,0},{1,17},{17,1},{2,18},{18,2},{3,19},{19,3},{4,20},{20... | collective-permute-start | bytes 4718600 | tf_op jit(solution)/shard_map/ppermute | solution.py:61
  113.1 16.0 %collective-permute-start.17 = (bf16[128,1536]{1,0:T(8,128)(2,1)S(1)}, bf16[128,1536]{1,0:T(8,128)(2,1)S(1)}, u32[]{:S(2)}, u32[]{:S(2)}) collective-permute-start(bf16[128,1536]{1,0:T(8,128)(2,1)S(1)} %get-tuple-element.84), channel_id=1, source_target_pairs={{0,4},{4,8},{8,12},{12,0},{1,5},{5,9},{9,13},{13,1},{2,6},{6,10},{... | collective-permute-start | bytes 1179656 | tf_op jit(solution)/shard_map/ppermute | solution.py:36
  113.4 15.7 %collective-permute-start.18 = (bf16[128,1536]{1,0:T(8,128)(2,1)S(1)}, bf16[128,1536]{1,0:T(8,128)(2,1)S(1)}, u32[]{:S(2)}, u32[]{:S(2)}) collective-permute-start(bf16[128,1536]{1,0:T(8,128)(2,1)S(1)} %get-tuple-element.85), channel_id=1, source_target_pairs={{0,12},{4,0},{8,4},{12,8},{1,13},{5,1},{9,5},{13,9},{2,14},{6,2},{... | collective-permute-start | bytes 1179656 | tf_op jit(solution)/shard_map/ppermute | solution.py:36
  130.0 58.1 %all-to-all-start.2 = ((bf16[8,4,2,32,384]{4,3,2,1,0:T(8,128)(2,1)}), bf16[8,4,2,32,384]{4,3,2,1,0:T(8,128)(2,1)S(1)}, u32[]{:S(2)}, u32[]{:S(2)}) async-start(bf16[8,4,2,32,384]{4,3,2,1,0:T(8,128)(2,1)} %get-tuple-element.92), calls=%async_computation.2 | async-start | bytes 3145728 | tf_op jit(solution)/shard_map/all_to_all | solution.py:44
  137.3 46.6 %collective-permute-start.22 = (bf16[8,2,64,384]{3,2,1,0:T(8,128)(2,1)}, bf16[8,2,64,384]{3,2,1,0:T(8,128)(2,1)S(1)}, u32[]{:S(2)}, u32[]{:S(2)}) collective-permute-start(bf16[8,2,64,384]{3,2,1,0:T(8,128)(2,1)} %copy-done.32), channel_id=1, source_target_pairs={{0,32},{32,64},{64,96},{96,0},{1,33},{33,65},{65,97},{97,1},{2,34}... | collective-permute-start | bytes 2359304 | tf_op jit(solution)/shard_map/ppermute | solution.py:40
  138.3 45.6 %collective-permute-start.23 = (bf16[8,2,64,384]{3,2,1,0:T(8,128)(2,1)}, bf16[8,2,64,384]{3,2,1,0:T(8,128)(2,1)S(1)}, u32[]{:S(2)}, u32[]{:S(2)}) collective-permute-start(bf16[8,2,64,384]{3,2,1,0:T(8,128)(2,1)} %copy-done.31), channel_id=1, source_target_pairs={{0,64},{32,96},{64,0},{96,32},{1,65},{33,97},{65,1},{97,33},{2,66}... | collective-permute-start | bytes 2359304 | tf_op jit(solution)/shard_map/ppermute | solution.py:40
  142.5 41.5 %collective-permute-start.24 = (bf16[8,2,64,384]{3,2,1,0:T(8,128)(2,1)}, bf16[8,2,64,384]{3,2,1,0:T(8,128)(2,1)S(1)}, u32[]{:S(2)}, u32[]{:S(2)}) collective-permute-start(bf16[8,2,64,384]{3,2,1,0:T(8,128)(2,1)} %copy-done.28), channel_id=1, source_target_pairs={{0,96},{32,0},{64,32},{96,64},{1,97},{33,1},{65,33},{97,65},{2,98}... | collective-permute-start | bytes 2359304 | tf_op jit(solution)/shard_map/ppermute | solution.py:40
  143.8 10.9 %collective-permute-start.19 = (bf16[128,1536]{1,0:T(8,128)(2,1)}, bf16[128,1536]{1,0:T(8,128)(2,1)S(1)}, u32[]{:S(2)}, u32[]{:S(2)}) collective-permute-start(bf16[128,1536]{1,0:T(8,128)(2,1)} %copy-done.37), channel_id=1, source_target_pairs={{0,8},{4,12},{8,0},{12,4},{1,9},{5,13},{9,1},{13,5},{2,10},{6,14},... | collective-permute-start | bytes 1179656 | tf_op jit(solution)/shard_map/ppermute | solution.py:36
  158.1 16.9 %collective-permute-start.20 = (bf16[8,3,1536]{2,1,0:T(4,128)(2,1)S(1)}, bf16[8,3,1536]{2,1,0:T(4,128)(2,1)S(1)}, u32[]{:S(2)}, u32[]{:S(2)}) collective-permute-start(bf16[8,3,1536]{2,1,0:T(4,128)(2,1)S(1)} %get-tuple-element.98), channel_id=1, source_target_pairs={{0,1},{1,2},{2,3},{3,4},{4,5},{5,6},{6,7},{7,8},{8,9},{9,10},{10,1... | collective-permute-start | bytes 221192 | tf_op jit(solution)/shard_map/ppermute | solution.py:74
  162.4 13.2 %collective-permute-start.21 = (bf16[8,3,1536]{2,1,0:T(4,128)(2,1)S(1)}, bf16[8,3,1536]{2,1,0:T(4,128)(2,1)S(1)}, u32[]{:S(2)}, u32[]{:S(2)}) collective-permute-start(bf16[8,3,1536]{2,1,0:T(4,128)(2,1)S(1)} %get-tuple-element.99), channel_id=1, source_target_pairs={{1,0},{2,1},{3,2},{4,3},{5,4},{6,5},{7,6},{8,7},{9,8},{10,9},{11,1... | collective-permute-start | bytes 221192 | tf_op jit(solution)/shard_map/ppermute | solution.py:74
  188.1 28.0 %all-to-all-start.3 = ((bf16[8,2,64,384]{3,2,1,0:T(8,128)(2,1)}), bf16[8,2,64,384]{3,2,1,0:T(8,128)(2,1)S(1)}, u32[]{:S(2)}, u32[]{:S(2)}) async-start(bf16[8,2,64,384]{3,2,1,0:T(8,128)(2,1)} %sum_y.1), calls=%async_computation.3 | async-start | bytes 1572864 | tf_op jit(solution)/shard_map/all_to_all | solution.py:44
  195.7 20.3 %collective-permute-start.27 = (bf16[2,32,384]{2,1,0:T(8,128)(2,1)S(1)}, bf16[2,32,384]{2,1,0:T(8,128)(2,1)S(1)}, u32[]{:S(2)}, u32[]{:S(2)}) collective-permute-start(bf16[2,32,384]{2,1,0:T(8,128)(2,1)S(1)} %get-tuple-element.111), channel_id=1, source_target_pairs={{0,32},{32,64},{64,96},{96,0},{1,33},{33,65},{65,97},{97,1},{2,34}... | collective-permute-start | bytes 147464 | tf_op jit(solution)/shard_map/ppermute | solution.py:40
  195.8 20.2 %collective-permute-start.28 = (bf16[2,32,384]{2,1,0:T(8,128)(2,1)S(1)}, bf16[2,32,384]{2,1,0:T(8,128)(2,1)S(1)}, u32[]{:S(2)}, u32[]{:S(2)}) collective-permute-start(bf16[2,32,384]{2,1,0:T(8,128)(2,1)S(1)} %get-tuple-element.112), channel_id=1, source_target_pairs={{0,64},{32,96},{64,0},{96,32},{1,65},{33,97},{65,1},{97,33},{2,66}... | collective-permute-start | bytes 147464 | tf_op jit(solution)/shard_map/ppermute | solution.py:40
  198.8 17.3 %collective-permute-start.29 = (bf16[2,32,384]{2,1,0:T(8,128)(2,1)S(1)}, bf16[2,32,384]{2,1,0:T(8,128)(2,1)S(1)}, u32[]{:S(2)}, u32[]{:S(2)}) collective-permute-start(bf16[2,32,384]{2,1,0:T(8,128)(2,1)S(1)} %get-tuple-element.113), channel_id=1, source_target_pairs={{0,96},{32,0},{64,32},{96,64},{1,97},{33,1},{65,33},{97,65},{2,98}... | collective-permute-start | bytes 147464 | tf_op jit(solution)/shard_map/ppermute | solution.py:40
  (55 other events, 306.1 us)
